TPU v7x, 32 devices: a whole 2x2x4 slice. The times are simulated.
32 devices in a mesh: row: 4 (over x, core), col: 8 (over z, y).
Axes of the slice: x: 2, y: 2, z: 4, core: 2. Of those that a mesh axis runs over, the one named last changes fastest.
Arguments:
- item_ids: int32 [8192], P(('row', 'col')), may hold values from 0 to 63
- user_lengths: int32 [8], replicated, may hold values from 1 to 2048, 8192 in all
- catalogue: bfloat16 [64, 1024], P(('row', 'col')), may hold values from -6 to 6
- tap_lengths: int32 [1, 1024], replicated, may hold values from 64 to 256
- conv_taps: bfloat16 [1, 256, 1024], replicated, may hold values from -0.375 to 0.375
- norm_gains: float32 [1, 2, 1024], replicated, may hold values from 0.1 to 1.9
- gate_weight: bfloat16 [1, 1024, 1024], P(None, 'col'), may hold values from -0.1875 to 0.1875
- up_weight: bfloat16 [1, 1024, 1024], P(None, 'col'), may hold values from -0.1875 to 0.1875
- down_weight: bfloat16 [1, 1024, 1024], P(None, 'col'), may hold values from -0.1875 to 0.1875
Outputs:
- history_out: bfloat16 [8192, 1024], P(('row', 'col'))
Inputs may be any that keep to these rules, and one draw needn't show every extreme that they name: `user_lengths`: the 8 lengths sum to 8192.
All inputs are finite; a program needn't handle non-finite values.
Results may differ from a plain program's by a relative error of at most 0.0054.
Values may be sent and summed in bfloat16 or wider, within the bound.
No kernel may reach another device: no remote copies, remote signals or barrier semaphores. Data moves between devices by JAX's collectives and lax.ppermute only.
A program may use at most 64 MiB of HBM per device.

v0:
```python
import jax
import jax.numpy as jnp
from jax import lax
from jax.sharding import PartitionSpec as P

epsilon = 1e-06
group_taps = 32


def from_behind(block, axis, distance):
    devices = range(lax.axis_size(axis))
    route = [(i - distance, i) for i in devices if i - distance in devices]
    return lax.ppermute(block, axis, route)


def rms_norm(values, gains):
    scale = lax.rsqrt(jnp.mean(values * values, axis=-1, keepdims=True) + epsilon)
    return values * scale * gains


def token_ages(positions, user_starts):
    reached = user_starts[None, :] <= positions[:, None]
    fallback = jnp.minimum(positions, 0)[:, None]
    seg_start = jnp.max(jnp.where(reached, user_starts[None, :], fallback), axis=1)
    return positions - seg_start


def earlier_items(item_ids, wanted):
    current = item_ids
    pieces = []
    current = from_behind(current, ("row", "col"), 1)
    pieces = [current] + pieces
    return pieces[0][-wanted:]


def convolve(extended, tap_table, token_age, out_rows):
    reach = extended.shape[0] - out_rows
    groups = -(-tap_table.shape[0] // group_taps)

    def one_group(group_index, accumulated):
        for within in range(group_taps):
            lag_index = group_index * group_taps + within
            shifted = lax.dynamic_slice_in_dim(extended, reach - lag_index, out_rows, 0)
            weights = lax.dynamic_slice_in_dim(tap_table, lag_index, 1, 0)
            keep = (lag_index <= token_age)[:, None]
            accumulated = accumulated + jnp.where(keep, shifted * weights, 0.0)
        return accumulated

    blank = jnp.zeros((out_rows, extended.shape[1]), jnp.float32)
    return lax.fori_loop(0, groups, one_group, blank)


def feed_forward(hidden, gains_row, gate_rows, up_rows, down_rows):
    inner = rms_norm(hidden, gains_row).astype(jnp.bfloat16)
    columns = inner
    first_sum = jnp.dot(
        columns,
        lax.all_gather(gate_rows, "col", axis=0, tiled=True),
        preferred_element_type=jnp.float32,
    )
    second_sum = jnp.dot(
        columns,
        lax.all_gather(up_rows, "col", axis=0, tiled=True),
        preferred_element_type=jnp.float32,
    )
    activated = (jax.nn.silu(first_sum) * second_sum).astype(jnp.bfloat16)
    columns = activated
    projected = jnp.dot(
        columns,
        lax.all_gather(down_rows, "col", axis=0, tiled=True),
        preferred_element_type=jnp.float32,
    )
    return hidden + projected


def body(
    item_ids,
    user_lengths,
    catalogue,
    tap_lengths,
    conv_taps,
    norm_gains,
    gate_weight,
    up_weight,
    down_weight,
):
    row_count = item_ids.shape[0]
    reach = conv_taps.shape[1] - 1
    layer_count = conv_taps.shape[0]
    catalogue_all = lax.all_gather(catalogue, ("row", "col"), axis=0, tiled=True)
    device_index = lax.axis_index("row") * lax.axis_size("col") + lax.axis_index("col")
    first_row = device_index * row_count
    user_starts = jnp.cumsum(user_lengths) - user_lengths
    lag_column = jnp.arange(conv_taps.shape[1], dtype=jnp.int32)[:, None]
    tap_tables = conv_taps.astype(jnp.float32) * (
        lag_column[None] < tap_lengths[:, None, :]
    ).astype(jnp.float32)
    extra = reach * layer_count
    wide_ids = jnp.concatenate([earlier_items(item_ids, extra), item_ids], axis=0)
    hidden = jnp.take(catalogue_all, wide_ids, axis=0).astype(jnp.float32)
    positions = first_row - extra + jnp.arange(row_count + extra, dtype=jnp.int32)
    all_ages = token_ages(positions, user_starts)
    out_rows = row_count + reach * (layer_count - 1)
    normed = rms_norm(hidden, norm_gains[0, 0]).astype(jnp.bfloat16)
    hidden = hidden[-out_rows:] + convolve(normed, tap_tables[0], all_ages[-out_rows:], out_rows)
    hidden = feed_forward(hidden, norm_gains[0, 1], gate_weight[0], up_weight[0], down_weight[0])
    return hidden.astype(jnp.bfloat16)


def solution(mesh):
    return jax.shard_map(
        body,
        mesh=mesh,
        in_specs=(
            P(("row", "col")),
            P(),
            P(("row", "col"), None),
            P(),
            P(),
            P(),
            P(None, "col", None),
            P(None, "col", None),
            P(None, "col", None),
        ),
        out_specs=P(("row", "col"), None),
        check_vma=False,
    )
```

profile of v0, /device:TPU:2, one launch (start us, length us, event | category | flops | bytes accessed | tf_op | source)
XLA Modules:
  0.0 230.7 jit_solution(10582264455192001664)
XLA Ops:
  6.5 0.7 all-gather.8.cloned.1.call-update
  7.3 0.0 all-gather.10.cloned.1.call-start
  7.3 0.7 all-gather.10.cloned.1.call-update
  8.1 3.4 %collective-permute-start = (s32[256]{0:T(256)}, s32[256]{0:T(256)S(1)}, u32[]{:S(2)}, u32[]{:S(2)}) collective-permute-start(s32[256]{0:T(256)} %param.11), channel_id=1, source_target_pairs={{0,1},{1,2},{2,3},{3,4},{4,5},{5,6},{6,7},{7,8},{8,9},{9,10},{10,1... | collective-permute-start | bytes 3080 | tf_op jit(solution)/shard_map/ppermute | solution.py:13
  11.5 0.8 fusion.52
  12.3 0.8 reduce-window.9
  13.2 0.7 bitcast_subtract_fusion
  13.8 0.1 select_reduce_fusion
  13.9 2.2 select_bitcast_fusion
  16.1 69.4 %all-gather.3 = bf16[32,2,1024]{2,1,0:T(2,128)(2,1)S(1)} all-gather(bf16[1,2,1024]{2,1,0:T(2,128)(2,1)S(1)} %bitcast.163), channel_id=1, replica_groups=mesh['row'=4,'col'=8] {'row','col'}, dimensions={0}, use_global_device_ids=true | all-gather | bytes 135168 | tf_op jit(solution)/shard_map/all_gather | solution.py:90
  85.5 0.1 reshape.389
  85.6 0.1 slice.17
  85.7 0.1 slice.15
  85.7 0.1 compare_and_fusion
  85.8 0.1 compare_select_fusion
  85.9 2.1 gather_fusion
  88.0 0.4 multiply_reduce_fusion
  88.4 0.4 multiply_convert_fusion
  88.8 124.7 %while.17 = (s32[]{:T(128)}, f32[256,1024]{1,0:T(8,128)S(1)}, s32[256]{0:T(256)S(1)}, bf16[511,1024]{1,0:T(8,128)(2,1)S(1)}, f32[256,1024]{1,0:T(8,128)}, /*inde...) while((s32[]{:T(128)}, f32[256,1024]{1,0:T(8,128)S(1)}, ...), condition=%wide.region_4.5_spmd.clone, body=%wide.region_3.4_spmd.clone.sunk | while | flops 33825024 | bytes 19289948 | solution.py:50
  88.9 1.5 constant_dynamic-slice_fusion.35
  90.5 1.4 constant_dynamic-slice_fusion.34
  92.3 12.3 %select_add_fusion.3 = f32[256,1024]{1,0:T(8,128)S(1)} fusion(f32[256,1024]{1,0:T(8,128)S(1)} %get-tuple-element.605, f32[1024]{0:T(1024)S(1)} %bitcast.128, bf16[511,1024]{1,0:T(8,128)(2,1)S(1)} %get-tuple-element.679, s32[]{:T(128)S(6)} %select_n.1373, f32[1024]{0:T(1024)S(1)} %bitcast.129, s32[]{:T(128)S(6)} %select_n.1374, ...), kind=kLoop, calls=%fused_computation.26.clone.1 | loop fusion | flops 33816576 | bytes 19013760 | tf_op jit(solution)/shard_map/while/body/eval_jaxpr/add | solution.py:46
  104.7 1.2 constant_dynamic-slice_fusion.35
  106.1 1.4 constant_dynamic-slice_fusion.34
  107.8 12.3 %select_add_fusion.3 = f32[256,1024]{1,0:T(8,128)S(1)} fusion(f32[256,1024]{1,0:T(8,128)S(1)} %get-tuple-element.605, f32[1024]{0:T(1024)S(1)} %bitcast.128, bf16[511,1024]{1,0:T(8,128)(2,1)S(1)} %get-tuple-element.679, s32[]{:T(128)S(6)} %select_n.1373, f32[1024]{0:T(1024)S(1)} %bitcast.129, s32[]{:T(128)S(6)} %select_n.1374, ...), kind=kLoop, calls=%fused_computation.26.clone.1 | loop fusion | flops 33816576 | bytes 19013760 | tf_op jit(solution)/shard_map/while/body/eval_jaxpr/add | solution.py:46
  120.3 1.2 constant_dynamic-slice_fusion.35
  121.6 1.4 constant_dynamic-slice_fusion.34
  123.4 12.3 %select_add_fusion.3 = f32[256,1024]{1,0:T(8,128)S(1)} fusion(f32[256,1024]{1,0:T(8,128)S(1)} %get-tuple-element.605, f32[1024]{0:T(1024)S(1)} %bitcast.128, bf16[511,1024]{1,0:T(8,128)(2,1)S(1)} %get-tuple-element.679, s32[]{:T(128)S(6)} %select_n.1373, f32[1024]{0:T(1024)S(1)} %bitcast.129, s32[]{:T(128)S(6)} %select_n.1374, ...), kind=kLoop, calls=%fused_computation.26.clone.1 | loop fusion | flops 33816576 | bytes 19013760 | tf_op jit(solution)/shard_map/while/body/eval_jaxpr/add | solution.py:46
  135.8 1.2 constant_dynamic-slice_fusion.35
  137.2 1.4 constant_dynamic-slice_fusion.34
  138.9 12.3 %select_add_fusion.3 = f32[256,1024]{1,0:T(8,128)S(1)} fusion(f32[256,1024]{1,0:T(8,128)S(1)} %get-tuple-element.605, f32[1024]{0:T(1024)S(1)} %bitcast.128, bf16[511,1024]{1,0:T(8,128)(2,1)S(1)} %get-tuple-element.679, s32[]{:T(128)S(6)} %select_n.1373, f32[1024]{0:T(1024)S(1)} %bitcast.129, s32[]{:T(128)S(6)} %select_n.1374, ...), kind=kLoop, calls=%fused_computation.26.clone.1 | loop fusion | flops 33816576 | bytes 19013760 | tf_op jit(solution)/shard_map/while/body/eval_jaxpr/add | solution.py:46
  151.4 1.2 constant_dynamic-slice_fusion.35
  152.7 1.4 constant_dynamic-slice_fusion.34
  154.5 12.3 %select_add_fusion.3 = f32[256,1024]{1,0:T(8,128)S(1)} fusion(f32[256,1024]{1,0:T(8,128)S(1)} %get-tuple-element.605, f32[1024]{0:T(1024)S(1)} %bitcast.128, bf16[511,1024]{1,0:T(8,128)(2,1)S(1)} %get-tuple-element.679, s32[]{:T(128)S(6)} %select_n.1373, f32[1024]{0:T(1024)S(1)} %bitcast.129, s32[]{:T(128)S(6)} %select_n.1374, ...), kind=kLoop, calls=%fused_computation.26.clone.1 | loop fusion | flops 33816576 | bytes 19013760 | tf_op jit(solution)/shard_map/while/body/eval_jaxpr/add | solution.py:46
  166.9 1.2 constant_dynamic-slice_fusion.35
  168.3 1.4 constant_dynamic-slice_fusion.34
  170.0 12.3 %select_add_fusion.3 = f32[256,1024]{1,0:T(8,128)S(1)} fusion(f32[256,1024]{1,0:T(8,128)S(1)} %get-tuple-element.605, f32[1024]{0:T(1024)S(1)} %bitcast.128, bf16[511,1024]{1,0:T(8,128)(2,1)S(1)} %get-tuple-element.679, s32[]{:T(128)S(6)} %select_n.1373, f32[1024]{0:T(1024)S(1)} %bitcast.129, s32[]{:T(128)S(6)} %select_n.1374, ...), kind=kLoop, calls=%fused_computation.26.clone.1 | loop fusion | flops 33816576 | bytes 19013760 | tf_op jit(solution)/shard_map/while/body/eval_jaxpr/add | solution.py:46
  182.5 1.2 constant_dynamic-slice_fusion.35
  183.8 1.4 constant_dynamic-slice_fusion.34
  185.6 12.3 %select_add_fusion.3 = f32[256,1024]{1,0:T(8,128)S(1)} fusion(f32[256,1024]{1,0:T(8,128)S(1)} %get-tuple-element.605, f32[1024]{0:T(1024)S(1)} %bitcast.128, bf16[511,1024]{1,0:T(8,128)(2,1)S(1)} %get-tuple-element.679, s32[]{:T(128)S(6)} %select_n.1373, f32[1024]{0:T(1024)S(1)} %bitcast.129, s32[]{:T(128)S(6)} %select_n.1374, ...), kind=kLoop, calls=%fused_computation.26.clone.1 | loop fusion | flops 33816576 | bytes 19013760 | tf_op jit(solution)/shard_map/while/body/eval_jaxpr/add | solution.py:46
  198.0 1.2 constant_dynamic-slice_fusion.35
  199.4 1.4 constant_dynamic-slice_fusion.34
  201.2 12.3 %select_add_fusion.3 = f32[256,1024]{1,0:T(8,128)S(1)} fusion(f32[256,1024]{1,0:T(8,128)S(1)} %get-tuple-element.605, f32[1024]{0:T(1024)S(1)} %bitcast.128, bf16[511,1024]{1,0:T(8,128)(2,1)S(1)} %get-tuple-element.679, s32[]{:T(128)S(6)} %select_n.1373, f32[1024]{0:T(1024)S(1)} %bitcast.129, s32[]{:T(128)S(6)} %select_n.1374, ...), kind=kLoop, calls=%fused_computation.26.clone.1 | loop fusion | flops 33816576 | bytes 19013760 | tf_op jit(solution)/shard_map/while/body/eval_jaxpr/add | solution.py:46
  213.5 0.2 fusion.51
  213.7 1.3 copy-done
  215.0 0.3 multiply_reduce_fusion.1
  215.4 3.9 %fusion.28 = f32[256,1024]{1,0:T(8,128)} fusion(bf16[1,1024,1024]{2,1,0:T(8,128)(2,1)} %all-gather.8.cloned.1.call-done, f32[1024]{0:T(1024)S(1)} %bitcast.165, f32[256]{0:T(256)S(1)} %add_rsqrt_fusion.1, f32[256,1024]{1,0:T(8,128)S(1)} %get-tuple-element.276, f32[511,1024]{1,0:T(8,128)} %copy-done), kind=kOutput, calls=%fused_computation.95 | convolution fusion | flops 537919488 | bytes 5248000 | tf_op jit(solution)/shard_map/dot_general | solution.py:56
  219.3 4.9 %fusion.36 = bf16[256,1024]{1,0:T(8,128)(2,1)} fusion(bf16[1,1024,1024]{2,1,0:T(8,128)(2,1)} %all-gather.12.cloned.1.call-done, bf16[1,1024,1024]{2,1,0:T(8,128)(2,1)} %all-gather.10.cloned.1.call-done, f32[256,1024]{1,0:T(8,128)} %fusion.28, f32[1024]{0:T(1024)S(1)} %bitcast.166, f32[256]{0:T(256)S(1)} %add_rsqrt_fusion.1, ...), kind=kOutput, calls=%fused_computation.101 | convolution fusion | flops 1077149696 | bytes 9966592 | tf_op jit(solution)/shard_map/dot_general | solution.py:68
  (36 shorter events, 0.7 us)
Async XLA Ops:
  6.5 79.2 %copy-start.3 = (s32[256]{0:T(256)S(1)}, s32[256]{0:T(256)}, u32[]{:S(2)}) copy-start(s32[256]{0:T(256)} %param.11) | copy-start | bytes 3076
  6.5 9.6 %copy-start.2 = (bf16[2,1024]{1,0:T(2,128)(2,1)S(1)}, bf16[2,1024]{1,0:T(2,128)(2,1)}, u32[]{:S(2)}) copy-start(bf16[2,1024]{1,0:T(2,128)(2,1)} %param.13) | copy-start | bytes 12292
  6.5 208.8 %all-gather.8.cloned.1.call-start = ((), (), s32[]{:S(2)}) async-start(), calls=%async_computation | async-start | bytes 2359296 | tf_op jit(solution)/shard_map/all_gather | solution.py:58
  7.3 212.0 %all-gather.10.cloned.1.call-start = ((), (), s32[]{:S(2)}) async-start(), calls=%async_computation.1 | async-start | bytes 2359296 | tf_op jit(solution)/shard_map/all_gather | solution.py:63
  8.0 211.3 %all-gather.12.cloned.1.call-start = ((), (), s32[]{:S(2)}) async-start(), calls=%async_computation.2 | async-start | bytes 2359296 | tf_op jit(solution)/shard_map/all_gather | solution.py:70
  8.1 77.6 %collective-permute-start = (s32[256]{0:T(256)}, s32[256]{0:T(256)S(1)}, u32[]{:S(2)}, u32[]{:S(2)}) collective-permute-start(s32[256]{0:T(256)} %param.11), channel_id=1, source_target_pairs={{0,1},{1,2},{2,3},{3,4},{4,5},{5,6},{6,7},{7,8},{8,9},{9,10},{10,1... | collective-permute-start | bytes 3080 | tf_op jit(solution)/shard_map/ppermute | solution.py:13
  213.7 1.4 copy-start
  215.4 3.9 %copy-start.1 = (f32[511,1024]{1,0:T(8,128)S(1)}, f32[511,1024]{1,0:T(8,128)}, u32[]{:S(2)}) copy-start(f32[511,1024]{1,0:T(8,128)} %copy-done) | copy-start | bytes 6279172
Sparse Core Ops, SparseCore 0:
  9.5 50.3 all-gather.7
  62.0 48.4 all-gather.9
  112.6 47.6 all-gather.11
where the time goes:
time: 233 us; the launch traced here: 231 us
  other arithmetic  104 us (45%)
  blocking collectives  69.4 us (30%)
  local copies, waits for them, and re-layouts  25.8 us (11%)
  between operations  13.2 us (6%)
  matrix products  8.77 us (4%)
  loops' own time  4.23 us (2%)
  starting transfers between devices  3.51 us (2%)
    add x8, other arithmetic, one_group(): accumulated = accumulated + jnp.where(keep, shifted * weights, 0.0)  98.5 us
    all_gather x1, blocking collectives, body(): lax.all_gather(catalogue, ('row', 'col'), axis=0, tiled=True)  69.4 us
    dynamic_slice x16, local copies, waits for them, and re-layouts, one_group(): weights = lax.dynamic_slice_in_dim(tap_table, lag_index, 1, 0)  21.4 us
    dot_general x1, matrix products, feed_forward(): jnp.dot(columns, lax.all_gather(down_rows, 'col', axis=0, tiled=True), pr...  4.87 us
  transfers between devices with their start and end apart: 4, of which 0 were waited for; matrix products, arithmetic and copies ran while one was open for 57% of the time, Pallas kernels for 0%

commit v1 on v0

v1 whole, which is shorter than its diff:
```python
import functools

import jax
import jax.numpy as jnp
import numpy as np
from jax import lax
from jax.experimental import pallas as pl
from jax.experimental.pallas import tpu as pltpu
from jax.sharding import PartitionSpec as P

epsilon = 1e-06
lane_chunk = 256
both = ("row", "col")
id_base = 256


def split_bf16(table):
    high = table.astype(jnp.bfloat16)
    low = (table - high.astype(np.float64)).astype(jnp.bfloat16)
    return high, low


def transform_tables(window, out_rows):
    half = window // 2
    angle = 2 * np.pi * np.outer(np.arange(half) + 0.5, np.arange(window)) / window
    forward = np.concatenate([np.cos(angle), np.sin(angle)], axis=0)
    inverse = forward[:, window - out_rows :].T * (2.0 / window)
    return np.concatenate([*split_bf16(forward), *split_bf16(inverse)], axis=0)


def parts_of(tables):
    window = tables.shape[1]
    count = (tables.shape[0] - 2 * window) // 2
    stops = (0, window, 2 * window, 2 * window + count, 2 * window + 2 * count)
    return [tables.at[pl.ds(a, b - a)] for a, b in zip(stops, stops[1:])]


def dot(a, b):
    return jnp.dot(a, b, preferred_element_type=jnp.float32)


def whole(memory_space=pltpu.VMEM):
    return pl.BlockSpec(memory_space=memory_space)


def shape(rows, width, dtype=jnp.bfloat16):
    return jax.ShapeDtypeStruct((rows, width), dtype)


def far(arrays):
    return [pltpu.with_memory_space_constraint(a, pltpu.HBM) for a in arrays]


def call(kernel, out_shape, in_specs, flops, nbytes, limit, scratch=()):
    return pl.pallas_call(
        kernel,
        out_shape=out_shape,
        in_specs=in_specs,
        out_specs=jax.tree.map(lambda _: whole(), out_shape),
        scratch_shapes=list(scratch),
        compiler_params=pltpu.CompilerParams(vmem_limit_bytes=limit << 20),
        cost_estimate=pl.CostEstimate(flops=flops, bytes_accessed=nbytes, transcendentals=0),
    )


def fetch(pairs, sems):
    copies = [pltpu.make_async_copy(a, b, sems.at[i]) for i, (a, b) in enumerate(pairs)]
    for copy in copies:
        copy.start()

    def wait(first=0, end=len(copies)):
        for copy in copies[first:end]:
            copy.wait()

    return wait


def pack_kernel(gate, up, down, own, sems):
    core = lax.axis_index("row") % 2
    depth, half = gate.shape[0], own.shape[1]
    cols = pl.ds(pl.multiple_of(core * half, half), half)
    parts = [(w.at[:, cols], own.at[pl.ds(i * depth, depth)]) for i, w in enumerate((gate, up, down))]
    fetch(parts, sems)()


def pack(gate, up, down):
    depth, width = gate.shape
    return call(
        pack_kernel, shape(3 * depth, width // 2), [whole(pltpu.HBM)] * 3, 0, 1 << 20, 4,
        [pltpu.SemaphoreType.DMA((3,))],
    )(*far((gate, up, down)))


def greet_kernel(ids_far, rows_far, out, ids, rows, sems):
    fetch([(ids_far, ids), (rows_far, rows)], sems)()
    _, width = rows.shape
    count = ids.shape[1]
    numbers = ids[...].astype(jnp.float32)
    high = jnp.floor(numbers * (1.0 / id_base))
    digits = [high, numbers - high * id_base]
    rest = jnp.zeros((1, width - 2 * count), jnp.float32)
    line = jnp.concatenate(digits + [rest], axis=1)
    block = jnp.concatenate([rows[...].astype(jnp.float32), line], axis=0).astype(jnp.bfloat16)

    def one(device, carry):
        out[device] = block
        return carry

    lax.fori_loop(0, out.shape[0], one, 0)


def greet(ids, rows):
    devices = lax.axis_size("row") * lax.axis_size("col")
    out = jax.ShapeDtypeStruct((devices, rows.shape[0] + 1, rows.shape[1]), jnp.bfloat16)
    scratch = [
        pltpu.VMEM(ids.shape, ids.dtype),
        pltpu.VMEM(rows.shape, rows.dtype),
        pltpu.SemaphoreType.DMA((2,)),
    ]
    return call(
        greet_kernel, out, [whole(pltpu.HBM)] * 2, 0, 1 << 18, 16, scratch
    )(*far((ids, rows)))


def taps_kernel(*refs):
    kept, (spectrum, *out), (taps, lengths, sems) = refs[2:5], refs[5:9], refs[9:]
    wait = fetch([*zip(refs[:2], (taps, lengths)), *zip(kept, out)], sems)
    count = taps.shape[0]
    lag = lax.broadcasted_iota(jnp.int32, taps.shape, 0)
    wait(0, 2)
    masked = jnp.where(lag < lengths[...], taps[...].astype(jnp.float32), 0.0).astype(jnp.bfloat16)
    wait(2, 3)
    f_high, f_low, _, _ = parts_of(out[0])
    spectrum[...] = dot(f_high[:, :count], masked) + dot(f_low[:, :count], masked)
    wait(3)


def taps_spectrum(taps, lengths, kept):
    window, (count, width) = kept[0].shape[1], taps.shape
    out = [pltpu.VMEM((window, width), jnp.float32)] + [pltpu.VMEM(k.shape, k.dtype) for k in kept]
    scratch = [
        pltpu.VMEM(taps.shape, taps.dtype),
        pltpu.VMEM(lengths.shape, lengths.dtype),
        pltpu.SemaphoreType.DMA((2 + len(kept),)),
    ]
    return call(
        taps_kernel, out, [whole(pltpu.HBM)] * (2 + len(kept)),
        4 * window * count * width, 5 << 20, 12, scratch,
    )(*far((taps, lengths, *kept)))


def mix_kernel(begin_col, per, lengths, own, table, gains, spectrum, tables, *refs):
    f_high, f_low, g_high, g_low = parts_of(tables)
    last = len(refs) == 5
    if last:
        first_cols, hidden, inner, normed, chosen = refs
    else:
        hidden, normed, chosen = refs
    lines, _ = table.shape
    count, cols_here = own.shape[1], normed.shape[1]
    window = 2 * count
    half = window // 2
    device = lax.axis_index("row") * lax.axis_size("col") + lax.axis_index("col")
    first = device * count
    base = begin_col if last else 0

    wanted = jnp.maximum(device - 1, 0) * (per + 1) + per
    pick = lax.broadcasted_iota(jnp.int32, (8, lines), 1) == wanted
    digits = dot(jnp.where(pick, 1.0, 0.0).astype(jnp.bfloat16), table[:, : 2 * count])[0:1]
    before = (digits[:, :count] * id_base + digits[:, count:]).astype(jnp.int32)

    rows = table[...].astype(jnp.float32)
    scale = lax.rsqrt(jnp.mean(rows * rows, axis=-1, keepdims=True) + epsilon)
    here = pl.ds(begin_col, cols_here)
    normed[...] = (table[:, here].astype(jnp.float32) * scale * gains[0:1, here]).astype(jnp.bfloat16)
    ids = jnp.concatenate([before, own[...]], axis=1)
    line_of = ids // per * (per + 1) + ids % per
    hit = lax.broadcasted_iota(jnp.int32, (lines, window), 0) == line_of
    chosen[...] = jnp.where(hit, 1.0, 0.0).T.astype(jnp.bfloat16)
    if last:
        hidden[:, :begin_col] = first_cols[...]
    hidden[:, base : base + cols_here] = dot(chosen[count:, :], table[:, here])

    at = lax.broadcasted_iota(jnp.int32, (window, 1), 0) + (first - count)

    def one_user(user, begin):
        end = begin + lengths[user]

        @pl.when(jnp.logical_and(begin < first + count, end > first))
        def _():
            inside = jnp.logical_and(at >= begin, at < end)
            picked = jnp.where(inside, chosen[...].astype(jnp.float32), 0.0).astype(jnp.bfloat16)
            for start in range(0, cols_here, lane_chunk):
                x = dot(picked, normed[:, start : start + lane_chunk]).astype(jnp.bfloat16)
                seen = dot(f_high[...], x) + dot(f_low[...], x)
                x_cos, x_sin = seen[:half], seen[half:]
                cols = pl.ds(begin_col + start, lane_chunk)
                w_cos, w_sin = spectrum[:half, cols], spectrum[half:, cols]
                y = jnp.concatenate(
                    [x_cos * w_cos - x_sin * w_sin, x_cos * w_sin + x_sin * w_cos], axis=0
                )
                y_high = y.astype(jnp.bfloat16)
                y_low = (y - y_high.astype(jnp.float32)).astype(jnp.bfloat16)
                mixed = dot(g_high[...], y_high) + dot(g_high[...], y_low) + dot(g_low[...], y_high)
                cols = pl.ds(base + start, lane_chunk)
                hidden[:, cols] += jnp.where(inside[count:], mixed, 0.0)

        return end

    lax.fori_loop(0, lengths.shape[0], one_user, jnp.int32(0))
    if last:
        mixed = hidden[...]
        scale = lax.rsqrt(jnp.mean(mixed * mixed, axis=-1, keepdims=True) + epsilon)
        inner[...] = (mixed * scale * gains[1:2, :]).astype(jnp.bfloat16)


def mix(begin_col, cols_here, per, lengths, own, table, gains, spectrum, tables, first_cols=None):
    count, (lines, width) = own.shape[1], table.shape
    operands = [lengths, own, table, gains, spectrum, tables]
    if first_cols is None:
        out = shape(count, cols_here, jnp.float32)
    else:
        operands.append(first_cols)
        out = (shape(count, width, jnp.float32), shape(count, width))
    return call(
        functools.partial(mix_kernel, begin_col, per),
        out,
        [whole(pltpu.SMEM)] + [whole()] * (len(operands) - 1),
        2 * cols_here * count * count * 16,
        4 << 20,
        24,
        [pltpu.VMEM((lines, cols_here), jnp.bfloat16), pltpu.VMEM((2 * count, lines), jnp.bfloat16)],
    )(*operands)


def col_route(lane, place):
    pairs = []
    for device in range(lax.axis_size("col")):
        target = place(device // 2)
        if target is not None:
            pairs.append((device, target * 2 + (device % 2 ^ lane)))
    return pairs


def partner(block):
    return lax.ppermute(block, "row", [(i, i ^ 1) for i in range(lax.axis_size("row"))])


def travel(own):
    ends = (0, 3)
    side = col_route(0, lambda p: p ^ 1)
    outward = col_route(0, lambda p: None if p in ends else p ^ 1)
    over_ends = col_route(1, lambda p: p if p in ends else None)
    over_middle = col_route(1, lambda p: None if p in ends else p)
    turn = over_ends + col_route(0, lambda p: None if p in ends else 3 - p)

    def send(block, route):
        return lax.ppermute(block, "col", route)

    b = send(own, side)
    m = send(own, turn)
    a = send(own, over_middle)
    c = send(m, side)
    d = send(b, turn)
    e = send(m, over_middle)
    f = send(d, outward)
    g = send(c, turn)
    cut = own.shape[0] // 2
    t = send(g[:cut], outward)
    u = send(f[cut:], over_ends)
    mine = [b, m, c, d, g, a, f, e, t, u]
    return mine, [partner(block) for block in mine]


def travelled(shares, mine, theirs, depth):
    core = lax.axis_index("row") % 2
    col = lax.axis_index("col")
    lane, place = col % 2, col // 2
    near = jnp.where(place % 2 == 0, place + 1, place - 1)
    middle = jnp.logical_or(place == 1, place == 2)
    at = lambda p, other: p * 2 + (1 - lane if other else lane)
    either = lambda p, q: jnp.where(middle, p, q)
    order = [
        col,
        at(near, False),
        either(at(3 - place, False), at(place, True)),
        either(at(near, True), at(3 - near, False)),
        either(at(3 - near, False), at(near, True)),
        at(3 - near, True),
        either(at(place, True), at(3 - place, False)),
        at(3 - place, True),
    ]
    half = mine[0].shape[1]

    def read(weight, part, start, size):
        rows, cols = slice(weight * depth, (weight + 1) * depth), slice(start, start + size)
        b, m, c, d, g, a, f, e, t, u = mine if part == 0 else theirs
        offset = (core if part == 0 else 1 - core) * half + start
        blocks = [shares[weight][:, pl.ds(pl.multiple_of(offset, size), size)]]
        blocks += [piece[rows, cols] for piece in (b, m, c, d, g)]
        blocks.append(jnp.where(middle, a[rows, cols], f[rows, cols]))
        cut = t.shape[0]
        if rows.stop <= cut:
            end = t[rows, cols]
        elif rows.start >= cut:
            end = u[rows.start - cut : rows.stop - cut, cols]
        else:
            end = jnp.concatenate([t[rows.start :, cols], u[: rows.stop - cut, cols]], axis=0)
        blocks.append(jnp.where(middle, e[rows, cols], end))
        return jnp.concatenate(blocks, axis=0)

    return order, read, core


def feed_kernel(inner, hidden, *refs):
    pieces, (out, ordered, active) = refs[:-3], refs[-3:]
    shares, mine, theirs = pieces[:3], pieces[3:13], pieces[13:]
    depth, half = shares[0].shape[0], mine[0].shape[1]
    order, read, core = travelled(shares, mine, theirs, depth)

    def in_order(source):
        for i, index in enumerate(order):
            cols = pl.ds(pl.multiple_of(index * depth, depth), depth)
            ordered[:, i * depth : (i + 1) * depth] = source[:, cols]

    in_order(inner)
    x = ordered[...]
    for part in range(2):
        for start in range(0, half, lane_chunk):
            gate_sum = dot(x, read(0, part, start, lane_chunk))
            up_sum = dot(x, read(1, part, start, lane_chunk))
            offset = (core if part == 0 else 1 - core) * half + start
            cols = pl.ds(pl.multiple_of(offset, lane_chunk), lane_chunk)
            active[:, cols] = (gate_sum / (1.0 + jnp.exp(-gate_sum)) * up_sum).astype(jnp.bfloat16)
    in_order(active)
    x = ordered[...]
    for part in range(2):
        for start in range(0, half, lane_chunk):
            offset = (core if part == 0 else 1 - core) * half + start
            cols = pl.ds(pl.multiple_of(offset, lane_chunk), lane_chunk)
            out[:, cols] = (hidden[:, cols] + dot(x, read(2, part, start, lane_chunk))).astype(
                jnp.bfloat16
            )


def plain_feed_kernel(inner, hidden, gate, up, down, out, active):
    for start in range(0, gate.shape[1], lane_chunk):
        cols = slice(start, start + lane_chunk)
        gate_sum, up_sum = dot(inner[...], gate[:, cols]), dot(inner[...], up[:, cols])
        active[:, cols] = (gate_sum / (1.0 + jnp.exp(-gate_sum)) * up_sum).astype(jnp.bfloat16)
    for start in range(0, down.shape[1], lane_chunk):
        cols = slice(start, start + lane_chunk)
        out[:, cols] = (hidden[:, cols] + dot(active[...], down[:, cols])).astype(jnp.bfloat16)


def feed(kernel, inner, hidden, pieces, inside, scratch):
    count, width = inner.shape
    return call(
        kernel, shape(count, width), [whole()] * (2 + len(pieces)),
        6 * count * width * inside, 8 << 20, 28, scratch,
    )(inner, hidden, *pieces)


def body(item_ids, user_lengths, catalogue, tap_lengths, conv_taps, norm_gains,
         gate_weight, up_weight, down_weight):
    count, (per, width) = item_ids.shape[0], catalogue.shape
    weights = (gate_weight, up_weight, down_weight)
    shares = [w[0] for w in weights]
    inside = gate_weight.shape[2]
    by_hops = travels()
    if by_hops:
        mine, theirs = travel(pack(*shares))
    sent = greet(item_ids[None], catalogue)
    table = lax.all_to_all(sent, both, 0, 0).reshape(-1, width)
    kept = [jnp.asarray(transform_tables(2 * count, count)), norm_gains[0], item_ids[None]]
    spectrum, tables, gains, ids = taps_spectrum(conv_taps[0], tap_lengths, kept)
    common = (per, user_lengths, ids, table, gains, spectrum, tables)
    first_cols = mix(0, width // 2, *common)
    hidden, inner = mix(width // 2, width // 2, *common, first_cols)
    active = pltpu.VMEM((count, inside), jnp.bfloat16)
    if by_hops:
        pieces, kernel = shares + mine + theirs, feed_kernel
        scratch = [pltpu.VMEM((count, width), jnp.bfloat16), active]
    else:
        pieces = [lax.all_gather(w[0], "col", axis=0, tiled=True) for w in weights]
        kernel, scratch = plain_feed_kernel, [active]
    return feed(kernel, inner, hidden, pieces, inside, scratch)


def travels():
    return lax.axis_size("col") == 8 and lax.axis_size("row") % 2 == 0


def solution(mesh):
    by_device = P(both)
    by_col = P(None, "col", None)
    return jax.shard_map(
        body,
        mesh=mesh,
        in_specs=(by_device, P(), P(both, None), P(), P(), P(), by_col, by_col, by_col),
        out_specs=P(both, None),
        check_vma=False,
    )
```

time: 233 us -> 75.2 us (0.32)
  the two profiles are of different devices: /device:TPU:2 before, /device:TPU:19 now
where the time goes in v1:
time: 75.2 us; the launch traced here: 74.7 us
  starting transfers between devices  31.5 us (42%)
  Pallas kernels  22.9 us (30%)
  waiting for transfers between devices  14.2 us (19%)
  local copies, waits for them, and re-layouts  5.9 us (8%)
    ppermute x10, starting transfers between devices, send(): return lax.ppermute(block, 'col', route)  17.9 us
    ppermute x10, waiting for transfers between devices, send(): return lax.ppermute(block, 'col', route)  14.2 us
    pallas_call x2, Pallas kernels, mix(): call(functools.partial(mix_kernel, begin_col, per), out, [whole(pltpu.SME...  12.9 us
    ppermute x10, starting transfers between devices, partner(): lax.ppermute(block, 'row', [(i, i ^ 1) for i in range(lax.axis_size('row'...  8.62 us
    pallas_call x1, Pallas kernels, feed(): call(kernel, shape(count, width), [whole()] * (2 + len(pieces)), 6 * coun...  4.95 us
    all_to_all x1, starting transfers between devices, body(): table = lax.all_to_all(sent, both, 0, 0).reshape(-1, width)  4.95 us
    unnamed x32, local copies, waits for them, and re-layouts  3.42 us
    pallas_call x1, Pallas kernels, taps_spectrum(): call(taps_kernel, out, [whole(pltpu.HBM)] * (2 + len(kept)), 4 * window *...  2.35 us
  transfers between devices with their start and end apart: 21, of which 4 were waited for; matrix products, arithmetic and copies ran while one was open for 3% of the time, Pallas kernels for 23%

profile of v1, /device:TPU:19, one launch (start us, length us, event | category | flops | bytes accessed | tf_op | source)
XLA Modules:
  0.0 74.7 jit_solution(7515765450562630150)
XLA Ops:
  0.0 1.1 %shard_map.104 = bf16[384,512]{1,0:T(8,128)(2,1)S(1)} custom-call(bf16[128,1024]{1,0:T(8,128)(2,1)} %bitcast.6, bf16[128,1024]{1,0:T(8,128)(2,1)} %bitcast.8, bf16[128,1024]{1,0:T(8,128)(2,1)} %bitcast.10), custom_call_target="tpu_custom_call" | custom-call | bytes 1048576 | tf_op jit(solution)/shard_map/pallas_call | solution.py:88
  1.1 0.2 collective-permute-start.1
  1.3 2.4 %collective-permute-start = (bf16[384,512]{1,0:T(8,128)(2,1)S(1)}, bf16[384,512]{1,0:T(8,128)(2,1)S(1)}, u32[]{:S(2)}, u32[]{:S(2)}) collective-permute-start(bf16[384,512]{1,0:T(8,128)(2,1)S(1)} %shard_map.104), channel_id=1, source_target_pairs={{0,2},{1,3},{2,0},{3,1},{4,6},{5,7},{6,4},{7,5},{8,10},{9,11},{10,... | collective-permute-start | bytes 1179656 | tf_op jit(solution)/shard_map/ppermute | solution.py:258
  3.7 7.5 %collective-permute-done.1.refs_4_ = bf16[384,512]{1,0:T(8,128)(2,1)S(1)} collective-permute-done((bf16[384,512]{1,0:T(8,128)(2,1)S(1)}, bf16[384,512]{1,0:T(8,128)(2,1)S(1)}, u32[]{:S(2)}, u32[]{:S(2)}) %collective-permute-start.1) | collective-permute-done | bytes 393248 | tf_op jit(solution)/shard_map/ppermute | solution.py:258
  11.1 1.3 %collective-permute-start.2 = (bf16[384,512]{1,0:T(8,128)(2,1)S(1)}, bf16[384,512]{1,0:T(8,128)(2,1)S(1)}, u32[]{:S(2)}, u32[]{:S(2)}) collective-permute-start(bf16[384,512]{1,0:T(8,128)(2,1)S(1)} %collective-permute-done.1.refs_4_), channel_id=1, source_target_pairs={{0,2},{1,3},{2,0},{3,1},{4,6},{5,7},{6,4},{7,5},{8,10},{9,11},{10,... | collective-permute-start | bytes 1179656 | tf_op jit(solution)/shard_map/ppermute | solution.py:258
  12.4 0.0 collective-permute-done.refs_3_
  12.4 0.0 collective-permute-start.3
  12.4 3.1 %collective-permute-start.5 = (bf16[384,512]{1,0:T(8,128)(2,1)S(1)}, bf16[384,512]{1,0:T(8,128)(2,1)S(1)}, u32[]{:S(2)}, u32[]{:S(2)}) collective-permute-start(bf16[384,512]{1,0:T(8,128)(2,1)S(1)} %shard_map.104), channel_id=1, source_target_pairs={{2,3},{3,2},{4,5},{5,4},{10,11},{11,10},{12,13},{13,12},{18,19},{1... | collective-permute-start | bytes 1179656 | tf_op jit(solution)/shard_map/ppermute | solution.py:258
  15.6 2.1 %collective-permute-start.7 = (bf16[384,512]{1,0:T(8,128)(2,1)S(1)}, bf16[384,512]{1,0:T(8,128)(2,1)}, u32[]{:S(2)}, u32[]{:S(2)}) collective-permute-start(bf16[384,512]{1,0:T(8,128)(2,1)S(1)} %collective-permute-done.1.refs_4_), channel_id=1, source_target_pairs={{2,3},{3,2},{4,5},{5,4},{10,11},{11,10},{12,13},{13,12},{18,19},{1... | collective-permute-start | bytes 1179656 | tf_op jit(solution)/shard_map/ppermute | solution.py:258
  17.7 2.5 %collective-permute-done.2.refs_5_ = bf16[384,512]{1,0:T(8,128)(2,1)S(1)} collective-permute-done((bf16[384,512]{1,0:T(8,128)(2,1)S(1)}, bf16[384,512]{1,0:T(8,128)(2,1)S(1)}, u32[]{:S(2)}, u32[]{:S(2)}) %collective-permute-start.2) | collective-permute-done | bytes 393248 | tf_op jit(solution)/shard_map/ppermute | solution.py:258
  20.3 0.2 collective-permute-start.4
  20.4 0.9 %collective-permute-done.3.refs_6_ = bf16[384,512]{1,0:T(8,128)(2,1)S(1)} collective-permute-done((bf16[384,512]{1,0:T(8,128)(2,1)S(1)}, bf16[384,512]{1,0:T(8,128)(2,1)S(1)}, u32[]{:S(2)}, u32[]{:S(2)}) %collective-permute-start.3) | collective-permute-done | bytes 393248 | tf_op jit(solution)/shard_map/ppermute | solution.py:258
  21.3 3.4 %collective-permute-start.6 = (bf16[384,512]{1,0:T(8,128)(2,1)S(1)}, bf16[384,512]{1,0:T(8,128)(2,1)S(1)}, u32[]{:S(2)}, u32[]{:S(2)}) collective-permute-start(bf16[384,512]{1,0:T(8,128)(2,1)S(1)} %collective-permute-done.3.refs_6_), channel_id=1, source_target_pairs={{2,0},{3,1},{4,6},{5,7},{10,8},{11,9},{12,14},{13,15},{18,16},{19,... | collective-permute-start | bytes 1179656 | tf_op jit(solution)/shard_map/ppermute | solution.py:258
  24.7 3.0 %collective-permute-start.11 = (bf16[384,512]{1,0:T(8,128)(2,1)S(1)}, bf16[384,512]{1,0:T(8,128)(2,1)S(1)}, u32[]{:S(2)}, u32[]{:S(2)}) collective-permute-start(bf16[384,512]{1,0:T(8,128)(2,1)S(1)} %collective-permute-done.1.refs_4_), channel_id=1, source_target_pairs={{0,8},{8,0},{16,24},{24,16},{1,9},{9,1},{17,25},{25,17},{2,10},{10... | collective-permute-start | bytes 1179656 | tf_op jit(solution)/shard_map/ppermute | solution.py:246
  27.8 0.0 collective-permute-done.5.refs_8_
  27.8 0.5 collective-permute-start.10
  28.3 3.3 %collective-permute-done.7.refs_10_ = bf16[384,512]{1,0:T(8,128)(2,1)} collective-permute-done((bf16[384,512]{1,0:T(8,128)(2,1)S(1)}, bf16[384,512]{1,0:T(8,128)(2,1)}, u32[]{:S(2)}, u32[]{:S(2)}) %collective-permute-start.7) | collective-permute-done | bytes 393248 | tf_op jit(solution)/shard_map/ppermute | solution.py:258
  31.6 2.8 %collective-permute-start.15 = (bf16[384,512]{1,0:T(8,128)(2,1)S(1)}, bf16[384,512]{1,0:T(8,128)(2,1)}, u32[]{:S(2)}, u32[]{:S(2)}) collective-permute-start(bf16[384,512]{1,0:T(8,128)(2,1)S(1)} %collective-permute-done.5.refs_8_), channel_id=1, source_target_pairs={{0,8},{8,0},{16,24},{24,16},{1,9},{9,1},{17,25},{25,17},{2,10},{10... | collective-permute-start | bytes 1179656 | tf_op jit(solution)/shard_map/ppermute | solution.py:246
  34.4 0.0 collective-permute-done.4.refs_7_
  34.4 0.0 collective-permute-start.12
  34.4 0.0 collective-permute-done.6.refs_9_
  34.4 0.5 collective-permute-start.13
  34.9 1.6 %shard_map.101 = bf16[32,3,1024]{2,1,0:T(4,128)(2,1)} custom-call(s32[1,256]{1,0:T(1,128)} %bitcast.14, bf16[2,1024]{1,0:T(2,128)(2,1)} %rows_far.1), custom_call_target="tpu_custom_call" | custom-call | bytes 262144 | tf_op jit(solution)/shard_map/pallas_call | solution.py:120
  36.6 4.9 %all-to-all-start = ((bf16[32,3,1024]{2,1,0:T(4,128)(2,1)}), bf16[32,3,1024]{2,1,0:T(4,128)(2,1)}, u32[]{:S(2)}, u32[]{:S(2)}) async-start(bf16[32,3,1024]{2,1,0:T(4,128)(2,1)} %shard_map.101), calls=%async_computation | async-start | bytes 524288 | tf_op jit(solution)/shard_map/all_to_all | solution.py:374
  41.5 0.7 slice.8
  42.2 0.7 slice.9
  42.9 0.0 collective-permute-done.11.refs_14_
  42.9 0.8 %copy-done.13 = bf16[384,512]{1,0:T(8,128)(2,1)} copy-done((bf16[384,512]{1,0:T(8,128)(2,1)}, bf16[384,512]{1,0:T(8,128)(2,1)S(1)}, u32[]{:S(2)}) %copy-start.13) | copy-done | bytes 393240
  43.6 3.8 %collective-permute-start.8 = (bf16[192,512]{1,0:T(8,128)(2,1)}, bf16[192,512]{1,0:T(8,128)(2,1)}, u32[]{:S(2)}, u32[]{:S(2)}) collective-permute-start(bf16[192,512]{1,0:T(8,128)(2,1)} %slice.8), channel_id=1, source_target_pairs={{2,0},{3,1},{4,6},{5,7},{10,8},{11,9},{12,14},{13,15},{18,16},{19,... | collective-permute-start | bytes 589832 | tf_op jit(solution)/shard_map/ppermute | solution.py:258
  47.5 1.3 %collective-permute-start.9 = (bf16[192,512]{1,0:T(8,128)(2,1)}, bf16[192,512]{1,0:T(8,128)(2,1)}, u32[]{:S(2)}, u32[]{:S(2)}) collective-permute-start(bf16[192,512]{1,0:T(8,128)(2,1)} %slice.9), channel_id=1, source_target_pairs={{0,1},{1,0},{6,7},{7,6},{8,9},{9,8},{14,15},{15,14},{16,17},{17,16... | collective-permute-start | bytes 589832 | tf_op jit(solution)/shard_map/ppermute | solution.py:258
  48.8 0.0 collective-permute-done.15.refs_18_
  48.8 0.7 collective-permute-start.17
  49.5 0.0 collective-permute-done.12.refs_15_
  49.5 0.1 collective-permute-start.14
  49.6 0.4 collective-permute-start.16
  50.0 2.4 %shard_map.100 = (f32[512,1024]{1,0:T(8,128)S(1)}, bf16[1536,512]{1,0:T(8,128)(2,1)S(1)}, f32[2,1024]{1,0:T(2,128)S(1)}, s32[1,256]{1,0:T(1,128)S(1)}) custom-call(bf16[256,1024]{1,0:T(8,128)(2,1)} %bitcast.12, s32[1,1024]{1,0:T(1,128)} %refs_1_.1, bf16[1536,512]{1,0:T(8,128)(2,1)} %constant.2.clone.refs_2_, f32[2,1024]{1,0:T(2,128)} %bitcast.13, ...), custom_call_target="tpu_custom_call" | custom-call | flops 536870912 | bytes 5242880 | tf_op jit(solution)/shard_map/pallas_call | solution.py:146
  52.4 1.2 %copy-done = bf16[1536,512]{1,0:T(8,128)(2,1)} copy-done((bf16[1536,512]{1,0:T(8,128)(2,1)}, bf16[1536,512]{1,0:T(8,128)(2,1)S(1)}, u32[]{:S(2)}) %copy-start) | copy-done | bytes 1572888
  53.6 1.1 %reshape.3.table = bf16[96,1024]{1,0:T(8,128)(2,1)S(1)} reshape(bf16[32,3,1024]{2,1,0:T(4,128)(2,1)} %all-to-all-done) | data formatting | bytes 393216 | tf_op jit(solution)/shard_map/reshape | solution.py:374
  54.7 0.1 collective-permute-start.18
  54.8 0.4 collective-permute-start.19
  55.3 1.4 %copy-done.1 = bf16[1536,512]{1,0:T(8,128)(2,1)S(1)} copy-done((bf16[1536,512]{1,0:T(8,128)(2,1)S(1)}, bf16[1536,512]{1,0:T(8,128)(2,1)}, u32[]{:S(2)}) %copy-start.1) | copy-done | bytes 1572888
  56.7 6.3 %shard_map.102.refs_0_ = f32[256,512]{1,0:T(8,128)S(1)} custom-call(s32[8]{0:T(128)S(1)} %copy-done.15, s32[1,256]{1,0:T(1,128)S(1)} %get-tuple-element.11.own, bf16[96,1024]{1,0:T(8,128)(2,1)S(1)} %reshape.3.table, f32[2,1024]{1,0:T(2,128)S(1)} %get-tuple-element.12.gains, f32[512,1024]{1,0:T(8,128)S(1)} %get-tuple-element.13.spectrum, ...), custom_call_target="tpu_custom_call" | custom-call | flops 1073741824 | bytes 4194304 | tf_op jit(solution)/shard_map/pallas_call | solution.py:225
  63.0 0.0 copy-start.2
  63.0 0.0 copy-start.3
  63.0 0.0 copy-start.4
  63.1 0.0 copy-start.6
  63.1 6.5 %shard_map.103 = (f32[256,1024]{1,0:T(8,128)S(1)}, bf16[256,1024]{1,0:T(8,128)(2,1)S(1)}) custom-call(s32[8]{0:T(128)S(1)} %copy-done.15, s32[1,256]{1,0:T(1,128)S(1)} %get-tuple-element.11.own, bf16[96,1024]{1,0:T(8,128)(2,1)S(1)} %reshape.3.table, f32[2,1024]{1,0:T(2,128)S(1)} %get-tuple-element.12.gains, f32[512,1024]{1,0:T(8,128)S(1)} %get-tuple-element.13.spectrum, ...), custom_call_target="tpu_custom_call" | custom-call | flops 1073741824 | bytes 4194304 | tf_op jit(solution)/shard_map/pallas_call | solution.py:225
  69.8 5.0 %shard_map.105 = bf16[256,1024]{1,0:T(8,128)(2,1)} custom-call(bf16[256,1024]{1,0:T(8,128)(2,1)S(1)} %get-tuple-element.15.inner, f32[256,1024]{1,0:T(8,128)S(1)} %get-tuple-element.16.hidden, bf16[128,1024]{1,0:T(8,128)(2,1)S(1)} %bitcast.7, bf16[128,1024]{1,0:T(8,128)(2,1)S(1)} %bitcast.9, bf16[128,1024]{1,0:T(8,128)(2,1)S(1)} %bitcast.11, ...), custom_call_target="tpu_custom_call" | custom-call | flops 1610612736 | bytes 8388608 | tf_op jit(solution)/shard_map/pallas_call | solution.py:358
  (35 shorter events, 0.1 us)
Async XLA Ops:
  1.1 10.1 %collective-permute-start.1 = (bf16[384,512]{1,0:T(8,128)(2,1)S(1)}, bf16[384,512]{1,0:T(8,128)(2,1)S(1)}, u32[]{:S(2)}, u32[]{:S(2)}) collective-permute-start(bf16[384,512]{1,0:T(8,128)(2,1)S(1)} %shard_map.104), channel_id=1, source_target_pairs={{0,1},{1,0},{6,7},{7,6},{2,4},{3,5},{4,2},{5,3},{8,9},{9,8},{14,15... | collective-permute-start | bytes 1179656 | tf_op jit(solution)/shard_map/ppermute | solution.py:258
  1.3 11.1 %collective-permute-start = (bf16[384,512]{1,0:T(8,128)(2,1)S(1)}, bf16[384,512]{1,0:T(8,128)(2,1)S(1)}, u32[]{:S(2)}, u32[]{:S(2)}) collective-permute-start(bf16[384,512]{1,0:T(8,128)(2,1)S(1)} %shard_map.104), channel_id=1, source_target_pairs={{0,2},{1,3},{2,0},{3,1},{4,6},{5,7},{6,4},{7,5},{8,10},{9,11},{10,... | collective-permute-start | bytes 1179656 | tf_op jit(solution)/shard_map/ppermute | solution.py:258
  11.1 9.1 %collective-permute-start.2 = (bf16[384,512]{1,0:T(8,128)(2,1)S(1)}, bf16[384,512]{1,0:T(8,128)(2,1)S(1)}, u32[]{:S(2)}, u32[]{:S(2)}) collective-permute-start(bf16[384,512]{1,0:T(8,128)(2,1)S(1)} %collective-permute-done.1.refs_4_), channel_id=1, source_target_pairs={{0,2},{1,3},{2,0},{3,1},{4,6},{5,7},{6,4},{7,5},{8,10},{9,11},{10,... | collective-permute-start | bytes 1179656 | tf_op jit(solution)/shard_map/ppermute | solution.py:258
  12.4 37.6 %copy-start.5 = (bf16[384,512]{1,0:T(8,128)(2,1)}, bf16[384,512]{1,0:T(8,128)(2,1)S(1)}, u32[]{:S(2)}) copy-start(bf16[384,512]{1,0:T(8,128)(2,1)S(1)} %collective-permute-done.refs_3_) | copy-start | bytes 1179652
  12.4 8.9 %collective-permute-start.3 = (bf16[384,512]{1,0:T(8,128)(2,1)S(1)}, bf16[384,512]{1,0:T(8,128)(2,1)S(1)}, u32[]{:S(2)}, u32[]{:S(2)}) collective-permute-start(bf16[384,512]{1,0:T(8,128)(2,1)S(1)} %collective-permute-done.refs_3_), channel_id=1, source_target_pairs={{0,1},{1,0},{6,7},{7,6},{2,4},{3,5},{4,2},{5,3},{8,9},{9,8},{14,15... | collective-permute-start | bytes 1179656 | tf_op jit(solution)/shard_map/ppermute | solution.py:258
  12.4 15.3 %collective-permute-start.5 = (bf16[384,512]{1,0:T(8,128)(2,1)S(1)}, bf16[384,512]{1,0:T(8,128)(2,1)S(1)}, u32[]{:S(2)}, u32[]{:S(2)}) collective-permute-start(bf16[384,512]{1,0:T(8,128)(2,1)S(1)} %shard_map.104), channel_id=1, source_target_pairs={{2,3},{3,2},{4,5},{5,4},{10,11},{11,10},{12,13},{13,12},{18,19},{1... | collective-permute-start | bytes 1179656 | tf_op jit(solution)/shard_map/ppermute | solution.py:258
  15.6 16.0 %collective-permute-start.7 = (bf16[384,512]{1,0:T(8,128)(2,1)S(1)}, bf16[384,512]{1,0:T(8,128)(2,1)}, u32[]{:S(2)}, u32[]{:S(2)}) collective-permute-start(bf16[384,512]{1,0:T(8,128)(2,1)S(1)} %collective-permute-done.1.refs_4_), channel_id=1, source_target_pairs={{2,3},{3,2},{4,5},{5,4},{10,11},{11,10},{12,13},{13,12},{18,19},{1... | collective-permute-start | bytes 1179656 | tf_op jit(solution)/shard_map/ppermute | solution.py:258
  20.3 29.7 %copy-start.7 = (bf16[384,512]{1,0:T(8,128)(2,1)}, bf16[384,512]{1,0:T(8,128)(2,1)S(1)}, u32[]{:S(2)}) copy-start(bf16[384,512]{1,0:T(8,128)(2,1)S(1)} %collective-permute-done.2.refs_5_) | copy-start | bytes 1179652
  20.3 14.1 %collective-permute-start.4 = (bf16[384,512]{1,0:T(8,128)(2,1)S(1)}, bf16[384,512]{1,0:T(8,128)(2,1)S(1)}, u32[]{:S(2)}, u32[]{:S(2)}) collective-permute-start(bf16[384,512]{1,0:T(8,128)(2,1)S(1)} %collective-permute-done.2.refs_5_), channel_id=1, source_target_pairs={{0,1},{1,0},{6,7},{7,6},{2,4},{3,5},{4,2},{5,3},{8,9},{9,8},{14,15... | collective-permute-start | bytes 1179656 | tf_op jit(solution)/shard_map/ppermute | solution.py:258
  21.3 28.7 %copy-start.9 = (bf16[384,512]{1,0:T(8,128)(2,1)}, bf16[384,512]{1,0:T(8,128)(2,1)S(1)}, u32[]{:S(2)}) copy-start(bf16[384,512]{1,0:T(8,128)(2,1)S(1)} %collective-permute-done.3.refs_6_) | copy-start | bytes 1179652
  21.3 13.1 %collective-permute-start.6 = (bf16[384,512]{1,0:T(8,128)(2,1)S(1)}, bf16[384,512]{1,0:T(8,128)(2,1)S(1)}, u32[]{:S(2)}, u32[]{:S(2)}) collective-permute-start(bf16[384,512]{1,0:T(8,128)(2,1)S(1)} %collective-permute-done.3.refs_6_), channel_id=1, source_target_pairs={{2,0},{3,1},{4,6},{5,7},{10,8},{11,9},{12,14},{13,15},{18,16},{19,... | collective-permute-start | bytes 1179656 | tf_op jit(solution)/shard_map/ppermute | solution.py:258
  24.7 18.1 %collective-permute-start.11 = (bf16[384,512]{1,0:T(8,128)(2,1)S(1)}, bf16[384,512]{1,0:T(8,128)(2,1)S(1)}, u32[]{:S(2)}, u32[]{:S(2)}) collective-permute-start(bf16[384,512]{1,0:T(8,128)(2,1)S(1)} %collective-permute-done.1.refs_4_), channel_id=1, source_target_pairs={{0,8},{8,0},{16,24},{24,16},{1,9},{9,1},{17,25},{25,17},{2,10},{10... | collective-permute-start | bytes 1179656 | tf_op jit(solution)/shard_map/ppermute | solution.py:246
  27.8 22.2 %copy-start.11 = (bf16[384,512]{1,0:T(8,128)(2,1)}, bf16[384,512]{1,0:T(8,128)(2,1)S(1)}, u32[]{:S(2)}) copy-start(bf16[384,512]{1,0:T(8,128)(2,1)S(1)} %collective-permute-done.5.refs_8_) | copy-start | bytes 1179652
  27.8 19.7 %collective-permute-start.10 = (bf16[384,512]{1,0:T(8,128)(2,1)S(1)}, bf16[384,512]{1,0:T(8,128)(2,1)}, u32[]{:S(2)}, u32[]{:S(2)}) collective-permute-start(bf16[384,512]{1,0:T(8,128)(2,1)S(1)} %collective-permute-done.refs_3_), channel_id=1, source_target_pairs={{0,8},{8,0},{16,24},{24,16},{1,9},{9,1},{17,25},{25,17},{2,10},{10... | collective-permute-start | bytes 1179656 | tf_op jit(solution)/shard_map/ppermute | solution.py:246
  31.6 17.2 %collective-permute-start.15 = (bf16[384,512]{1,0:T(8,128)(2,1)S(1)}, bf16[384,512]{1,0:T(8,128)(2,1)}, u32[]{:S(2)}, u32[]{:S(2)}) collective-permute-start(bf16[384,512]{1,0:T(8,128)(2,1)S(1)} %collective-permute-done.5.refs_8_), channel_id=1, source_target_pairs={{0,8},{8,0},{16,24},{24,16},{1,9},{9,1},{17,25},{25,17},{2,10},{10... | collective-permute-start | bytes 1179656 | tf_op jit(solution)/shard_map/ppermute | solution.py:246
  34.4 15.1 %collective-permute-start.12 = (bf16[384,512]{1,0:T(8,128)(2,1)S(1)}, bf16[384,512]{1,0:T(8,128)(2,1)}, u32[]{:S(2)}, u32[]{:S(2)}) collective-permute-start(bf16[384,512]{1,0:T(8,128)(2,1)S(1)} %collective-permute-done.2.refs_5_), channel_id=1, source_target_pairs={{0,8},{8,0},{16,24},{24,16},{1,9},{9,1},{17,25},{25,17},{2,10},{10... | collective-permute-start | bytes 1179656 | tf_op jit(solution)/shard_map/ppermute | solution.py:246
  34.4 15.1 %collective-permute-start.13 = (bf16[384,512]{1,0:T(8,128)(2,1)S(1)}, bf16[384,512]{1,0:T(8,128)(2,1)}, u32[]{:S(2)}, u32[]{:S(2)}) collective-permute-start(bf16[384,512]{1,0:T(8,128)(2,1)S(1)} %collective-permute-done.3.refs_6_), channel_id=1, source_target_pairs={{0,8},{8,0},{16,24},{24,16},{1,9},{9,1},{17,25},{25,17},{2,10},{10... | collective-permute-start | bytes 1179656 | tf_op jit(solution)/shard_map/ppermute | solution.py:246
  36.6 17.0 %all-to-all-start = ((bf16[32,3,1024]{2,1,0:T(4,128)(2,1)}), bf16[32,3,1024]{2,1,0:T(4,128)(2,1)}, u32[]{:S(2)}, u32[]{:S(2)}) async-start(bf16[32,3,1024]{2,1,0:T(4,128)(2,1)} %shard_map.101), calls=%async_computation | async-start | bytes 524288 | tf_op jit(solution)/shard_map/all_to_all | solution.py:374
  42.2 13.1 %copy-start.15 = (s32[8]{0:T(128)S(1)}, s32[8]{0:T(128)}, u32[]{:S(2)}) copy-start(s32[8]{0:T(128)} %lengths.3) | copy-start | bytes 100
  42.9 0.8 %copy-start.13 = (bf16[384,512]{1,0:T(8,128)(2,1)}, bf16[384,512]{1,0:T(8,128)(2,1)S(1)}, u32[]{:S(2)}) copy-start(bf16[384,512]{1,0:T(8,128)(2,1)S(1)} %collective-permute-done.11.refs_14_) | copy-start | bytes 1179652
  43.6 11.0 %collective-permute-start.8 = (bf16[192,512]{1,0:T(8,128)(2,1)}, bf16[192,512]{1,0:T(8,128)(2,1)}, u32[]{:S(2)}, u32[]{:S(2)}) collective-permute-start(bf16[192,512]{1,0:T(8,128)(2,1)} %slice.8), channel_id=1, source_target_pairs={{2,0},{3,1},{4,6},{5,7},{10,8},{11,9},{12,14},{13,15},{18,16},{19,... | collective-permute-start | bytes 589832 | tf_op jit(solution)/shard_map/ppermute | solution.py:258
  47.5 7.4 %collective-permute-start.9 = (bf16[192,512]{1,0:T(8,128)(2,1)}, bf16[192,512]{1,0:T(8,128)(2,1)}, u32[]{:S(2)}, u32[]{:S(2)}) collective-permute-start(bf16[192,512]{1,0:T(8,128)(2,1)} %slice.9), channel_id=1, source_target_pairs={{0,1},{1,0},{6,7},{7,6},{8,9},{9,8},{14,15},{15,14},{16,17},{17,16... | collective-permute-start | bytes 589832 | tf_op jit(solution)/shard_map/ppermute | solution.py:258
  48.8 20.8 %collective-permute-start.17 = (bf16[384,512]{1,0:T(8,128)(2,1)}, bf16[384,512]{1,0:T(8,128)(2,1)}, u32[]{:S(2)}, u32[]{:S(2)}) collective-permute-start(bf16[384,512]{1,0:T(8,128)(2,1)} %collective-permute-done.7.refs_10_), channel_id=1, source_target_pairs={{0,8},{8,0},{16,24},{24,16},{1,9},{9,1},{17,25},{25,17},{2,10},{10... | collective-permute-start | bytes 1179656 | tf_op jit(solution)/shard_map/ppermute | solution.py:246
  49.5 20.2 %collective-permute-start.14 = (bf16[384,512]{1,0:T(8,128)(2,1)S(1)}, bf16[384,512]{1,0:T(8,128)(2,1)}, u32[]{:S(2)}, u32[]{:S(2)}) collective-permute-start(bf16[384,512]{1,0:T(8,128)(2,1)S(1)} %collective-permute-done.4.refs_7_), channel_id=1, source_target_pairs={{0,8},{8,0},{16,24},{24,16},{1,9},{9,1},{17,25},{25,17},{2,10},{10... | collective-permute-start | bytes 1179656 | tf_op jit(solution)/shard_map/ppermute | solution.py:246
  49.6 20.1 %collective-permute-start.16 = (bf16[384,512]{1,0:T(8,128)(2,1)S(1)}, bf16[384,512]{1,0:T(8,128)(2,1)}, u32[]{:S(2)}, u32[]{:S(2)}) collective-permute-start(bf16[384,512]{1,0:T(8,128)(2,1)S(1)} %collective-permute-done.6.refs_9_), channel_id=1, source_target_pairs={{0,8},{8,0},{16,24},{24,16},{1,9},{9,1},{17,25},{25,17},{2,10},{10... | collective-permute-start | bytes 1179656 | tf_op jit(solution)/shard_map/ppermute | solution.py:246
  52.4 1.2 %copy-start = (bf16[1536,512]{1,0:T(8,128)(2,1)}, bf16[1536,512]{1,0:T(8,128)(2,1)S(1)}, u32[]{:S(2)}) copy-start(bf16[1536,512]{1,0:T(8,128)(2,1)S(1)} %get-tuple-element.14.tables) | copy-start | bytes 4718596
  54.7 15.0 %collective-permute-start.18 = (bf16[192,512]{1,0:T(8,128)(2,1)}, bf16[192,512]{1,0:T(8,128)(2,1)S(1)}, u32[]{:S(2)}, u32[]{:S(2)}) collective-permute-start(bf16[192,512]{1,0:T(8,128)(2,1)} %collective-permute-done.8.refs_11_), channel_id=1, source_target_pairs={{0,8},{8,0},{16,24},{24,16},{1,9},{9,1},{17,25},{25,17},{2,10},{10... | collective-permute-start | bytes 589832 | tf_op jit(solution)/shard_map/ppermute | solution.py:246
  54.8 14.8 %collective-permute-start.19 = (bf16[192,512]{1,0:T(8,128)(2,1)}, bf16[192,512]{1,0:T(8,128)(2,1)S(1)}, u32[]{:S(2)}, u32[]{:S(2)}) collective-permute-start(bf16[192,512]{1,0:T(8,128)(2,1)} %collective-permute-done.9.refs_12_), channel_id=1, source_target_pairs={{0,8},{8,0},{16,24},{24,16},{1,9},{9,1},{17,25},{25,17},{2,10},{10... | collective-permute-start | bytes 589832 | tf_op jit(solution)/shard_map/ppermute | solution.py:246
  55.3 1.4 %copy-start.1 = (bf16[1536,512]{1,0:T(8,128)(2,1)S(1)}, bf16[1536,512]{1,0:T(8,128)(2,1)}, u32[]{:S(2)}) copy-start(bf16[1536,512]{1,0:T(8,128)(2,1)} %copy-done) | copy-start | bytes 4718596
  63.0 6.7 %copy-start.2 = (bf16[1,128,1024]{2,1,0:T(8,128)(2,1)S(1)}, bf16[1,128,1024]{2,1,0:T(8,128)(2,1)}, u32[]{:S(2)}) copy-start(bf16[1,128,1024]{2,1,0:T(8,128)(2,1)} %param.16) | copy-start | bytes 786436
  63.0 6.7 %copy-start.3 = (bf16[1,128,1024]{2,1,0:T(8,128)(2,1)S(1)}, bf16[1,128,1024]{2,1,0:T(8,128)(2,1)}, u32[]{:S(2)}) copy-start(bf16[1,128,1024]{2,1,0:T(8,128)(2,1)} %param.17) | copy-start | bytes 786436
  63.0 6.7 %copy-start.4 = (bf16[1,128,1024]{2,1,0:T(8,128)(2,1)S(1)}, bf16[1,128,1024]{2,1,0:T(8,128)(2,1)}, u32[]{:S(2)}) copy-start(bf16[1,128,1024]{2,1,0:T(8,128)(2,1)} %param.18) | copy-start | bytes 786436
  63.1 6.7 %copy-start.6 = (bf16[384,512]{1,0:T(8,128)(2,1)S(1)}, bf16[384,512]{1,0:T(8,128)(2,1)}, u32[]{:S(2)}) copy-start(bf16[384,512]{1,0:T(8,128)(2,1)} %copy-done.5) | copy-start | bytes 1179652
  63.1 6.7 %copy-start.8 = (bf16[384,512]{1,0:T(8,128)(2,1)S(1)}, bf16[384,512]{1,0:T(8,128)(2,1)}, u32[]{:S(2)}) copy-start(bf16[384,512]{1,0:T(8,128)(2,1)} %copy-done.7) | copy-start | bytes 1179652
  63.1 6.7 %copy-start.10 = (bf16[384,512]{1,0:T(8,128)(2,1)S(1)}, bf16[384,512]{1,0:T(8,128)(2,1)}, u32[]{:S(2)}) copy-start(bf16[384,512]{1,0:T(8,128)(2,1)} %copy-done.9) | copy-start | bytes 1179652
  63.1 6.7 %copy-start.12 = (bf16[384,512]{1,0:T(8,128)(2,1)S(1)}, bf16[384,512]{1,0:T(8,128)(2,1)}, u32[]{:S(2)}) copy-start(bf16[384,512]{1,0:T(8,128)(2,1)} %copy-done.11) | copy-start | bytes 1179652
  63.1 6.7 %copy-start.14 = (bf16[384,512]{1,0:T(8,128)(2,1)S(1)}, bf16[384,512]{1,0:T(8,128)(2,1)}, u32[]{:S(2)}) copy-start(bf16[384,512]{1,0:T(8,128)(2,1)} %copy-done.13) | copy-start | bytes 1179652

commit v2 on v1

v2 whole, which is shorter than its diff:
```python
import functools

import jax
import jax.numpy as jnp
import numpy as np
from jax import lax
from jax.experimental import pallas as pl
from jax.experimental.pallas import tpu as pltpu
from jax.sharding import PartitionSpec as P

epsilon = 1e-06
lane_chunk = 256
mix_chunk = 512
both = ("row", "col")
id_base = 256


def split_bf16(table):
    high = table.astype(jnp.bfloat16)
    low = (table - high.astype(np.float64)).astype(jnp.bfloat16)
    return high, low


def transform_tables(window, out_rows):
    half = window // 2
    angle = 2 * np.pi * np.outer(np.arange(half) + 0.5, np.arange(window)) / window
    forward = np.concatenate([np.cos(angle), np.sin(angle)], axis=0)
    inverse = forward[:, window - out_rows :].T * (2.0 / window)
    (f_high, f_low), (g_high, g_low) = split_bf16(forward), split_bf16(inverse)
    return np.concatenate([f_high, f_low], axis=1), np.concatenate([g_high, g_high, g_low], axis=1)


def dot(a, b):
    return jnp.dot(a, b, preferred_element_type=jnp.float32)


def whole(memory_space=pltpu.VMEM):
    return pl.BlockSpec(memory_space=memory_space)


def shape(rows, width, dtype=jnp.bfloat16):
    return jax.ShapeDtypeStruct((rows, width), dtype)


def far(arrays):
    return [pltpu.with_memory_space_constraint(a, pltpu.HBM) for a in arrays]


def near(arrays):
    return [pltpu.with_memory_space_constraint(a, pltpu.VMEM) for a in arrays]


def call(kernel, out_shape, in_specs, flops, nbytes, limit, scratch=()):
    return pl.pallas_call(
        kernel,
        out_shape=out_shape,
        in_specs=in_specs,
        out_specs=jax.tree.map(lambda _: whole(), out_shape),
        scratch_shapes=list(scratch),
        compiler_params=pltpu.CompilerParams(vmem_limit_bytes=limit << 20),
        cost_estimate=pl.CostEstimate(flops=flops, bytes_accessed=nbytes, transcendentals=0),
    )


def fetch(pairs, sems):
    copies = [pltpu.make_async_copy(a, b, sems.at[i]) for i, (a, b) in enumerate(pairs)]
    for copy in copies:
        copy.start()

    def wait(first=0, end=len(copies)):
        for copy in copies[first:end]:
            copy.wait()

    return wait


def pack_kernel(gate, up, down, own, sems):
    core = lax.axis_index("row") % 2
    depth, half = gate.shape[0], own.shape[1]
    cols = pl.ds(pl.multiple_of(core * half, half), half)
    parts = [(w.at[:, cols], own.at[pl.ds(i * depth, depth)]) for i, w in enumerate((gate, up, down))]
    fetch(parts, sems)()


def pack(gate, up, down):
    depth, width = gate.shape
    return call(
        pack_kernel, pltpu.VMEM((3 * depth, width // 2), gate.dtype), [whole(pltpu.HBM)] * 3, 0, 1 << 20, 4,
        [pltpu.SemaphoreType.DMA((3,))],
    )(*far((gate, up, down)))


def greet_kernel(ids_far, gains_far, rows_far, out, ids, gains, rows, sems):
    wait = fetch([(ids_far, ids), (rows_far, rows), (gains_far, gains)], sems)
    wait(0, 2)
    numbers = ids[...].astype(jnp.float32)
    high = jnp.floor(numbers * (1.0 / id_base))
    digits = [high, numbers - high * id_base]
    digits += [jnp.zeros_like(high)] * (rows.shape[0] - 2)
    digits = jnp.concatenate(digits, axis=0)
    block = jnp.concatenate([rows[...].astype(jnp.float32), digits], axis=1).astype(jnp.bfloat16)

    def one(device, carry):
        out[device] = block
        return carry

    lax.fori_loop(0, out.shape[0], one, 0)
    wait(2)


def greet(ids, gains, rows):
    devices = lax.axis_size("row") * lax.axis_size("col")
    out = jax.ShapeDtypeStruct((devices, rows.shape[0], rows.shape[1] + ids.shape[1]), jnp.bfloat16)
    out = (out, pltpu.VMEM(ids.shape, ids.dtype), pltpu.VMEM(gains.shape, gains.dtype))
    scratch = [pltpu.VMEM(rows.shape, rows.dtype), pltpu.SemaphoreType.DMA((3,))]
    return call(
        greet_kernel, out, [whole(pltpu.HBM)] * 3, 0, 1 << 18, 4, scratch
    )(*far((ids, gains, rows)))


def taps_kernel(after, taps_far, lengths_far, *refs):
    kept, (spectrum, *out), (taps, lengths, sems) = refs[:2], refs[2:5], refs[5:]
    wait = fetch([(taps_far, taps), (lengths_far, lengths), *zip(kept, out)], sems)
    count, window = taps.shape[0], spectrum.shape[0]
    lag = lax.broadcasted_iota(jnp.int32, taps.shape, 0)
    wait(0, 2)
    masked = jnp.where(lag < lengths[...], taps[...].astype(jnp.float32), 0.0).astype(jnp.bfloat16)
    wait(2, 3)
    forward = jnp.concatenate([out[0][:, :count], out[0][:, window : window + count]], axis=1)
    spectrum[...] = dot(forward, jnp.concatenate([masked, masked], axis=0))
    wait(3)


def taps_spectrum(taps, lengths, kept, after):
    window, (count, width) = kept[0].shape[0], taps.shape
    out = [pltpu.VMEM((window, width), jnp.float32)] + [pltpu.VMEM(k.shape, k.dtype) for k in kept]
    scratch = [
        pltpu.VMEM(taps.shape, taps.dtype),
        pltpu.VMEM(lengths.shape, lengths.dtype),
        pltpu.SemaphoreType.DMA((2 + len(kept),)),
    ]
    return call(
        taps_kernel, out, [whole()] + [whole(pltpu.HBM)] * (2 + len(kept)),
        4 * window * count * width, 5 << 20, 8, scratch,
    )(after, *far((taps, lengths, *kept)))


def shelve_kernel(got, own, gains, table, normed, chosen, lines):
    devices, per, _ = got.shape
    items, width = table.shape
    count = own.shape[1]

    group = 8 // per

    def one(index, carry):
        blocks = [got[index * group + i].astype(jnp.float32) for i in range(group)]
        lines[pl.ds(pl.multiple_of(index * 8, 8), 8), :] = jnp.concatenate(blocks, axis=0)
        return carry

    lax.fori_loop(0, devices // group, one, 0, unroll=4)
    rows = lines[:, :width]
    table[...] = rows.astype(jnp.bfloat16)
    scale = lax.rsqrt(jnp.mean(rows * rows, axis=-1, keepdims=True) + epsilon)
    normed[...] = (rows * scale * gains[0:1, :]).astype(jnp.bfloat16)

    device = lax.axis_index("row") * lax.axis_size("col") + lax.axis_index("col")
    wanted = jnp.maximum(device - 1, 0) * per
    line = lax.broadcasted_iota(jnp.int32, (8, items), 1)
    digit = lax.broadcasted_iota(jnp.int32, (8, items), 0)
    pick = jnp.logical_and(line == wanted + digit, digit < 2)
    pick = jnp.where(pick, 1.0, 0.0).astype(jnp.bfloat16)
    digits = dot(pick, lines[:, width:].astype(jnp.bfloat16))
    before = (digits[0:1] * id_base + digits[1:2]).astype(jnp.int32)
    ids = jnp.concatenate([before, own[...]], axis=1)
    hit = lax.broadcasted_iota(jnp.int32, (items, 2 * count), 0) == ids
    chosen[...] = jnp.where(hit, 1.0, 0.0).T.astype(jnp.bfloat16)


def shelve(got, own, gains):
    devices, per, lanes = got.shape
    items, width, count = devices * per, gains.shape[1], own.shape[1]
    rows = pltpu.VMEM((items, width), jnp.bfloat16)
    return call(
        shelve_kernel, (rows, rows, pltpu.VMEM((2 * count, items), jnp.bfloat16)),
        [whole()] * 3, 1 << 20, 1 << 19, 16, [pltpu.VMEM((items, lanes), jnp.float32)],
    )(got, own, gains)


def mix_kernel(begin_col, lengths, table, normed, chosen, gains, spectrum, forward, inverse, *refs):
    last = len(refs) == 3
    first_cols, hidden, inner = refs if last else (None, *refs, None)
    window = chosen.shape[0]
    count, half = window // 2, window // 2
    cols_here = hidden.shape[1] - begin_col if last else hidden.shape[1]
    first = (lax.axis_index("row") * lax.axis_size("col") + lax.axis_index("col")) * count
    base = begin_col if last else 0
    if last:
        hidden[:, :begin_col] = first_cols[...]
    hidden[:, base : base + cols_here] = dot(
        chosen[count:, :], table[:, begin_col : begin_col + cols_here]
    )

    at = lax.broadcasted_iota(jnp.int32, (window, 1), 0) + (first - count)

    def one_user(user, begin):
        end = begin + lengths[user]

        @pl.when(jnp.logical_and(begin < first + count, end > first))
        def _():
            inside = jnp.logical_and(at >= begin, at < end)
            picked = jnp.where(inside, chosen[...].astype(jnp.float32), 0.0).astype(jnp.bfloat16)
            for start in range(0, cols_here, mix_chunk):
                cols = pl.ds(begin_col + start, mix_chunk)
                x = dot(picked, normed[:, cols]).astype(jnp.bfloat16)
                seen = dot(forward[...], jnp.concatenate([x, x], axis=0))
                x_cos, x_sin = seen[:half], seen[half:]
                w_cos, w_sin = spectrum[:half, cols], spectrum[half:, cols]
                y = jnp.concatenate(
                    [x_cos * w_cos - x_sin * w_sin, x_cos * w_sin + x_sin * w_cos], axis=0
                )
                y_high = y.astype(jnp.bfloat16)
                y_low = (y - y_high.astype(jnp.float32)).astype(jnp.bfloat16)
                mixed = dot(inverse[...], jnp.concatenate([y_high, y_low, y_high], axis=0))
                cols = pl.ds(base + start, mix_chunk)
                hidden[:, cols] += jnp.where(inside[count:], mixed, 0.0)

        return end

    lax.fori_loop(0, lengths.shape[0], one_user, jnp.int32(0))
    if last:
        mixed = hidden[...]
        scale = lax.rsqrt(jnp.mean(mixed * mixed, axis=-1, keepdims=True) + epsilon)
        inner[...] = (mixed * scale * gains[1:2, :]).astype(jnp.bfloat16)


def mix(begin_col, cols_here, lengths, looked_up, gains, spectrum, tables, first_cols=None):
    (items, width), window = looked_up[0].shape, looked_up[2].shape[0]
    operands = [lengths, *near(looked_up), gains, spectrum, *near(tables)]
    if first_cols is None:
        out = shape(window // 2, cols_here, jnp.float32)
    else:
        operands.append(first_cols)
        out = (shape(window // 2, width, jnp.float32), shape(window // 2, width))
    return call(
        functools.partial(mix_kernel, begin_col),
        out,
        [whole(pltpu.SMEM)] + [whole()] * (len(operands) - 1),
        8 * cols_here * window * window,
        4 << 20,
        10,
    )(*operands)


def col_route(lane, place):
    pairs = []
    for device in range(lax.axis_size("col")):
        target = place(device // 2)
        if target is not None:
            pairs.append((device, target * 2 + (device % 2 ^ lane)))
    return pairs


def partner(block):
    return lax.ppermute(block, "row", [(i, i ^ 1) for i in range(lax.axis_size("row"))])


def rows_half(block, which):
    cut = block.shape[0] // 2

    def kernel(source, out):
        out[...] = source[which * cut : (which + 1) * cut, :]

    return call(
        kernel, pltpu.VMEM((cut, block.shape[1]), block.dtype), [whole()], 0, 1 << 16, 2
    )(*near([block]))


def travel(own):
    ends = (0, 3)
    side = col_route(0, lambda p: p ^ 1)
    outward = col_route(0, lambda p: None if p in ends else p ^ 1)
    over_ends = col_route(1, lambda p: p if p in ends else None)
    over_middle = col_route(1, lambda p: None if p in ends else p)
    turn = over_ends + col_route(0, lambda p: None if p in ends else 3 - p)

    def send(block, route):
        return lax.ppermute(block, "col", route)

    b = send(own, side)
    m = send(own, turn)
    a = send(own, over_middle)
    c = send(m, side)
    d = send(b, turn)
    e = send(m, over_middle)
    f = send(d, outward)
    g = send(c, turn)
    t = send(rows_half(g, 0), outward)
    u = send(rows_half(f, 1), over_ends)
    mine = [b, m, c, d, g, a, f, e, t, u]
    return mine, [partner(block) for block in mine]


def travelled(shares, mine, theirs, depth):
    core = lax.axis_index("row") % 2
    col = lax.axis_index("col")
    lane, place = col % 2, col // 2
    near = jnp.where(place % 2 == 0, place + 1, place - 1)
    middle = jnp.logical_or(place == 1, place == 2)
    at = lambda p, other: p * 2 + (1 - lane if other else lane)
    either = lambda p, q: jnp.where(middle, p, q)
    order = [
        col,
        at(near, False),
        either(at(3 - place, False), at(place, True)),
        either(at(near, True), at(3 - near, False)),
        either(at(3 - near, False), at(near, True)),
        at(3 - near, True),
        either(at(place, True), at(3 - place, False)),
        at(3 - place, True),
    ]
    half = mine[0].shape[1]

    def read(weight, part, start, size, span):
        rows, cols = slice(weight * depth, (weight + 1) * depth), slice(start, start + size)
        offset = (core if part == 0 else 1 - core) * half + start
        pieces = mine if part == 0 else theirs
        blocks = []
        for i in span:
            if i == 0:
                block = shares[weight][:, pl.ds(pl.multiple_of(offset, size), size)]
            elif i < 6:
                block = pieces[i - 1][rows, cols]
            elif i == 6:
                block = jnp.where(middle, pieces[5][rows, cols], pieces[6][rows, cols])
            else:
                ends = [pieces[8], pieces[9]]
                cut, parts = ends[0].shape[0], []
                for at_row, piece in zip((0, cut), ends):
                    low, high = max(rows.start, at_row) - at_row, min(rows.stop, at_row + cut) - at_row
                    if low < high:
                        parts.append(piece[low:high, cols])
                block = jnp.where(middle, pieces[7][rows, cols], jnp.concatenate(parts, axis=0))
            blocks.append(block)
        return jnp.concatenate(blocks, axis=0)

    def own_cols(part, start, size):
        offset = (core if part == 0 else 1 - core) * half + start
        return pl.ds(pl.multiple_of(offset, size), size)

    def in_order(source, ordered):
        for i, index in enumerate(order):
            cols = pl.ds(pl.multiple_of(index * depth, depth), depth)
            ordered[:, i * depth : (i + 1) * depth] = source[:, cols]

    spots = [(part, start) for part in range(2) for start in range(0, half, lane_chunk)]
    return spots, read, own_cols, in_order


def open_kernel(inner, *refs):
    pieces, (ordered, gate_sums, up_sums) = refs[:-3], refs[-3:]
    shares, mine, theirs = pieces[:2], pieces[2:9], pieces[9:]
    depth = shares[0].shape[0]
    spots, read, _, in_order = travelled(shares, mine, theirs, depth)
    in_order(inner, ordered)
    x = ordered[:, : 7 * depth]
    for i, (part, start) in enumerate(spots):
        cols = slice(i * lane_chunk, (i + 1) * lane_chunk)
        gate_sums[:, cols] = dot(x, read(0, part, start, lane_chunk, range(7)))
        up_sums[:, cols] = dot(x, read(1, part, start, lane_chunk, range(7)))


def close_kernel(hidden, given, gate_sums, up_sums, *refs):
    pieces, (out, ordered, active) = refs[:-3], refs[-3:]
    shares, mine, theirs = pieces[:1], pieces[1:11], pieces[11:]
    depth = shares[0].shape[0]
    spots, read, own_cols, in_order = travelled([None, None, *shares], mine, theirs, depth)
    x = given[:, 7 * depth :]
    for i, (part, start) in enumerate(spots):
        cols = slice(i * lane_chunk, (i + 1) * lane_chunk)
        gate_sum = gate_sums[:, cols] + dot(x, read(0, part, start, lane_chunk, (7,)))
        up_sum = up_sums[:, cols] + dot(x, read(1, part, start, lane_chunk, (7,)))
        active[:, own_cols(part, start, lane_chunk)] = (
            gate_sum / (1.0 + jnp.exp(-gate_sum)) * up_sum
        ).astype(jnp.bfloat16)
    in_order(active, ordered)
    x = ordered[...]
    for part, start in spots:
        cols = own_cols(part, start, lane_chunk)
        out[:, cols] = (hidden[:, cols] + dot(x, read(2, part, start, lane_chunk, range(8)))).astype(
            jnp.bfloat16
        )


def hop_feed(inner, hidden, shares, mine, theirs):
    (count, width), inside = inner.shape, shares[0].shape[1]
    sums = shape(count, inside, jnp.float32)
    early = [*shares[:2], *mine[:7], *theirs[:7]]
    ordered, gate_sums, up_sums = call(
        open_kernel, (shape(count, width), sums, sums), [whole()] * (1 + len(early)),
        4 * count * width * inside, 4 << 20, 8,
    )(inner, *early)
    late = [hidden, ordered, gate_sums, up_sums, shares[2], *mine, *theirs]
    scratch = [pltpu.VMEM((count, inside), jnp.bfloat16), pltpu.VMEM((count, inside), jnp.bfloat16)]
    return call(
        close_kernel, shape(count, width), [whole()] * len(late),
        2 * count * width * inside, 4 << 20, 8, scratch,
    )(*late)


def plain_feed_kernel(inner, hidden, gate, up, down, out, active):
    for start in range(0, gate.shape[1], lane_chunk):
        cols = slice(start, start + lane_chunk)
        gate_sum, up_sum = dot(inner[...], gate[:, cols]), dot(inner[...], up[:, cols])
        active[:, cols] = (gate_sum / (1.0 + jnp.exp(-gate_sum)) * up_sum).astype(jnp.bfloat16)
    for start in range(0, down.shape[1], lane_chunk):
        cols = slice(start, start + lane_chunk)
        out[:, cols] = (hidden[:, cols] + dot(active[...], down[:, cols])).astype(jnp.bfloat16)


def plain_feed(inner, hidden, pieces):
    (count, width), inside = inner.shape, pieces[0].shape[1]
    return call(
        plain_feed_kernel, shape(count, width), [whole()] * 5,
        6 * count * width * inside, 8 << 20, 28, [pltpu.VMEM((count, inside), jnp.bfloat16)],
    )(inner, hidden, *pieces)


def body(item_ids, user_lengths, catalogue, tap_lengths, conv_taps, norm_gains,
         gate_weight, up_weight, down_weight):
    count, width = item_ids.shape[0], catalogue.shape[1]
    weights = (gate_weight, up_weight, down_weight)
    shares = [w[0] for w in weights]
    by_hops = travels()
    if by_hops:
        mine, theirs = travel(pack(*shares))
    sent, ids, gains = greet(item_ids[None], norm_gains[0], catalogue)
    got = lax.all_to_all(sent, both, 0, 0)
    looked_up = shelve(got, ids, gains)
    tables = [*map(jnp.asarray, transform_tables(2 * count, count))]
    spectrum, *tables = taps_spectrum(conv_taps[0], tap_lengths, tables, looked_up[2])
    common = (user_lengths, looked_up, gains, spectrum, tables)
    first_cols = mix(0, width // 2, *common)
    hidden, inner = mix(width // 2, width // 2, *common, first_cols)
    if by_hops:
        return hop_feed(inner, hidden, shares, mine, theirs)
    return plain_feed(
        inner, hidden, [lax.all_gather(w[0], "col", axis=0, tiled=True) for w in weights]
    )


def travels():
    return lax.axis_size("col") == 8 and lax.axis_size("row") % 2 == 0


def solution(mesh):
    by_device = P(both)
    by_col = P(None, "col", None)
    return jax.shard_map(
        body,
        mesh=mesh,
        in_specs=(by_device, P(), P(both, None), P(), P(), P(), by_col, by_col, by_col),
        out_specs=P(both, None),
        check_vma=False,
    )
```

time: 75.2 us -> 64.6 us (0.86)
  local copies, waits for them, and re-layouts: 5.9 us -> 1.42 us
  waiting for transfers between devices: 14.2 us -> 9.99 us
  Pallas kernels: 22.9 us -> 21.4 us
    ppermute x10, waiting for transfers between devices: 14.2 us -> 9.96 us  [send(): return lax.ppermute(block, 'col', route)]
    unnamed x32 -> x14, local copies, waits for them, and re-layouts: 3.42 us -> 1.42 us
    pallas_call x6 -> x10, Pallas kernels: 22.9 us -> 21.4 us  [the longest x2 7.94 us: mix(): call(functools.partial(mix_kernel, begin_col), out, [whole(pltpu.SMEM)] +...]
    slice x2 -> x0, local copies, waits for them, and re-layouts: 1.37 us -> none  [the longest x1 0.69 us: travel(): t = send(g[:cut], outward)]
    reshape x1 -> x0, local copies, waits for them, and re-layouts: 1.12 us -> none  [body(): table = lax.all_to_all(sent, both, 0, 0).reshape(-1, width)]
    ppermute x10, starting transfers between devices: 17.9 us -> 16.9 us  [send(): return lax.ppermute(block, 'col', route)]
  transfers between devices with their start and end apart: 21 -> 21, of which waited for: 4 -> 4; matrix products, arithmetic and copies ran while one was open for 3% -> 0% of each run, Pallas kernels for 23% -> 26%
where the time goes in v2:
time: 64.6 us; the launch traced here: 64.2 us
  starting transfers between devices  31.2 us (48%)
  Pallas kernels  21.4 us (33%)
  waiting for transfers between devices  9.99 us (15%)
  local copies, waits for them, and re-layouts  1.42 us (2%)
    ppermute x10, starting transfers between devices, send(): return lax.ppermute(block, 'col', route)  16.9 us
    ppermute x10, waiting for transfers between devices, send(): return lax.ppermute(block, 'col', route)  9.96 us
    ppermute x10, starting transfers between devices, partner(): lax.ppermute(block, 'row', [(i, i ^ 1) for i in range(lax.axis_size('row'...  9.19 us
    pallas_call x2, Pallas kernels, mix(): call(functools.partial(mix_kernel, begin_col), out, [whole(pltpu.SMEM)] +...  7.94 us
    all_to_all x1, starting transfers between devices, body(): got = lax.all_to_all(sent, both, 0, 0)  5.04 us
    pallas_call x1, Pallas kernels, hop_feed(): call(close_kernel, shape(count, width), [whole()] * len(late), 2 * count...  3.86 us
    pallas_call x1, Pallas kernels, hop_feed(): call(open_kernel, (shape(count, width), sums, sums), [whole()] * (1 + len...  2.72 us
    pallas_call x1, Pallas kernels, taps_spectrum(): call(taps_kernel, out, [whole()] + [whole(pltpu.HBM)] * (2 + len(kept)),...  2.14 us
  transfers between devices with their start and end apart: 21, of which 4 were waited for; matrix products, arithmetic and copies ran while one was open for 0% of the time, Pallas kernels for 26%

profile of v2, /device:TPU:19, one launch (start us, length us, event | category | flops | bytes accessed | tf_op | source)
XLA Modules:
  0.0 64.2 jit_solution(15851817500502504112)
XLA Ops:
  0.0 1.1 %shard_map.114 = bf16[384,512]{1,0:T(8,128)(2,1)S(1)} custom-call(bf16[128,1024]{1,0:T(8,128)(2,1)} %bitcast.6, bf16[128,1024]{1,0:T(8,128)(2,1)} %bitcast.8, bf16[128,1024]{1,0:T(8,128)(2,1)} %bitcast.10), custom_call_target="tpu_custom_call" | custom-call | bytes 1048576 | tf_op jit(solution)/shard_map/pallas_call | solution.py:87
  1.1 0.2 collective-permute-start.1
  1.3 2.4 %collective-permute-start = (bf16[384,512]{1,0:T(8,128)(2,1)S(1)}, bf16[384,512]{1,0:T(8,128)(2,1)S(1)}, u32[]{:S(2)}, u32[]{:S(2)}) collective-permute-start(bf16[384,512]{1,0:T(8,128)(2,1)S(1)} %shard_map.114), channel_id=1, source_target_pairs={{0,2},{1,3},{2,0},{3,1},{4,6},{5,7},{6,4},{7,5},{8,10},{9,11},{10,... | collective-permute-start | bytes 1179656 | tf_op jit(solution)/shard_map/ppermute | solution.py:287
  3.7 2.1 %collective-permute-start.5 = (bf16[384,512]{1,0:T(8,128)(2,1)S(1)}, bf16[384,512]{1,0:T(8,128)(2,1)S(1)}, u32[]{:S(2)}, u32[]{:S(2)}) collective-permute-start(bf16[384,512]{1,0:T(8,128)(2,1)S(1)} %shard_map.114), channel_id=1, source_target_pairs={{2,3},{3,2},{4,5},{5,4},{10,11},{11,10},{12,13},{13,12},{18,19},{1... | collective-permute-start | bytes 1179656 | tf_op jit(solution)/shard_map/ppermute | solution.py:287
  5.8 5.3 %collective-permute-done.1.refs_3_.refs_2_ = bf16[384,512]{1,0:T(8,128)(2,1)S(1)} collective-permute-done((bf16[384,512]{1,0:T(8,128)(2,1)S(1)}, bf16[384,512]{1,0:T(8,128)(2,1)S(1)}, u32[]{:S(2)}, u32[]{:S(2)}) %collective-permute-start.1) | collective-permute-done | bytes 393248 | tf_op jit(solution)/shard_map/ppermute | solution.py:287
  11.1 1.3 %collective-permute-start.2 = (bf16[384,512]{1,0:T(8,128)(2,1)S(1)}, bf16[384,512]{1,0:T(8,128)(2,1)S(1)}, u32[]{:S(2)}, u32[]{:S(2)}) collective-permute-start(bf16[384,512]{1,0:T(8,128)(2,1)S(1)} %collective-permute-done.1.refs_3_.refs_2_), channel_id=1, source_target_pairs={{0,2},{1,3},{2,0},{3,1},{4,6},{5,7},{6,4},{7,5},{8,10},{9,11},{10,... | collective-permute-start | bytes 1179656 | tf_op jit(solution)/shard_map/ppermute | solution.py:287
  12.4 0.0 collective-permute-done.refs_2_.refs_1_
  12.4 2.0 %collective-permute-start.8 = (bf16[384,512]{1,0:T(8,128)(2,1)S(1)}, bf16[384,512]{1,0:T(8,128)(2,1)S(1)}, u32[]{:S(2)}, u32[]{:S(2)}) collective-permute-start(bf16[384,512]{1,0:T(8,128)(2,1)S(1)} %collective-permute-done.1.refs_3_.refs_2_), channel_id=1, source_target_pairs={{0,8},{8,0},{16,24},{24,16},{1,9},{9,1},{17,25},{25,17},{2,10},{10... | collective-permute-start | bytes 1179656 | tf_op jit(solution)/shard_map/ppermute | solution.py:264
  14.4 0.6 collective-permute-done.5.refs_7_.refs_6_
  15.0 2.1 %collective-permute-start.12 = (bf16[384,512]{1,0:T(8,128)(2,1)S(1)}, bf16[384,512]{1,0:T(8,128)(2,1)S(1)}, u32[]{:S(2)}, u32[]{:S(2)}) collective-permute-start(bf16[384,512]{1,0:T(8,128)(2,1)S(1)} %collective-permute-done.5.refs_7_.refs_6_), channel_id=1, source_target_pairs={{0,8},{8,0},{16,24},{24,16},{1,9},{9,1},{17,25},{25,17},{2,10},{10... | collective-permute-start | bytes 1179656 | tf_op jit(solution)/shard_map/ppermute | solution.py:264
  17.1 3.2 %collective-permute-done.2.refs_4_.refs_3_ = bf16[384,512]{1,0:T(8,128)(2,1)S(1)} collective-permute-done((bf16[384,512]{1,0:T(8,128)(2,1)S(1)}, bf16[384,512]{1,0:T(8,128)(2,1)S(1)}, u32[]{:S(2)}, u32[]{:S(2)}) %collective-permute-start.2) | collective-permute-done | bytes 393248 | tf_op jit(solution)/shard_map/ppermute | solution.py:287
  20.3 0.2 collective-permute-start.4
  20.4 0.9 %collective-permute-done.3.refs_5_.refs_4_ = bf16[384,512]{1,0:T(8,128)(2,1)S(1)} collective-permute-done((bf16[384,512]{1,0:T(8,128)(2,1)S(1)}, bf16[384,512]{1,0:T(8,128)(2,1)S(1)}, u32[]{:S(2)}, u32[]{:S(2)}) %collective-permute-start.3) | collective-permute-done | bytes 393248 | tf_op jit(solution)/shard_map/ppermute | solution.py:287
  21.3 3.4 %collective-permute-start.6 = (bf16[384,512]{1,0:T(8,128)(2,1)S(1)}, bf16[384,512]{1,0:T(8,128)(2,1)S(1)}, u32[]{:S(2)}, u32[]{:S(2)}) collective-permute-start(bf16[384,512]{1,0:T(8,128)(2,1)S(1)} %collective-permute-done.3.refs_5_.refs_4_), channel_id=1, source_target_pairs={{2,0},{3,1},{4,6},{5,7},{10,8},{11,9},{12,14},{13,15},{18,16},{19,... | collective-permute-start | bytes 1179656 | tf_op jit(solution)/shard_map/ppermute | solution.py:287
  24.7 0.0 collective-permute-done.8.refs_10_.refs_12_
  24.7 2.1 %collective-permute-start.14 = (bf16[384,512]{1,0:T(8,128)(2,1)S(1)}, bf16[384,512]{1,0:T(8,128)(2,1)}, u32[]{:S(2)}, u32[]{:S(2)}) collective-permute-start(bf16[384,512]{1,0:T(8,128)(2,1)S(1)} %collective-permute-done.1.refs_3_.refs_2_), channel_id=1, source_target_pairs={{2,3},{3,2},{4,5},{5,4},{10,11},{11,10},{12,13},{13,12},{18,19},{1... | collective-permute-start | bytes 1179656 | tf_op jit(solution)/shard_map/ppermute | solution.py:287
  26.9 3.3 %collective-permute-start.9 = (bf16[384,512]{1,0:T(8,128)(2,1)S(1)}, bf16[384,512]{1,0:T(8,128)(2,1)}, u32[]{:S(2)}, u32[]{:S(2)}) collective-permute-start(bf16[384,512]{1,0:T(8,128)(2,1)S(1)} %collective-permute-done.2.refs_4_.refs_3_), channel_id=1, source_target_pairs={{0,8},{8,0},{16,24},{24,16},{1,9},{9,1},{17,25},{25,17},{2,10},{10... | collective-permute-start | bytes 1179656 | tf_op jit(solution)/shard_map/ppermute | solution.py:264
  30.2 0.0 collective-permute-done.12.refs_14_.refs_16_
  30.2 0.7 %copy-done = bf16[384,512]{1,0:T(8,128)(2,1)} copy-done((bf16[384,512]{1,0:T(8,128)(2,1)}, bf16[384,512]{1,0:T(8,128)(2,1)S(1)}, u32[]{:S(2)}) %copy-start) | copy-done | bytes 393240
  30.9 0.0 collective-permute-start.10
  31.0 1.0 %shard_map.109 = (bf16[32,2,1280]{2,1,0:T(2,128)(2,1)S(1)}, s32[1,256]{1,0:T(1,128)S(1)}, f32[2,1024]{1,0:T(2,128)S(1)}) custom-call(s32[1,256]{1,0:T(1,128)} %bitcast.14, f32[2,1024]{1,0:T(2,128)} %bitcast.13, bf16[2,1024]{1,0:T(2,128)(2,1)} %rows_far.1), custom_call_target="tpu_custom_call" | custom-call | bytes 262144 | tf_op jit(solution)/shard_map/pallas_call | solution.py:116
  32.0 0.6 %copy-done.5 = bf16[32,2,1280]{2,1,0:T(2,128)(2,1)} copy-done((bf16[32,2,1280]{2,1,0:T(2,128)(2,1)}, bf16[32,2,1280]{2,1,0:T(2,128)(2,1)S(1)}, u32[]{:S(2)}) %copy-start.5) | copy-done | bytes 163864
  32.6 5.0 %all-to-all-start = ((bf16[32,2,1280]{2,1,0:T(2,128)(2,1)}), bf16[32,2,1280]{2,1,0:T(2,128)(2,1)}, u32[]{:S(2)}, u32[]{:S(2)}) async-start(bf16[32,2,1280]{2,1,0:T(2,128)(2,1)} %copy-done.5), calls=%async_computation | async-start | bytes 327680 | tf_op jit(solution)/shard_map/all_to_all | solution.py:437
  37.7 0.0 collective-permute-done.4.refs_6_.source.refs_5_
  37.7 0.5 collective-permute-start.11
  38.2 0.1 collective-permute-start.13
  38.3 0.7 %shard_map.116 = bf16[192,512]{1,0:T(8,128)(2,1)} custom-call(bf16[384,512]{1,0:T(8,128)(2,1)S(1)} %collective-permute-done.4.refs_6_.source.refs_5_), custom_call_target="tpu_custom_call" | custom-call | bytes 65536 | tf_op jit(solution)/shard_map/pallas_call | solution.py:273
  39.0 0.7 %shard_map.117 = bf16[192,512]{1,0:T(8,128)(2,1)} custom-call(bf16[384,512]{1,0:T(8,128)(2,1)S(1)} %collective-permute-done.6.refs_8_.source.refs_7_), custom_call_target="tpu_custom_call" | custom-call | bytes 65536 | tf_op jit(solution)/shard_map/pallas_call | solution.py:273
  39.6 0.0 collective-permute-done.14.refs_8_
  39.6 3.8 %collective-permute-start.15 = (bf16[192,512]{1,0:T(8,128)(2,1)}, bf16[192,512]{1,0:T(8,128)(2,1)}, u32[]{:S(2)}, u32[]{:S(2)}) collective-permute-start(bf16[192,512]{1,0:T(8,128)(2,1)} %shard_map.116), channel_id=1, source_target_pairs={{2,0},{3,1},{4,6},{5,7},{10,8},{11,9},{12,14},{13,15},{18,16},{19,... | collective-permute-start | bytes 589832 | tf_op jit(solution)/shard_map/ppermute | solution.py:287
  43.5 0.0 collective-permute-done.9.refs_11_.refs_13_
  43.5 1.3 %collective-permute-start.16 = (bf16[192,512]{1,0:T(8,128)(2,1)}, bf16[192,512]{1,0:T(8,128)(2,1)}, u32[]{:S(2)}, u32[]{:S(2)}) collective-permute-start(bf16[192,512]{1,0:T(8,128)(2,1)} %shard_map.117), channel_id=1, source_target_pairs={{0,1},{1,0},{6,7},{7,6},{8,9},{9,8},{14,15},{15,14},{16,17},{17,16... | collective-permute-start | bytes 589832 | tf_op jit(solution)/shard_map/ppermute | solution.py:287
  44.8 0.7 %collective-permute-start.17 = (bf16[384,512]{1,0:T(8,128)(2,1)}, bf16[384,512]{1,0:T(8,128)(2,1)}, u32[]{:S(2)}, u32[]{:S(2)}) collective-permute-start(bf16[384,512]{1,0:T(8,128)(2,1)} %collective-permute-done.14.refs_8_), channel_id=1, source_target_pairs={{0,8},{8,0},{16,24},{24,16},{1,9},{9,1},{17,25},{25,17},{2,10},{10... | collective-permute-start | bytes 1179656 | tf_op jit(solution)/shard_map/ppermute | solution.py:264
  45.5 0.0 all-to-all-done.got
  45.5 1.3 %shard_map.110 = (bf16[64,1024]{1,0:T(8,128)(2,1)S(1)}, bf16[64,1024]{1,0:T(8,128)(2,1)S(1)}, bf16[512,64]{1,0:T(8,128)(2,1)S(1)}) custom-call(bf16[32,2,1280]{2,1,0:T(2,128)(2,1)} %all-to-all-done.got, s32[1,256]{1,0:T(1,128)S(1)} %get-tuple-element.20.own, f32[2,1024]{1,0:T(2,128)S(1)} %get-tuple-element.21.gains), custom_call_target="tpu_custom_call" | custom-call | flops 1048576 | bytes 524288 | tf_op jit(solution)/shard_map/pallas_call | solution.py:183
  46.8 2.1 %shard_map.111 = (f32[512,1024]{1,0:T(8,128)S(1)}, bf16[512,1024]{1,0:T(8,128)(2,1)S(1)}, bf16[256,1536]{1,0:T(8,128)(2,1)S(1)}) custom-call(bf16[512,64]{1,0:T(8,128)(2,1)S(1)} %get-tuple-element.24.after.chosen, bf16[256,1024]{1,0:T(8,128)(2,1)} %bitcast.12, s32[1,1024]{1,0:T(1,128)} %lengths_far.1, bf16[512,1024]{1,0:T(8,128)(2,1)} %constant.4.clone.refs_0_, ...), custom_call_target="tpu_custom_call" | custom-call | flops 536870912 | bytes 5242880 | tf_op jit(solution)/shard_map/pallas_call | solution.py:142
  48.9 3.9 %shard_map.112.refs_0_ = f32[256,512]{1,0:T(8,128)S(1)} custom-call(s32[8]{0:T(128)S(1)} %copy-done.6, bf16[64,1024]{1,0:T(8,128)(2,1)S(1)} %get-tuple-element.22.table, bf16[64,1024]{1,0:T(8,128)(2,1)S(1)} %get-tuple-element.23.normed, bf16[512,64]{1,0:T(8,128)(2,1)S(1)} %get-tuple-element.24.after.chosen, f32[2,1024]{1,0:T(2,128)S(1)} %get-tuple-element.21.gains, ...), custom_call_target="tpu_custom_call" | custom-call | flops 1073741824 | bytes 4194304 | tf_op jit(solution)/shard_map/pallas_call | solution.py:244
  52.8 0.0 copy-start.1
  52.8 0.0 copy-start.2
  52.8 0.0 copy-start.3
  52.8 0.0 collective-permute-done.15.refs_9_
  52.8 0.1 collective-permute-start.18
  52.9 0.5 collective-permute-start.19
  53.4 4.1 %shard_map.113 = (f32[256,1024]{1,0:T(8,128)S(1)}, bf16[256,1024]{1,0:T(8,128)(2,1)S(1)}) custom-call(s32[8]{0:T(128)S(1)} %copy-done.6, bf16[64,1024]{1,0:T(8,128)(2,1)S(1)} %get-tuple-element.22.table, bf16[64,1024]{1,0:T(8,128)(2,1)S(1)} %get-tuple-element.23.normed, bf16[512,64]{1,0:T(8,128)(2,1)S(1)} %get-tuple-element.24.after.chosen, ...), custom_call_target="tpu_custom_call" | custom-call | flops 1073741824 | bytes 4194304 | tf_op jit(solution)/shard_map/pallas_call | solution.py:244
  57.5 0.0 collective-permute-done.11.refs_13_.refs_15_
  57.6 0.0 copy-start.4
  57.6 2.7 %shard_map.115 = (bf16[256,1024]{1,0:T(8,128)(2,1)S(1)}, f32[256,1024]{1,0:T(8,128)S(1)}, f32[256,1024]{1,0:T(8,128)S(1)}) custom-call(bf16[256,1024]{1,0:T(8,128)(2,1)S(1)} %get-tuple-element.29.inner, bf16[128,1024]{1,0:T(8,128)(2,1)S(1)} %bitcast.7, bf16[128,1024]{1,0:T(8,128)(2,1)S(1)} %bitcast.9, ...), custom_call_target="tpu_custom_call" | custom-call | flops 1073741824 | bytes 4194304 | tf_op jit(solution)/shard_map/pallas_call | solution.py:398
  60.3 3.9 %shard_map.118 = bf16[256,1024]{1,0:T(8,128)(2,1)} custom-call(f32[256,1024]{1,0:T(8,128)S(1)} %get-tuple-element.28.hidden, bf16[256,1024]{1,0:T(8,128)(2,1)S(1)} %get-tuple-element.30.given, f32[256,1024]{1,0:T(8,128)S(1)} %get-tuple-element.31.gate_sums, f32[256,1024]{1,0:T(8,128)S(1)} %get-tuple-element.32.up_sums, bf16[128,1024]{1,0:T(8,128)(2,1)S(1)} %bitcast.11, ...), custom_call_target="tpu_custom_call" | custom-call | flops 536870912 | bytes 4194304 | tf_op jit(solution)/shard_map/pallas_call | solution.py:404
  (18 shorter events, 0.0 us)
Async XLA Ops:
  1.1 10.1 %collective-permute-start.1 = (bf16[384,512]{1,0:T(8,128)(2,1)S(1)}, bf16[384,512]{1,0:T(8,128)(2,1)S(1)}, u32[]{:S(2)}, u32[]{:S(2)}) collective-permute-start(bf16[384,512]{1,0:T(8,128)(2,1)S(1)} %shard_map.114), channel_id=1, source_target_pairs={{0,1},{1,0},{6,7},{7,6},{2,4},{3,5},{4,2},{5,3},{8,9},{9,8},{14,15... | collective-permute-start | bytes 1179656 | tf_op jit(solution)/shard_map/ppermute | solution.py:287
  1.3 11.1 %collective-permute-start = (bf16[384,512]{1,0:T(8,128)(2,1)S(1)}, bf16[384,512]{1,0:T(8,128)(2,1)S(1)}, u32[]{:S(2)}, u32[]{:S(2)}) collective-permute-start(bf16[384,512]{1,0:T(8,128)(2,1)S(1)} %shard_map.114), channel_id=1, source_target_pairs={{0,2},{1,3},{2,0},{3,1},{4,6},{5,7},{6,4},{7,5},{8,10},{9,11},{10,... | collective-permute-start | bytes 1179656 | tf_op jit(solution)/shard_map/ppermute | solution.py:287
  3.7 11.3 %collective-permute-start.5 = (bf16[384,512]{1,0:T(8,128)(2,1)S(1)}, bf16[384,512]{1,0:T(8,128)(2,1)S(1)}, u32[]{:S(2)}, u32[]{:S(2)}) collective-permute-start(bf16[384,512]{1,0:T(8,128)(2,1)S(1)} %shard_map.114), channel_id=1, source_target_pairs={{2,3},{3,2},{4,5},{5,4},{10,11},{11,10},{12,13},{13,12},{18,19},{1... | collective-permute-start | bytes 1179656 | tf_op jit(solution)/shard_map/ppermute | solution.py:287
  11.1 9.1 %collective-permute-start.2 = (bf16[384,512]{1,0:T(8,128)(2,1)S(1)}, bf16[384,512]{1,0:T(8,128)(2,1)S(1)}, u32[]{:S(2)}, u32[]{:S(2)}) collective-permute-start(bf16[384,512]{1,0:T(8,128)(2,1)S(1)} %collective-permute-done.1.refs_3_.refs_2_), channel_id=1, source_target_pairs={{0,2},{1,3},{2,0},{3,1},{4,6},{5,7},{6,4},{7,5},{8,10},{9,11},{10,... | collective-permute-start | bytes 1179656 | tf_op jit(solution)/shard_map/ppermute | solution.py:287
  12.4 8.9 %collective-permute-start.3 = (bf16[384,512]{1,0:T(8,128)(2,1)S(1)}, bf16[384,512]{1,0:T(8,128)(2,1)S(1)}, u32[]{:S(2)}, u32[]{:S(2)}) collective-permute-start(bf16[384,512]{1,0:T(8,128)(2,1)S(1)} %collective-permute-done.refs_2_.refs_1_), channel_id=1, source_target_pairs={{0,1},{1,0},{6,7},{7,6},{2,4},{3,5},{4,2},{5,3},{8,9},{9,8},{14,15... | collective-permute-start | bytes 1179656 | tf_op jit(solution)/shard_map/ppermute | solution.py:287
  12.4 12.3 %collective-permute-start.8 = (bf16[384,512]{1,0:T(8,128)(2,1)S(1)}, bf16[384,512]{1,0:T(8,128)(2,1)S(1)}, u32[]{:S(2)}, u32[]{:S(2)}) collective-permute-start(bf16[384,512]{1,0:T(8,128)(2,1)S(1)} %collective-permute-done.1.refs_3_.refs_2_), channel_id=1, source_target_pairs={{0,8},{8,0},{16,24},{24,16},{1,9},{9,1},{17,25},{25,17},{2,10},{10... | collective-permute-start | bytes 1179656 | tf_op jit(solution)/shard_map/ppermute | solution.py:264
  14.4 12.5 %collective-permute-start.7 = (bf16[384,512]{1,0:T(8,128)(2,1)S(1)}, bf16[384,512]{1,0:T(8,128)(2,1)S(1)}, u32[]{:S(2)}, u32[]{:S(2)}) collective-permute-start(bf16[384,512]{1,0:T(8,128)(2,1)S(1)} %collective-permute-done.refs_2_.refs_1_), channel_id=1, source_target_pairs={{0,8},{8,0},{16,24},{24,16},{1,9},{9,1},{17,25},{25,17},{2,10},{10... | collective-permute-start | bytes 1179656 | tf_op jit(solution)/shard_map/ppermute | solution.py:264
  15.0 15.2 %collective-permute-start.12 = (bf16[384,512]{1,0:T(8,128)(2,1)S(1)}, bf16[384,512]{1,0:T(8,128)(2,1)S(1)}, u32[]{:S(2)}, u32[]{:S(2)}) collective-permute-start(bf16[384,512]{1,0:T(8,128)(2,1)S(1)} %collective-permute-done.5.refs_7_.refs_6_), channel_id=1, source_target_pairs={{0,8},{8,0},{16,24},{24,16},{1,9},{9,1},{17,25},{25,17},{2,10},{10... | collective-permute-start | bytes 1179656 | tf_op jit(solution)/shard_map/ppermute | solution.py:264
  20.3 17.4 %collective-permute-start.4 = (bf16[384,512]{1,0:T(8,128)(2,1)S(1)}, bf16[384,512]{1,0:T(8,128)(2,1)S(1)}, u32[]{:S(2)}, u32[]{:S(2)}) collective-permute-start(bf16[384,512]{1,0:T(8,128)(2,1)S(1)} %collective-permute-done.2.refs_4_.refs_3_), channel_id=1, source_target_pairs={{0,1},{1,0},{6,7},{7,6},{2,4},{3,5},{4,2},{5,3},{8,9},{9,8},{14,15... | collective-permute-start | bytes 1179656 | tf_op jit(solution)/shard_map/ppermute | solution.py:287
  21.3 16.9 %collective-permute-start.6 = (bf16[384,512]{1,0:T(8,128)(2,1)S(1)}, bf16[384,512]{1,0:T(8,128)(2,1)S(1)}, u32[]{:S(2)}, u32[]{:S(2)}) collective-permute-start(bf16[384,512]{1,0:T(8,128)(2,1)S(1)} %collective-permute-done.3.refs_5_.refs_4_), channel_id=1, source_target_pairs={{2,0},{3,1},{4,6},{5,7},{10,8},{11,9},{12,14},{13,15},{18,16},{19,... | collective-permute-start | bytes 1179656 | tf_op jit(solution)/shard_map/ppermute | solution.py:287
  24.7 14.9 %collective-permute-start.14 = (bf16[384,512]{1,0:T(8,128)(2,1)S(1)}, bf16[384,512]{1,0:T(8,128)(2,1)}, u32[]{:S(2)}, u32[]{:S(2)}) collective-permute-start(bf16[384,512]{1,0:T(8,128)(2,1)S(1)} %collective-permute-done.1.refs_3_.refs_2_), channel_id=1, source_target_pairs={{2,3},{3,2},{4,5},{5,4},{10,11},{11,10},{12,13},{13,12},{18,19},{1... | collective-permute-start | bytes 1179656 | tf_op jit(solution)/shard_map/ppermute | solution.py:287
  26.9 16.6 %collective-permute-start.9 = (bf16[384,512]{1,0:T(8,128)(2,1)S(1)}, bf16[384,512]{1,0:T(8,128)(2,1)}, u32[]{:S(2)}, u32[]{:S(2)}) collective-permute-start(bf16[384,512]{1,0:T(8,128)(2,1)S(1)} %collective-permute-done.2.refs_4_.refs_3_), channel_id=1, source_target_pairs={{0,8},{8,0},{16,24},{24,16},{1,9},{9,1},{17,25},{25,17},{2,10},{10... | collective-permute-start | bytes 1179656 | tf_op jit(solution)/shard_map/ppermute | solution.py:264
  30.2 0.7 %copy-start = (bf16[384,512]{1,0:T(8,128)(2,1)}, bf16[384,512]{1,0:T(8,128)(2,1)S(1)}, u32[]{:S(2)}) copy-start(bf16[384,512]{1,0:T(8,128)(2,1)S(1)} %collective-permute-done.12.refs_14_.refs_16_) | copy-start | bytes 1179652
  30.9 13.9 %collective-permute-start.10 = (bf16[384,512]{1,0:T(8,128)(2,1)S(1)}, bf16[384,512]{1,0:T(8,128)(2,1)}, u32[]{:S(2)}, u32[]{:S(2)}) collective-permute-start(bf16[384,512]{1,0:T(8,128)(2,1)S(1)} %collective-permute-done.3.refs_5_.refs_4_), channel_id=1, source_target_pairs={{0,8},{8,0},{16,24},{24,16},{1,9},{9,1},{17,25},{25,17},{2,10},{10... | collective-permute-start | bytes 1179656 | tf_op jit(solution)/shard_map/ppermute | solution.py:264
  32.0 0.7 %copy-start.5 = (bf16[32,2,1280]{2,1,0:T(2,128)(2,1)}, bf16[32,2,1280]{2,1,0:T(2,128)(2,1)S(1)}, u32[]{:S(2)}) copy-start(bf16[32,2,1280]{2,1,0:T(2,128)(2,1)S(1)} %get-tuple-element.19) | copy-start | bytes 491524
  32.6 16.3 %copy-start.6 = (s32[8]{0:T(128)S(1)}, s32[8]{0:T(128)}, u32[]{:S(2)}) copy-start(s32[8]{0:T(128)} %lengths.3) | copy-start | bytes 100
  32.6 12.9 %all-to-all-start = ((bf16[32,2,1280]{2,1,0:T(2,128)(2,1)}), bf16[32,2,1280]{2,1,0:T(2,128)(2,1)}, u32[]{:S(2)}, u32[]{:S(2)}) async-start(bf16[32,2,1280]{2,1,0:T(2,128)(2,1)} %copy-done.5), calls=%async_computation | async-start | bytes 327680 | tf_op jit(solution)/shard_map/all_to_all | solution.py:437
  37.7 19.8 %collective-permute-start.11 = (bf16[384,512]{1,0:T(8,128)(2,1)S(1)}, bf16[384,512]{1,0:T(8,128)(2,1)}, u32[]{:S(2)}, u32[]{:S(2)}) collective-permute-start(bf16[384,512]{1,0:T(8,128)(2,1)S(1)} %collective-permute-done.4.refs_6_.source.refs_5_), channel_id=1, source_target_pairs={{0,8},{8,0},{16,24},{24,16},{1,9},{9,1},{17,25},{25,17},{2,10},{10... | collective-permute-start | bytes 1179656 | tf_op jit(solution)/shard_map/ppermute | solution.py:264
  38.2 19.4 %collective-permute-start.13 = (bf16[384,512]{1,0:T(8,128)(2,1)S(1)}, bf16[384,512]{1,0:T(8,128)(2,1)}, u32[]{:S(2)}, u32[]{:S(2)}) collective-permute-start(bf16[384,512]{1,0:T(8,128)(2,1)S(1)} %collective-permute-done.6.refs_8_.source.refs_7_), channel_id=1, source_target_pairs={{0,8},{8,0},{16,24},{24,16},{1,9},{9,1},{17,25},{25,17},{2,10},{10... | collective-permute-start | bytes 1179656 | tf_op jit(solution)/shard_map/ppermute | solution.py:264
  39.6 13.2 %collective-permute-start.15 = (bf16[192,512]{1,0:T(8,128)(2,1)}, bf16[192,512]{1,0:T(8,128)(2,1)}, u32[]{:S(2)}, u32[]{:S(2)}) collective-permute-start(bf16[192,512]{1,0:T(8,128)(2,1)} %shard_map.116), channel_id=1, source_target_pairs={{2,0},{3,1},{4,6},{5,7},{10,8},{11,9},{12,14},{13,15},{18,16},{19,... | collective-permute-start | bytes 589832 | tf_op jit(solution)/shard_map/ppermute | solution.py:287
  43.5 9.4 %collective-permute-start.16 = (bf16[192,512]{1,0:T(8,128)(2,1)}, bf16[192,512]{1,0:T(8,128)(2,1)}, u32[]{:S(2)}, u32[]{:S(2)}) collective-permute-start(bf16[192,512]{1,0:T(8,128)(2,1)} %shard_map.117), channel_id=1, source_target_pairs={{0,1},{1,0},{6,7},{7,6},{8,9},{9,8},{14,15},{15,14},{16,17},{17,16... | collective-permute-start | bytes 589832 | tf_op jit(solution)/shard_map/ppermute | solution.py:287
  44.8 15.5 %collective-permute-start.17 = (bf16[384,512]{1,0:T(8,128)(2,1)}, bf16[384,512]{1,0:T(8,128)(2,1)}, u32[]{:S(2)}, u32[]{:S(2)}) collective-permute-start(bf16[384,512]{1,0:T(8,128)(2,1)} %collective-permute-done.14.refs_8_), channel_id=1, source_target_pairs={{0,8},{8,0},{16,24},{24,16},{1,9},{9,1},{17,25},{25,17},{2,10},{10... | collective-permute-start | bytes 1179656 | tf_op jit(solution)/shard_map/ppermute | solution.py:264
  52.8 4.7 %copy-start.1 = (bf16[384,512]{1,0:T(8,128)(2,1)S(1)}, bf16[384,512]{1,0:T(8,128)(2,1)}, u32[]{:S(2)}) copy-start(bf16[384,512]{1,0:T(8,128)(2,1)} %copy-done) | copy-start | bytes 1179652
  52.8 4.7 %copy-start.2 = (bf16[1,128,1024]{2,1,0:T(8,128)(2,1)S(1)}, bf16[1,128,1024]{2,1,0:T(8,128)(2,1)}, u32[]{:S(2)}) copy-start(bf16[1,128,1024]{2,1,0:T(8,128)(2,1)} %param.17) | copy-start | bytes 786436
  52.8 4.7 %copy-start.3 = (bf16[1,128,1024]{2,1,0:T(8,128)(2,1)S(1)}, bf16[1,128,1024]{2,1,0:T(8,128)(2,1)}, u32[]{:S(2)}) copy-start(bf16[1,128,1024]{2,1,0:T(8,128)(2,1)} %param.18) | copy-start | bytes 786436
  52.8 7.5 %collective-permute-start.18 = (bf16[192,512]{1,0:T(8,128)(2,1)}, bf16[192,512]{1,0:T(8,128)(2,1)S(1)}, u32[]{:S(2)}, u32[]{:S(2)}) collective-permute-start(bf16[192,512]{1,0:T(8,128)(2,1)} %collective-permute-done.15.refs_9_), channel_id=1, source_target_pairs={{0,8},{8,0},{16,24},{24,16},{1,9},{9,1},{17,25},{25,17},{2,10},{10... | collective-permute-start | bytes 589832 | tf_op jit(solution)/shard_map/ppermute | solution.py:264
  52.9 7.4 %collective-permute-start.19 = (bf16[192,512]{1,0:T(8,128)(2,1)}, bf16[192,512]{1,0:T(8,128)(2,1)S(1)}, u32[]{:S(2)}, u32[]{:S(2)}) collective-permute-start(bf16[192,512]{1,0:T(8,128)(2,1)} %collective-permute-done.16.refs_10_), channel_id=1, source_target_pairs={{0,8},{8,0},{16,24},{24,16},{1,9},{9,1},{17,25},{25,17},{2,10},{10... | collective-permute-start | bytes 589832 | tf_op jit(solution)/shard_map/ppermute | solution.py:264
  57.6 2.8 %copy-start.4 = (bf16[1,128,1024]{2,1,0:T(8,128)(2,1)S(1)}, bf16[1,128,1024]{2,1,0:T(8,128)(2,1)}, u32[]{:S(2)}) copy-start(bf16[1,128,1024]{2,1,0:T(8,128)(2,1)} %param.19) | copy-start | bytes 786436

commit v3 on v2

--- a/solution.py
+++ b/solution.py
@@ -74,18 +74,23 @@
     return wait
 
 
-def pack_kernel(gate, up, down, own, sems):
+def pack_kernel(gate, up, down, own, part, sems):
     core = lax.axis_index("row") % 2
     depth, half = gate.shape[0], own.shape[1]
     cols = pl.ds(pl.multiple_of(core * half, half), half)
     parts = [(w.at[:, cols], own.at[pl.ds(i * depth, depth)]) for i, w in enumerate((gate, up, down))]
     fetch(parts, sems)()
+    rows = part.shape[0]
+    begin = lax.axis_index("row") // 2 % 2 * rows
+    part[...] = own[pl.ds(pl.multiple_of(begin, rows), rows), :]
 
 
 def pack(gate, up, down):
     depth, width = gate.shape
     return call(
-        pack_kernel, pltpu.VMEM((3 * depth, width // 2), gate.dtype), [whole(pltpu.HBM)] * 3, 0, 1 << 20, 4,
+        pack_kernel,
+        tuple(pltpu.VMEM((rows, width // 2), gate.dtype) for rows in (3 * depth, 3 * depth // 2)),
+        [whole(pltpu.HBM)] * 3, 0, 1 << 20, 4,
         [pltpu.SemaphoreType.DMA((3,))],
     )(*far((gate, up, down)))
 
@@ -260,48 +265,40 @@
     return pairs
 
 
-def partner(block):
-    return lax.ppermute(block, "row", [(i, i ^ 1) for i in range(lax.axis_size("row"))])
-
-
-def rows_half(block, which):
-    cut = block.shape[0] // 2
-
-    def kernel(source, out):
-        out[...] = source[which * cut : (which + 1) * cut, :]
-
-    return call(
-        kernel, pltpu.VMEM((cut, block.shape[1]), block.dtype), [whole()], 0, 1 << 16, 2
-    )(*near([block]))
-
-
-def travel(own):
+def partner(block, distance=1):
+    return lax.ppermute(
+        block, "row", [(i, i ^ distance) for i in range(lax.axis_size("row"))]
+    )
+
+
+def travel(own, part):
     ends = (0, 3)
     side = col_route(0, lambda p: p ^ 1)
     outward = col_route(0, lambda p: None if p in ends else p ^ 1)
-    over_ends = col_route(1, lambda p: p if p in ends else None)
     over_middle = col_route(1, lambda p: None if p in ends else p)
-    turn = over_ends + col_route(0, lambda p: None if p in ends else 3 - p)
+    turn = col_route(1, lambda p: p if p in ends else None)
+    turn += col_route(0, lambda p: None if p in ends else 3 - p)
+    corner = col_route(1, lambda p: 3 - p if p in ends else p)
 
     def send(block, route):
         return lax.ppermute(block, "col", route)
 
     b = send(own, side)
     m = send(own, turn)
-    a = send(own, over_middle)
+    k = send(part, corner)
     c = send(m, side)
     d = send(b, turn)
     e = send(m, over_middle)
+    kx = partner(k, 2)
     f = send(d, outward)
     g = send(c, turn)
-    t = send(rows_half(g, 0), outward)
-    u = send(rows_half(f, 1), over_ends)
-    mine = [b, m, c, d, g, a, f, e, t, u]
-    return mine, [partner(block) for block in mine]
+    mine = dict(b=b, m=m, c=c, d=d, k=k, kx=kx, g=g, f=f, e=e)
+    return [*mine.values()], [partner(block) for block in mine.values()]
 
 
 def travelled(shares, mine, theirs, depth):
     core = lax.axis_index("row") % 2
+    first_side = lax.axis_index("row") // 2 % 2 == 0
     col = lax.axis_index("col")
     lane, place = col % 2, col // 2
     near = jnp.where(place % 2 == 0, place + 1, place - 1)
@@ -314,9 +311,9 @@
         either(at(3 - place, False), at(place, True)),
         either(at(near, True), at(3 - near, False)),
         either(at(3 - near, False), at(near, True)),
+        either(at(place, True), at(3 - place, True)),
         at(3 - near, True),
-        either(at(place, True), at(3 - place, False)),
-        at(3 - place, True),
+        either(at(3 - place, True), at(3 - place, False)),
     ]
     half = mine[0].shape[1]
 
@@ -328,18 +325,21 @@
         for i in span:
             if i == 0:
                 block = shares[weight][:, pl.ds(pl.multiple_of(offset, size), size)]
-            elif i < 6:
+            elif i < 5:
                 block = pieces[i - 1][rows, cols]
+            elif i == 5:
+                cut, parts = pieces[4].shape[0], []
+                for begin, flip in ((0, False), (cut, True)):
+                    low, high = max(rows.start, begin) - begin, min(rows.stop, begin + cut) - begin
+                    if low < high:
+                        here, there = (piece[low:high, cols] for piece in pieces[4:6])
+                        here_first = jnp.logical_not(first_side) if flip else first_side
+                        parts.append(jnp.where(here_first, here, there))
+                block = jnp.concatenate(parts, axis=0)
             elif i == 6:
-                block = jnp.where(middle, pieces[5][rows, cols], pieces[6][rows, cols])
+                block = pieces[6][rows, cols]
             else:
-                ends = [pieces[8], pieces[9]]
-                cut, parts = ends[0].shape[0], []
-                for at_row, piece in zip((0, cut), ends):
-                    low, high = max(rows.start, at_row) - at_row, min(rows.stop, at_row + cut) - at_row
-                    if low < high:
-                        parts.append(piece[low:high, cols])
-                block = jnp.where(middle, pieces[7][rows, cols], jnp.concatenate(parts, axis=0))
+                block = jnp.where(middle, pieces[8][rows, cols], pieces[7][rows, cols])
             blocks.append(block)
         return jnp.concatenate(blocks, axis=0)
 
@@ -358,27 +358,27 @@
 
 def open_kernel(inner, *refs):
     pieces, (ordered, gate_sums, up_sums) = refs[:-3], refs[-3:]
-    shares, mine, theirs = pieces[:2], pieces[2:9], pieces[9:]
+    shares, mine, theirs = pieces[:2], pieces[2:6], pieces[6:]
     depth = shares[0].shape[0]
     spots, read, _, in_order = travelled(shares, mine, theirs, depth)
     in_order(inner, ordered)
-    x = ordered[:, : 7 * depth]
+    x = ordered[:, : 5 * depth]
     for i, (part, start) in enumerate(spots):
         cols = slice(i * lane_chunk, (i + 1) * lane_chunk)
-        gate_sums[:, cols] = dot(x, read(0, part, start, lane_chunk, range(7)))
-        up_sums[:, cols] = dot(x, read(1, part, start, lane_chunk, range(7)))
+        gate_sums[:, cols] = dot(x, read(0, part, start, lane_chunk, range(5)))
+        up_sums[:, cols] = dot(x, read(1, part, start, lane_chunk, range(5)))
 
 
 def close_kernel(hidden, given, gate_sums, up_sums, *refs):
     pieces, (out, ordered, active) = refs[:-3], refs[-3:]
-    shares, mine, theirs = pieces[:1], pieces[1:11], pieces[11:]
+    shares, mine, theirs = pieces[:1], pieces[1:10], pieces[10:]
     depth = shares[0].shape[0]
     spots, read, own_cols, in_order = travelled([None, None, *shares], mine, theirs, depth)
-    x = given[:, 7 * depth :]
+    x = given[:, 5 * depth :]
     for i, (part, start) in enumerate(spots):
         cols = slice(i * lane_chunk, (i + 1) * lane_chunk)
-        gate_sum = gate_sums[:, cols] + dot(x, read(0, part, start, lane_chunk, (7,)))
-        up_sum = up_sums[:, cols] + dot(x, read(1, part, start, lane_chunk, (7,)))
+        gate_sum = gate_sums[:, cols] + dot(x, read(0, part, start, lane_chunk, (5, 6, 7)))
+        up_sum = up_sums[:, cols] + dot(x, read(1, part, start, lane_chunk, (5, 6, 7)))
         active[:, own_cols(part, start, lane_chunk)] = (
             gate_sum / (1.0 + jnp.exp(-gate_sum)) * up_sum
         ).astype(jnp.bfloat16)
@@ -394,7 +394,7 @@
 def hop_feed(inner, hidden, shares, mine, theirs):
     (count, width), inside = inner.shape, shares[0].shape[1]
     sums = shape(count, inside, jnp.float32)
-    early = [*shares[:2], *mine[:7], *theirs[:7]]
+    early = [*shares[:2], *mine[:4], *theirs[:4]]
     ordered, gate_sums, up_sums = call(
         open_kernel, (shape(count, width), sums, sums), [whole()] * (1 + len(early)),
         4 * count * width * inside, 4 << 20, 8,
@@ -432,7 +432,7 @@
     shares = [w[0] for w in weights]
     by_hops = travels()
     if by_hops:
-        mine, theirs = travel(pack(*shares))
+        mine, theirs = travel(*pack(*shares))
     sent, ids, gains = greet(item_ids[None], norm_gains[0], catalogue)
     got = lax.all_to_all(sent, both, 0, 0)
     looked_up = shelve(got, ids, gains)
@@ -449,7 +449,7 @@
 
 
 def travels():
-    return lax.axis_size("col") == 8 and lax.axis_size("row") % 2 == 0
+    return lax.axis_size("col") == 8 and lax.axis_size("row") == 4
 
 
 def solution(mesh):

time: 64.6 us -> 61.9 us (0.958)
  the two profiles are of different devices: /device:TPU:19 before, /device:TPU:7 now
where the time goes in v3:
time: 61.9 us; the launch traced here: 61.6 us
  starting transfers between devices  22.8 us (37%)
  waiting for transfers between devices  20.2 us (33%)
  Pallas kernels  18.3 us (30%)
    ppermute x8, waiting for transfers between devices, send(): return lax.ppermute(block, 'col', route)  10.4 us
    ppermute x8, starting transfers between devices, send(): return lax.ppermute(block, 'col', route)  9.22 us
    all_to_all x1, starting transfers between devices, body(): got = lax.all_to_all(sent, both, 0, 0)  9.02 us
    pallas_call x2, Pallas kernels, mix(): call(functools.partial(mix_kernel, begin_col), out, [whole(pltpu.SMEM)] +...  8 us
    all_to_all x1, waiting for transfers between devices, body(): got = lax.all_to_all(sent, both, 0, 0)  5.21 us
    ppermute x10, starting transfers between devices, partner(): lax.ppermute(block, 'row', [(i, i ^ distance) for i in range(lax.axis_siz...  4.62 us
    ppermute x10, waiting for transfers between devices, partner(): lax.ppermute(block, 'row', [(i, i ^ distance) for i in range(lax.axis_siz...  4.58 us
    pallas_call x1, Pallas kernels, hop_feed(): call(close_kernel, shape(count, width), [whole()] * len(late), 2 * count...  3.97 us
  transfers between devices with their start and end apart: 19, of which 6 were waited for; matrix products, arithmetic and copies ran while one was open for 0% of the time, Pallas kernels for 22%

profile of v3, /device:TPU:7, one launch (start us, length us, event | category | flops | bytes accessed | tf_op | source)
XLA Modules:
  0.0 61.6 jit_solution(5292454371489951298)
XLA Ops:
  0.0 1.1 %shard_map.114 = (bf16[384,512]{1,0:T(8,128)(2,1)S(1)}, bf16[192,512]{1,0:T(8,128)(2,1)S(1)}) custom-call(bf16[128,1024]{1,0:T(8,128)(2,1)} %bitcast.6, bf16[128,1024]{1,0:T(8,128)(2,1)} %bitcast.8, bf16[128,1024]{1,0:T(8,128)(2,1)} %bitcast.10), custom_call_target="tpu_custom_call" | custom-call | bytes 1048576 | tf_op jit(solution)/shard_map/pallas_call | solution.py:90
  1.1 0.3 collective-permute-start.1
  1.4 2.4 %collective-permute-start = (bf16[384,512]{1,0:T(8,128)(2,1)S(1)}, bf16[384,512]{1,0:T(8,128)(2,1)S(1)}, u32[]{:S(2)}, u32[]{:S(2)}) collective-permute-start(bf16[384,512]{1,0:T(8,128)(2,1)S(1)} %get-tuple-element.32), channel_id=1, source_target_pairs={{0,2},{1,3},{2,0},{3,1},{4,6},{5,7},{6,4},{7,5},{8,10},{9,11},{10,... | collective-permute-start | bytes 1179656 | tf_op jit(solution)/shard_map/ppermute | solution.py:284
  3.8 1.9 %collective-permute-start.8 = (bf16[192,512]{1,0:T(8,128)(2,1)S(1)}, bf16[192,512]{1,0:T(8,128)(2,1)S(1)}, u32[]{:S(2)}, u32[]{:S(2)}) collective-permute-start(bf16[192,512]{1,0:T(8,128)(2,1)S(1)} %get-tuple-element.36), channel_id=1, source_target_pairs={{0,7},{1,6},{2,3},{3,2},{4,5},{5,4},{6,1},{7,0},{8,15},{9,14},{10,... | collective-permute-start | bytes 589832 | tf_op jit(solution)/shard_map/ppermute | solution.py:284
  5.7 5.5 %collective-permute-done.1.refs_3_.refs_2_ = bf16[384,512]{1,0:T(8,128)(2,1)S(1)} collective-permute-done((bf16[384,512]{1,0:T(8,128)(2,1)S(1)}, bf16[384,512]{1,0:T(8,128)(2,1)S(1)}, u32[]{:S(2)}, u32[]{:S(2)}) %collective-permute-start.1) | collective-permute-done | bytes 393248 | tf_op jit(solution)/shard_map/ppermute | solution.py:284
  11.2 1.3 %collective-permute-start.2 = (bf16[384,512]{1,0:T(8,128)(2,1)S(1)}, bf16[384,512]{1,0:T(8,128)(2,1)S(1)}, u32[]{:S(2)}, u32[]{:S(2)}) collective-permute-start(bf16[384,512]{1,0:T(8,128)(2,1)S(1)} %collective-permute-done.1.refs_3_.refs_2_), channel_id=1, source_target_pairs={{0,2},{1,3},{2,0},{3,1},{4,6},{5,7},{6,4},{7,5},{8,10},{9,11},{10,... | collective-permute-start | bytes 1179656 | tf_op jit(solution)/shard_map/ppermute | solution.py:284
  12.5 0.0 collective-permute-done.refs_2_.refs_1_
  12.5 0.2 collective-permute-start.3
  12.7 2.3 %collective-permute-start.5 = (bf16[384,512]{1,0:T(8,128)(2,1)S(1)}, bf16[384,512]{1,0:T(8,128)(2,1)S(1)}, u32[]{:S(2)}, u32[]{:S(2)}) collective-permute-start(bf16[384,512]{1,0:T(8,128)(2,1)S(1)} %collective-permute-done.1.refs_3_.refs_2_), channel_id=1, source_target_pairs={{0,8},{8,0},{16,24},{24,16},{1,9},{9,1},{17,25},{25,17},{2,10},{10... | collective-permute-start | bytes 1179656 | tf_op jit(solution)/shard_map/ppermute | solution.py:269
  15.0 0.0 collective-permute-start.4
  15.0 3.5 %collective-permute-done.8.refs_5_ = bf16[192,512]{1,0:T(8,128)(2,1)S(1)} collective-permute-done((bf16[192,512]{1,0:T(8,128)(2,1)S(1)}, bf16[192,512]{1,0:T(8,128)(2,1)S(1)}, u32[]{:S(2)}, u32[]{:S(2)}) %collective-permute-start.8) | collective-permute-done | bytes 196640 | tf_op jit(solution)/shard_map/ppermute | solution.py:284
  18.5 0.3 collective-permute-start.9
  18.7 4.6 %collective-permute-done.9.refs_6_ = bf16[192,512]{1,0:T(8,128)(2,1)S(1)} collective-permute-done((bf16[192,512]{1,0:T(8,128)(2,1)S(1)}, bf16[192,512]{1,0:T(8,128)(2,1)S(1)}, u32[]{:S(2)}, u32[]{:S(2)}) %collective-permute-start.9) | collective-permute-done | bytes 196640 | tf_op jit(solution)/shard_map/ppermute | solution.py:269
  23.3 1.4 %collective-permute-start.12 = (bf16[384,512]{1,0:T(8,128)(2,1)S(1)}, bf16[384,512]{1,0:T(8,128)(2,1)}, u32[]{:S(2)}, u32[]{:S(2)}) collective-permute-start(bf16[384,512]{1,0:T(8,128)(2,1)S(1)} %collective-permute-done.1.refs_3_.refs_2_), channel_id=1, source_target_pairs={{2,3},{3,2},{4,5},{5,4},{10,11},{11,10},{12,13},{13,12},{18,19},{1... | collective-permute-start | bytes 1179656 | tf_op jit(solution)/shard_map/ppermute | solution.py:284
  24.7 0.4 collective-permute-done.2.refs_4_.refs_3_
  25.1 0.4 collective-permute-start.10
  25.5 1.0 %collective-permute-done.3.refs_5_.refs_4_ = bf16[384,512]{1,0:T(8,128)(2,1)S(1)} collective-permute-done((bf16[384,512]{1,0:T(8,128)(2,1)S(1)}, bf16[384,512]{1,0:T(8,128)(2,1)S(1)}, u32[]{:S(2)}, u32[]{:S(2)}) %collective-permute-start.3) | collective-permute-done | bytes 393248 | tf_op jit(solution)/shard_map/ppermute | solution.py:284
  26.6 1.3 %collective-permute-start.11 = (bf16[384,512]{1,0:T(8,128)(2,1)S(1)}, bf16[384,512]{1,0:T(8,128)(2,1)}, u32[]{:S(2)}, u32[]{:S(2)}) collective-permute-start(bf16[384,512]{1,0:T(8,128)(2,1)S(1)} %collective-permute-done.3.refs_5_.refs_4_), channel_id=1, source_target_pairs={{2,0},{3,1},{4,6},{5,7},{10,8},{11,9},{12,14},{13,15},{18,16},{19,... | collective-permute-start | bytes 1179656 | tf_op jit(solution)/shard_map/ppermute | solution.py:284
  27.9 1.7 %shard_map.109 = (bf16[32,2,1280]{2,1,0:T(2,128)(2,1)}, s32[1,256]{1,0:T(1,128)S(1)}, f32[2,1024]{1,0:T(2,128)S(1)}) custom-call(s32[1,256]{1,0:T(1,128)} %bitcast.14, f32[2,1024]{1,0:T(2,128)} %bitcast.13, bf16[2,1024]{1,0:T(2,128)(2,1)} %rows_far.1), custom_call_target="tpu_custom_call" | custom-call | bytes 262144 | tf_op jit(solution)/shard_map/pallas_call | solution.py:121
  29.5 9.0 %all-to-all-start = ((bf16[32,2,1280]{2,1,0:T(2,128)(2,1)}), bf16[32,2,1280]{2,1,0:T(2,128)(2,1)S(1)}, u32[]{:S(2)}, u32[]{:S(2)}) async-start(bf16[32,2,1280]{2,1,0:T(2,128)(2,1)} %get-tuple-element.21), calls=%async_computation | async-start | bytes 327680 | tf_op jit(solution)/shard_map/all_to_all | solution.py:437
  38.6 0.0 collective-permute-done.5.refs_7_.refs_11_
  38.6 0.5 collective-permute-start.6
  39.0 0.0 collective-permute-done.4.refs_6_.refs_10_
  39.0 0.1 collective-permute-start.7
  39.2 0.0 collective-permute-done.12.refs_9_
  39.2 0.4 collective-permute-start.17
  39.6 0.0 collective-permute-done.10.refs_7_
  39.6 0.1 collective-permute-start.15
  39.7 0.0 collective-permute-done.11.refs_8_
  39.7 0.4 collective-permute-start.16
  40.1 5.2 %all-to-all-done.got = bf16[32,2,1280]{2,1,0:T(2,128)(2,1)S(1)} async-done(((bf16[32,2,1280]{2,1,0:T(2,128)(2,1)}), bf16[32,2,1280]{2,1,0:T(2,128)(2,1)S(1)}, u32[]{:S(2)}, u32[]{:S(2)}) %all-to-all-start) | async-done | bytes 163872 | tf_op jit(solution)/shard_map/all_to_all | solution.py:437
  45.3 0.3 shard_map.110
  45.6 2.1 %shard_map.111 = (f32[512,1024]{1,0:T(8,128)S(1)}, bf16[512,1024]{1,0:T(8,128)(2,1)S(1)}, bf16[256,1536]{1,0:T(8,128)(2,1)S(1)}) custom-call(bf16[512,64]{1,0:T(8,128)(2,1)S(1)} %get-tuple-element.26.after.chosen, bf16[256,1024]{1,0:T(8,128)(2,1)} %bitcast.12, s32[1,1024]{1,0:T(1,128)} %lengths_far.1, bf16[512,1024]{1,0:T(8,128)(2,1)} %constant.4.clone.refs_0_, ...), custom_call_target="tpu_custom_call" | custom-call | flops 536870912 | bytes 5242880 | tf_op jit(solution)/shard_map/pallas_call | solution.py:147
  47.8 0.0 copy-start.4
  47.8 3.9 %shard_map.112.refs_0_ = f32[256,512]{1,0:T(8,128)S(1)} custom-call(s32[8]{0:T(128)S(1)} %copy-done.5, bf16[64,1024]{1,0:T(8,128)(2,1)S(1)} %get-tuple-element.24.table, bf16[64,1024]{1,0:T(8,128)(2,1)S(1)} %get-tuple-element.25.normed, bf16[512,64]{1,0:T(8,128)(2,1)S(1)} %get-tuple-element.26.after.chosen, f32[2,1024]{1,0:T(2,128)S(1)} %get-tuple-element.23.gains, ...), custom_call_target="tpu_custom_call" | custom-call | flops 1073741824 | bytes 4194304 | tf_op jit(solution)/shard_map/pallas_call | solution.py:249
  51.7 0.0 copy-start
  51.7 0.0 copy-start.1
  51.8 0.0 collective-permute-done.6.refs_8_.refs_12_
  51.8 0.1 collective-permute-start.13
  51.8 0.0 collective-permute-done.7.refs_9_.refs_13_
  51.9 0.5 collective-permute-start.14
  52.3 4.1 %shard_map.113 = (f32[256,1024]{1,0:T(8,128)S(1)}, bf16[256,1024]{1,0:T(8,128)(2,1)S(1)}) custom-call(s32[8]{0:T(128)S(1)} %copy-done.5, bf16[64,1024]{1,0:T(8,128)(2,1)S(1)} %get-tuple-element.24.table, bf16[64,1024]{1,0:T(8,128)(2,1)S(1)} %get-tuple-element.25.normed, bf16[512,64]{1,0:T(8,128)(2,1)S(1)} %get-tuple-element.26.after.chosen, ...), custom_call_target="tpu_custom_call" | custom-call | flops 1073741824 | bytes 4194304 | tf_op jit(solution)/shard_map/pallas_call | solution.py:249
  56.5 0.0 copy-start.2
  56.5 1.1 %shard_map.115 = (bf16[256,1024]{1,0:T(8,128)(2,1)S(1)}, f32[256,1024]{1,0:T(8,128)S(1)}, f32[256,1024]{1,0:T(8,128)S(1)}) custom-call(bf16[256,1024]{1,0:T(8,128)(2,1)S(1)} %get-tuple-element.31.inner, bf16[128,1024]{1,0:T(8,128)(2,1)S(1)} %bitcast.7, bf16[128,1024]{1,0:T(8,128)(2,1)S(1)} %bitcast.9, ...), custom_call_target="tpu_custom_call" | custom-call | flops 1073741824 | bytes 4194304 | tf_op jit(solution)/shard_map/pallas_call | solution.py:398
  57.6 0.0 collective-permute-done.13.refs_14_
  57.6 0.0 collective-permute-done.17.refs_18_
  57.6 0.0 collective-permute-done.15.refs_16_
  57.7 4.0 %shard_map.116 = bf16[256,1024]{1,0:T(8,128)(2,1)} custom-call(f32[256,1024]{1,0:T(8,128)S(1)} %get-tuple-element.30.hidden, bf16[256,1024]{1,0:T(8,128)(2,1)S(1)} %get-tuple-element.33.given, f32[256,1024]{1,0:T(8,128)S(1)} %get-tuple-element.34.gate_sums, f32[256,1024]{1,0:T(8,128)S(1)} %get-tuple-element.35.up_sums, bf16[128,1024]{1,0:T(8,128)(2,1)S(1)} %bitcast.11, ...), custom_call_target="tpu_custom_call" | custom-call | flops 536870912 | bytes 4194304 | tf_op jit(solution)/shard_map/pallas_call | solution.py:404
  (10 shorter events, 0.0 us)
Async XLA Ops:
  0.0 47.8 %copy-start.5 = (s32[8]{0:T(128)S(1)}, s32[8]{0:T(128)}, u32[]{:S(2)}) copy-start(s32[8]{0:T(128)} %lengths.3) | copy-start | bytes 100
  1.1 10.1 %collective-permute-start.1 = (bf16[384,512]{1,0:T(8,128)(2,1)S(1)}, bf16[384,512]{1,0:T(8,128)(2,1)S(1)}, u32[]{:S(2)}, u32[]{:S(2)}) collective-permute-start(bf16[384,512]{1,0:T(8,128)(2,1)S(1)} %get-tuple-element.32), channel_id=1, source_target_pairs={{0,1},{1,0},{6,7},{7,6},{2,4},{3,5},{4,2},{5,3},{8,9},{9,8},{14,15... | collective-permute-start | bytes 1179656 | tf_op jit(solution)/shard_map/ppermute | solution.py:284
  1.4 11.1 %collective-permute-start = (bf16[384,512]{1,0:T(8,128)(2,1)S(1)}, bf16[384,512]{1,0:T(8,128)(2,1)S(1)}, u32[]{:S(2)}, u32[]{:S(2)}) collective-permute-start(bf16[384,512]{1,0:T(8,128)(2,1)S(1)} %get-tuple-element.32), channel_id=1, source_target_pairs={{0,2},{1,3},{2,0},{3,1},{4,6},{5,7},{6,4},{7,5},{8,10},{9,11},{10,... | collective-permute-start | bytes 1179656 | tf_op jit(solution)/shard_map/ppermute | solution.py:284
  3.8 14.7 %collective-permute-start.8 = (bf16[192,512]{1,0:T(8,128)(2,1)S(1)}, bf16[192,512]{1,0:T(8,128)(2,1)S(1)}, u32[]{:S(2)}, u32[]{:S(2)}) collective-permute-start(bf16[192,512]{1,0:T(8,128)(2,1)S(1)} %get-tuple-element.36), channel_id=1, source_target_pairs={{0,7},{1,6},{2,3},{3,2},{4,5},{5,4},{6,1},{7,0},{8,15},{9,14},{10,... | collective-permute-start | bytes 589832 | tf_op jit(solution)/shard_map/ppermute | solution.py:284
  11.2 14.0 %collective-permute-start.2 = (bf16[384,512]{1,0:T(8,128)(2,1)S(1)}, bf16[384,512]{1,0:T(8,128)(2,1)S(1)}, u32[]{:S(2)}, u32[]{:S(2)}) collective-permute-start(bf16[384,512]{1,0:T(8,128)(2,1)S(1)} %collective-permute-done.1.refs_3_.refs_2_), channel_id=1, source_target_pairs={{0,2},{1,3},{2,0},{3,1},{4,6},{5,7},{6,4},{7,5},{8,10},{9,11},{10,... | collective-permute-start | bytes 1179656 | tf_op jit(solution)/shard_map/ppermute | solution.py:284
  12.5 14.1 %collective-permute-start.3 = (bf16[384,512]{1,0:T(8,128)(2,1)S(1)}, bf16[384,512]{1,0:T(8,128)(2,1)S(1)}, u32[]{:S(2)}, u32[]{:S(2)}) collective-permute-start(bf16[384,512]{1,0:T(8,128)(2,1)S(1)} %collective-permute-done.refs_2_.refs_1_), channel_id=1, source_target_pairs={{0,1},{1,0},{6,7},{7,6},{2,4},{3,5},{4,2},{5,3},{8,9},{9,8},{14,15... | collective-permute-start | bytes 1179656 | tf_op jit(solution)/shard_map/ppermute | solution.py:284
  12.7 25.9 %collective-permute-start.5 = (bf16[384,512]{1,0:T(8,128)(2,1)S(1)}, bf16[384,512]{1,0:T(8,128)(2,1)S(1)}, u32[]{:S(2)}, u32[]{:S(2)}) collective-permute-start(bf16[384,512]{1,0:T(8,128)(2,1)S(1)} %collective-permute-done.1.refs_3_.refs_2_), channel_id=1, source_target_pairs={{0,8},{8,0},{16,24},{24,16},{1,9},{9,1},{17,25},{25,17},{2,10},{10... | collective-permute-start | bytes 1179656 | tf_op jit(solution)/shard_map/ppermute | solution.py:269
  15.0 24.0 %collective-permute-start.4 = (bf16[384,512]{1,0:T(8,128)(2,1)S(1)}, bf16[384,512]{1,0:T(8,128)(2,1)S(1)}, u32[]{:S(2)}, u32[]{:S(2)}) collective-permute-start(bf16[384,512]{1,0:T(8,128)(2,1)S(1)} %collective-permute-done.refs_2_.refs_1_), channel_id=1, source_target_pairs={{0,8},{8,0},{16,24},{24,16},{1,9},{9,1},{17,25},{25,17},{2,10},{10... | collective-permute-start | bytes 1179656 | tf_op jit(solution)/shard_map/ppermute | solution.py:269
  18.5 4.8 %collective-permute-start.9 = (bf16[192,512]{1,0:T(8,128)(2,1)S(1)}, bf16[192,512]{1,0:T(8,128)(2,1)S(1)}, u32[]{:S(2)}, u32[]{:S(2)}) collective-permute-start(bf16[192,512]{1,0:T(8,128)(2,1)S(1)} %collective-permute-done.8.refs_5_), channel_id=1, source_target_pairs={{0,16},{8,24},{16,0},{24,8},{1,17},{9,25},{17,1},{25,9},{2,18},{10... | collective-permute-start | bytes 589832 | tf_op jit(solution)/shard_map/ppermute | solution.py:269
  23.3 15.3 %copy-start.3 = (bf16[192,512]{1,0:T(8,128)(2,1)}, bf16[192,512]{1,0:T(8,128)(2,1)S(1)}, u32[]{:S(2)}) copy-start(bf16[192,512]{1,0:T(8,128)(2,1)S(1)} %collective-permute-done.9.refs_6_) | copy-start | bytes 589828
  23.3 15.9 %collective-permute-start.12 = (bf16[384,512]{1,0:T(8,128)(2,1)S(1)}, bf16[384,512]{1,0:T(8,128)(2,1)}, u32[]{:S(2)}, u32[]{:S(2)}) collective-permute-start(bf16[384,512]{1,0:T(8,128)(2,1)S(1)} %collective-permute-done.1.refs_3_.refs_2_), channel_id=1, source_target_pairs={{2,3},{3,2},{4,5},{5,4},{10,11},{11,10},{12,13},{13,12},{18,19},{1... | collective-permute-start | bytes 1179656 | tf_op jit(solution)/shard_map/ppermute | solution.py:284
  25.1 14.4 %collective-permute-start.10 = (bf16[384,512]{1,0:T(8,128)(2,1)S(1)}, bf16[384,512]{1,0:T(8,128)(2,1)}, u32[]{:S(2)}, u32[]{:S(2)}) collective-permute-start(bf16[384,512]{1,0:T(8,128)(2,1)S(1)} %collective-permute-done.2.refs_4_.refs_3_), channel_id=1, source_target_pairs={{0,1},{1,0},{6,7},{7,6},{2,4},{3,5},{4,2},{5,3},{8,9},{9,8},{14,15... | collective-permute-start | bytes 1179656 | tf_op jit(solution)/shard_map/ppermute | solution.py:284
  26.6 13.1 %collective-permute-start.11 = (bf16[384,512]{1,0:T(8,128)(2,1)S(1)}, bf16[384,512]{1,0:T(8,128)(2,1)}, u32[]{:S(2)}, u32[]{:S(2)}) collective-permute-start(bf16[384,512]{1,0:T(8,128)(2,1)S(1)} %collective-permute-done.3.refs_5_.refs_4_), channel_id=1, source_target_pairs={{2,0},{3,1},{4,6},{5,7},{10,8},{11,9},{12,14},{13,15},{18,16},{19,... | collective-permute-start | bytes 1179656 | tf_op jit(solution)/shard_map/ppermute | solution.py:284
  29.5 15.8 %all-to-all-start = ((bf16[32,2,1280]{2,1,0:T(2,128)(2,1)}), bf16[32,2,1280]{2,1,0:T(2,128)(2,1)S(1)}, u32[]{:S(2)}, u32[]{:S(2)}) async-start(bf16[32,2,1280]{2,1,0:T(2,128)(2,1)} %get-tuple-element.21), calls=%async_computation | async-start | bytes 327680 | tf_op jit(solution)/shard_map/all_to_all | solution.py:437
  38.6 13.2 %collective-permute-start.6 = (bf16[384,512]{1,0:T(8,128)(2,1)S(1)}, bf16[384,512]{1,0:T(8,128)(2,1)S(1)}, u32[]{:S(2)}, u32[]{:S(2)}) collective-permute-start(bf16[384,512]{1,0:T(8,128)(2,1)S(1)} %collective-permute-done.2.refs_4_.refs_3_), channel_id=1, source_target_pairs={{0,8},{8,0},{16,24},{24,16},{1,9},{9,1},{17,25},{25,17},{2,10},{10... | collective-permute-start | bytes 1179656 | tf_op jit(solution)/shard_map/ppermute | solution.py:269
  39.0 12.8 %collective-permute-start.7 = (bf16[384,512]{1,0:T(8,128)(2,1)S(1)}, bf16[384,512]{1,0:T(8,128)(2,1)S(1)}, u32[]{:S(2)}, u32[]{:S(2)}) collective-permute-start(bf16[384,512]{1,0:T(8,128)(2,1)S(1)} %collective-permute-done.3.refs_5_.refs_4_), channel_id=1, source_target_pairs={{0,8},{8,0},{16,24},{24,16},{1,9},{9,1},{17,25},{25,17},{2,10},{10... | collective-permute-start | bytes 1179656 | tf_op jit(solution)/shard_map/ppermute | solution.py:269
  39.2 18.4 %collective-permute-start.17 = (bf16[384,512]{1,0:T(8,128)(2,1)}, bf16[384,512]{1,0:T(8,128)(2,1)}, u32[]{:S(2)}, u32[]{:S(2)}) collective-permute-start(bf16[384,512]{1,0:T(8,128)(2,1)} %collective-permute-done.12.refs_9_), channel_id=1, source_target_pairs={{0,8},{8,0},{16,24},{24,16},{1,9},{9,1},{17,25},{25,17},{2,10},{10... | collective-permute-start | bytes 1179656 | tf_op jit(solution)/shard_map/ppermute | solution.py:269
  39.6 18.1 %collective-permute-start.15 = (bf16[384,512]{1,0:T(8,128)(2,1)}, bf16[384,512]{1,0:T(8,128)(2,1)}, u32[]{:S(2)}, u32[]{:S(2)}) collective-permute-start(bf16[384,512]{1,0:T(8,128)(2,1)} %collective-permute-done.10.refs_7_), channel_id=1, source_target_pairs={{0,8},{8,0},{16,24},{24,16},{1,9},{9,1},{17,25},{25,17},{2,10},{10... | collective-permute-start | bytes 1179656 | tf_op jit(solution)/shard_map/ppermute | solution.py:269
  39.7 18.0 %collective-permute-start.16 = (bf16[384,512]{1,0:T(8,128)(2,1)}, bf16[384,512]{1,0:T(8,128)(2,1)}, u32[]{:S(2)}, u32[]{:S(2)}) collective-permute-start(bf16[384,512]{1,0:T(8,128)(2,1)} %collective-permute-done.11.refs_8_), channel_id=1, source_target_pairs={{0,8},{8,0},{16,24},{24,16},{1,9},{9,1},{17,25},{25,17},{2,10},{10... | collective-permute-start | bytes 1179656 | tf_op jit(solution)/shard_map/ppermute | solution.py:269
  47.8 4.0 %copy-start.4 = (bf16[192,512]{1,0:T(8,128)(2,1)S(1)}, bf16[192,512]{1,0:T(8,128)(2,1)}, u32[]{:S(2)}) copy-start(bf16[192,512]{1,0:T(8,128)(2,1)} %copy-done.3) | copy-start | bytes 589828
  51.7 4.7 %copy-start = (bf16[1,128,1024]{2,1,0:T(8,128)(2,1)S(1)}, bf16[1,128,1024]{2,1,0:T(8,128)(2,1)}, u32[]{:S(2)}) copy-start(bf16[1,128,1024]{2,1,0:T(8,128)(2,1)} %param.17) | copy-start | bytes 786436
  51.7 4.7 %copy-start.1 = (bf16[1,128,1024]{2,1,0:T(8,128)(2,1)S(1)}, bf16[1,128,1024]{2,1,0:T(8,128)(2,1)}, u32[]{:S(2)}) copy-start(bf16[1,128,1024]{2,1,0:T(8,128)(2,1)} %param.18) | copy-start | bytes 786436
  51.8 5.8 %collective-permute-start.13 = (bf16[192,512]{1,0:T(8,128)(2,1)S(1)}, bf16[192,512]{1,0:T(8,128)(2,1)S(1)}, u32[]{:S(2)}, u32[]{:S(2)}) collective-permute-start(bf16[192,512]{1,0:T(8,128)(2,1)S(1)} %collective-permute-done.8.refs_5_), channel_id=1, source_target_pairs={{0,8},{8,0},{16,24},{24,16},{1,9},{9,1},{17,25},{25,17},{2,10},{10... | collective-permute-start | bytes 589832 | tf_op jit(solution)/shard_map/ppermute | solution.py:269
  51.9 5.7 %collective-permute-start.14 = (bf16[192,512]{1,0:T(8,128)(2,1)S(1)}, bf16[192,512]{1,0:T(8,128)(2,1)S(1)}, u32[]{:S(2)}, u32[]{:S(2)}) collective-permute-start(bf16[192,512]{1,0:T(8,128)(2,1)S(1)} %copy-done.4), channel_id=1, source_target_pairs={{0,8},{8,0},{16,24},{24,16},{1,9},{9,1},{17,25},{25,17},{2,10},{10... | collective-permute-start | bytes 589832 | tf_op jit(solution)/shard_map/ppermute | solution.py:269
  56.5 1.2 %copy-start.2 = (bf16[1,128,1024]{2,1,0:T(8,128)(2,1)S(1)}, bf16[1,128,1024]{2,1,0:T(8,128)(2,1)}, u32[]{:S(2)}) copy-start(bf16[1,128,1024]{2,1,0:T(8,128)(2,1)} %param.19) | copy-start | bytes 786436

commit v4 on v3

--- a/solution.py
+++ b/solution.py
@@ -1,5 +1,3 @@
-import functools
-
 import jax
 import jax.numpy as jnp
 import numpy as np
@@ -10,7 +8,7 @@
 
 epsilon = 1e-06
 lane_chunk = 256
-mix_chunk = 512
+mix_chunk = 1024
 both = ("row", "col")
 id_base = 256
 
@@ -191,69 +189,57 @@
     )(got, own, gains)
 
 
-def mix_kernel(begin_col, lengths, table, normed, chosen, gains, spectrum, forward, inverse, *refs):
-    last = len(refs) == 3
-    first_cols, hidden, inner = refs if last else (None, *refs, None)
-    window = chosen.shape[0]
+def mix_kernel(lengths, given, normed, chosen, gains, spectrum, forward, inverse, hidden, *inner):
+    window, width = chosen.shape[0], hidden.shape[1]
     count, half = window // 2, window // 2
-    cols_here = hidden.shape[1] - begin_col if last else hidden.shape[1]
     first = (lax.axis_index("row") * lax.axis_size("col") + lax.axis_index("col")) * count
-    base = begin_col if last else 0
-    if last:
-        hidden[:, :begin_col] = first_cols[...]
-    hidden[:, base : base + cols_here] = dot(
-        chosen[count:, :], table[:, begin_col : begin_col + cols_here]
-    )
-
-    at = lax.broadcasted_iota(jnp.int32, (window, 1), 0) + (first - count)
+    hidden[...] = given[...] if inner else dot(chosen[count:, :], given[...])
+
+    def add_user(begin, end, skip):
+        at = lax.broadcasted_iota(jnp.int32, (window - skip, 1), 0) + (first - count + skip)
+        inside = jnp.logical_and(at >= begin, at < end)
+        picked = jnp.where(inside, chosen[skip:, :].astype(jnp.float32), 0.0).astype(jnp.bfloat16)
+        for start in range(0, width, mix_chunk):
+            cols = pl.ds(start, mix_chunk)
+            x = dot(picked, normed[:, cols]).astype(jnp.bfloat16)
+            table_parts = [forward[:, part + skip : part + window] for part in (0, window)]
+            seen = dot(jnp.concatenate(table_parts, axis=1), jnp.concatenate([x, x], axis=0))
+            x_cos, x_sin = seen[:half], seen[half:]
+            w_cos, w_sin = spectrum[:half, cols], spectrum[half:, cols]
+            y = jnp.concatenate(
+                [x_cos * w_cos - x_sin * w_sin, x_cos * w_sin + x_sin * w_cos], axis=0
+            )
+            y_high = y.astype(jnp.bfloat16)
+            y_low = (y - y_high.astype(jnp.float32)).astype(jnp.bfloat16)
+            mixed = dot(inverse[...], jnp.concatenate([y_high, y_low, y_high], axis=0))
+            hidden[:, cols] += jnp.where(inside[count - skip :], mixed, 0.0)
 
     def one_user(user, begin):
         end = begin + lengths[user]
-
-        @pl.when(jnp.logical_and(begin < first + count, end > first))
-        def _():
-            inside = jnp.logical_and(at >= begin, at < end)
-            picked = jnp.where(inside, chosen[...].astype(jnp.float32), 0.0).astype(jnp.bfloat16)
-            for start in range(0, cols_here, mix_chunk):
-                cols = pl.ds(begin_col + start, mix_chunk)
-                x = dot(picked, normed[:, cols]).astype(jnp.bfloat16)
-                seen = dot(forward[...], jnp.concatenate([x, x], axis=0))
-                x_cos, x_sin = seen[:half], seen[half:]
-                w_cos, w_sin = spectrum[:half, cols], spectrum[half:, cols]
-                y = jnp.concatenate(
-                    [x_cos * w_cos - x_sin * w_sin, x_cos * w_sin + x_sin * w_cos], axis=0
-                )
-                y_high = y.astype(jnp.bfloat16)
-                y_low = (y - y_high.astype(jnp.float32)).astype(jnp.bfloat16)
-                mixed = dot(inverse[...], jnp.concatenate([y_high, y_low, y_high], axis=0))
-                cols = pl.ds(base + start, mix_chunk)
-                hidden[:, cols] += jnp.where(inside[count:], mixed, 0.0)
-
+        here = jnp.logical_and(begin < first + count, end > first)
+        if inner:
+            pl.when(jnp.logical_and(here, begin >= first))(lambda: add_user(begin, end, count))
+        else:
+            pl.when(jnp.logical_and(here, begin < first))(lambda: add_user(begin, end, 0))
         return end
 
     lax.fori_loop(0, lengths.shape[0], one_user, jnp.int32(0))
-    if last:
+    if inner:
         mixed = hidden[...]
         scale = lax.rsqrt(jnp.mean(mixed * mixed, axis=-1, keepdims=True) + epsilon)
-        inner[...] = (mixed * scale * gains[1:2, :]).astype(jnp.bfloat16)
-
-
-def mix(begin_col, cols_here, lengths, looked_up, gains, spectrum, tables, first_cols=None):
-    (items, width), window = looked_up[0].shape, looked_up[2].shape[0]
-    operands = [lengths, *near(looked_up), gains, spectrum, *near(tables)]
-    if first_cols is None:
-        out = shape(window // 2, cols_here, jnp.float32)
-    else:
-        operands.append(first_cols)
-        out = (shape(window // 2, width, jnp.float32), shape(window // 2, width))
-    return call(
-        functools.partial(mix_kernel, begin_col),
-        out,
-        [whole(pltpu.SMEM)] + [whole()] * (len(operands) - 1),
-        8 * cols_here * window * window,
-        4 << 20,
-        10,
-    )(*operands)
+        inner[0][...] = (mixed * scale * gains[1:2, :]).astype(jnp.bfloat16)
+
+
+def mix(lengths, given, normed, chosen, gains, spectrum, tables, norm):
+    (items, width), window = normed.shape, chosen.shape[0]
+    operands = near([given, normed, chosen, gains, spectrum, *tables])
+    out = [pltpu.VMEM((window // 2, width), jnp.float32)]
+    if norm:
+        out.append(pltpu.VMEM((window // 2, width), jnp.bfloat16))
+    return call(
+        mix_kernel, out, [whole(pltpu.SMEM)] + [whole()] * len(operands),
+        8 * width * window * window, 4 << 20, 14,
+    )(lengths, *operands)
 
 
 def col_route(lane, place):
@@ -427,7 +413,7 @@
 
 def body(item_ids, user_lengths, catalogue, tap_lengths, conv_taps, norm_gains,
          gate_weight, up_weight, down_weight):
-    count, width = item_ids.shape[0], catalogue.shape[1]
+    count = item_ids.shape[0]
     weights = (gate_weight, up_weight, down_weight)
     shares = [w[0] for w in weights]
     by_hops = travels()
@@ -438,9 +424,10 @@
     looked_up = shelve(got, ids, gains)
     tables = [*map(jnp.asarray, transform_tables(2 * count, count))]
     spectrum, *tables = taps_spectrum(conv_taps[0], tap_lengths, tables, looked_up[2])
-    common = (user_lengths, looked_up, gains, spectrum, tables)
-    first_cols = mix(0, width // 2, *common)
-    hidden, inner = mix(width // 2, width // 2, *common, first_cols)
+    table, *looked_up = looked_up
+    common = (*looked_up, gains, spectrum, tables)
+    (hidden,) = mix(user_lengths, table, *common, False)
+    hidden, inner = mix(user_lengths, hidden, *common, True)
     if by_hops:
         return hop_feed(inner, hidden, shares, mine, theirs)
     return plain_feed(

time: 61.9 us -> 63 us (1.018)
  the two profiles are of different devices: /device:TPU:7 before, /device:TPU:0 now
where the time goes in v4:
time: 63 us; the launch traced here: 62.7 us
  starting transfers between devices  26.7 us (42%)
  waiting for transfers between devices  22 us (35%)
  Pallas kernels  13.9 us (22%)
    ppermute x8, starting transfers between devices, send(): return lax.ppermute(block, 'col', route)  14.2 us
    ppermute x8, waiting for transfers between devices, send(): return lax.ppermute(block, 'col', route)  10.9 us
    all_to_all x1, waiting for transfers between devices, body(): got = lax.all_to_all(sent, both, 0, 0)  7.4 us
    ppermute x10, starting transfers between devices, partner(): lax.ppermute(block, 'row', [(i, i ^ distance) for i in range(lax.axis_siz...  6.49 us
    all_to_all x1, starting transfers between devices, body(): got = lax.all_to_all(sent, both, 0, 0)  5.99 us
    pallas_call x2, Pallas kernels, mix(): call(mix_kernel, out, [whole(pltpu.SMEM)] + [whole()] * len(operands), 8...  3.88 us
    ppermute x10, waiting for transfers between devices, partner(): lax.ppermute(block, 'row', [(i, i ^ distance) for i in range(lax.axis_siz...  3.69 us
    pallas_call x1, Pallas kernels, hop_feed(): call(close_kernel, shape(count, width), [whole()] * len(late), 2 * count...  3.63 us
  transfers between devices with their start and end apart: 19, of which 5 were waited for; matrix products, arithmetic and copies ran while one was open for 0% of the time, Pallas kernels for 15%

profile of v4, /device:TPU:0, one launch (start us, length us, event | category | flops | bytes accessed | tf_op | source)
XLA Modules:
  0.0 62.7 jit_solution(1487620701398498495)
XLA Ops:
  0.0 1.1 %shard_map.114 = (bf16[384,512]{1,0:T(8,128)(2,1)S(1)}, bf16[192,512]{1,0:T(8,128)(2,1)S(1)}) custom-call(bf16[128,1024]{1,0:T(8,128)(2,1)} %bitcast.6, bf16[128,1024]{1,0:T(8,128)(2,1)} %bitcast.8, bf16[128,1024]{1,0:T(8,128)(2,1)} %bitcast.10), custom_call_target="tpu_custom_call" | custom-call | bytes 1048576 | tf_op jit(solution)/shard_map/pallas_call | solution.py:88
  1.1 3.1 %collective-permute-start.1 = (bf16[384,512]{1,0:T(8,128)(2,1)S(1)}, bf16[384,512]{1,0:T(8,128)(2,1)S(1)}, u32[]{:S(2)}, u32[]{:S(2)}) collective-permute-start(bf16[384,512]{1,0:T(8,128)(2,1)S(1)} %get-tuple-element.32), channel_id=1, source_target_pairs={{0,1},{1,0},{6,7},{7,6},{2,4},{3,5},{4,2},{5,3},{8,9},{9,8},{14,15... | collective-permute-start | bytes 1179656 | tf_op jit(solution)/shard_map/ppermute | solution.py:270
  4.2 1.6 %collective-permute-start = (bf16[384,512]{1,0:T(8,128)(2,1)S(1)}, bf16[384,512]{1,0:T(8,128)(2,1)S(1)}, u32[]{:S(2)}, u32[]{:S(2)}) collective-permute-start(bf16[384,512]{1,0:T(8,128)(2,1)S(1)} %get-tuple-element.32), channel_id=1, source_target_pairs={{0,2},{1,3},{2,0},{3,1},{4,6},{5,7},{6,4},{7,5},{8,10},{9,11},{10,... | collective-permute-start | bytes 1179656 | tf_op jit(solution)/shard_map/ppermute | solution.py:270
  5.8 2.3 %collective-permute-start.8 = (bf16[192,512]{1,0:T(8,128)(2,1)S(1)}, bf16[192,512]{1,0:T(8,128)(2,1)S(1)}, u32[]{:S(2)}, u32[]{:S(2)}) collective-permute-start(bf16[192,512]{1,0:T(8,128)(2,1)S(1)} %get-tuple-element.36), channel_id=1, source_target_pairs={{0,7},{1,6},{2,3},{3,2},{4,5},{5,4},{6,1},{7,0},{8,15},{9,14},{10,... | collective-permute-start | bytes 589832 | tf_op jit(solution)/shard_map/ppermute | solution.py:270
  8.1 5.2 %collective-permute-done.1.refs_3_.refs_2_ = bf16[384,512]{1,0:T(8,128)(2,1)S(1)} collective-permute-done((bf16[384,512]{1,0:T(8,128)(2,1)S(1)}, bf16[384,512]{1,0:T(8,128)(2,1)S(1)}, u32[]{:S(2)}, u32[]{:S(2)}) %collective-permute-start.1) | collective-permute-done | bytes 393248 | tf_op jit(solution)/shard_map/ppermute | solution.py:270
  13.3 1.8 %collective-permute-start.2 = (bf16[384,512]{1,0:T(8,128)(2,1)S(1)}, bf16[384,512]{1,0:T(8,128)(2,1)S(1)}, u32[]{:S(2)}, u32[]{:S(2)}) collective-permute-start(bf16[384,512]{1,0:T(8,128)(2,1)S(1)} %collective-permute-done.1.refs_3_.refs_2_), channel_id=1, source_target_pairs={{0,2},{1,3},{2,0},{3,1},{4,6},{5,7},{6,4},{7,5},{8,10},{9,11},{10,... | collective-permute-start | bytes 1179656 | tf_op jit(solution)/shard_map/ppermute | solution.py:270
  15.1 0.2 collective-permute-done.refs_2_.refs_1_
  15.3 1.5 %collective-permute-start.3 = (bf16[384,512]{1,0:T(8,128)(2,1)S(1)}, bf16[384,512]{1,0:T(8,128)(2,1)S(1)}, u32[]{:S(2)}, u32[]{:S(2)}) collective-permute-start(bf16[384,512]{1,0:T(8,128)(2,1)S(1)} %collective-permute-done.refs_2_.refs_1_), channel_id=1, source_target_pairs={{0,1},{1,0},{6,7},{7,6},{2,4},{3,5},{4,2},{5,3},{8,9},{9,8},{14,15... | collective-permute-start | bytes 1179656 | tf_op jit(solution)/shard_map/ppermute | solution.py:270
  16.8 5.5 %collective-permute-done.8.refs_5_ = bf16[192,512]{1,0:T(8,128)(2,1)S(1)} collective-permute-done((bf16[192,512]{1,0:T(8,128)(2,1)S(1)}, bf16[192,512]{1,0:T(8,128)(2,1)S(1)}, u32[]{:S(2)}, u32[]{:S(2)}) %collective-permute-start.8) | collective-permute-done | bytes 196640 | tf_op jit(solution)/shard_map/ppermute | solution.py:270
  22.3 1.5 %collective-permute-start.9 = (bf16[192,512]{1,0:T(8,128)(2,1)S(1)}, bf16[192,512]{1,0:T(8,128)(2,1)S(1)}, u32[]{:S(2)}, u32[]{:S(2)}) collective-permute-start(bf16[192,512]{1,0:T(8,128)(2,1)S(1)} %collective-permute-done.8.refs_5_), channel_id=1, source_target_pairs={{0,16},{8,24},{16,0},{24,8},{1,17},{9,25},{17,1},{25,9},{2,18},{10... | collective-permute-start | bytes 589832 | tf_op jit(solution)/shard_map/ppermute | solution.py:255
  23.8 0.0 collective-permute-start.5
  23.8 0.5 collective-permute-start.4
  24.3 3.7 %collective-permute-done.9.refs_6_ = bf16[192,512]{1,0:T(8,128)(2,1)S(1)} collective-permute-done((bf16[192,512]{1,0:T(8,128)(2,1)S(1)}, bf16[192,512]{1,0:T(8,128)(2,1)S(1)}, u32[]{:S(2)}, u32[]{:S(2)}) %collective-permute-start.9) | collective-permute-done | bytes 196640 | tf_op jit(solution)/shard_map/ppermute | solution.py:255
  27.9 1.4 %collective-permute-start.12 = (bf16[384,512]{1,0:T(8,128)(2,1)S(1)}, bf16[384,512]{1,0:T(8,128)(2,1)}, u32[]{:S(2)}, u32[]{:S(2)}) collective-permute-start(bf16[384,512]{1,0:T(8,128)(2,1)S(1)} %collective-permute-done.1.refs_3_.refs_2_), channel_id=1, source_target_pairs={{2,3},{3,2},{4,5},{5,4},{10,11},{11,10},{12,13},{13,12},{18,19},{1... | collective-permute-start | bytes 1179656 | tf_op jit(solution)/shard_map/ppermute | solution.py:270
  29.4 0.0 collective-permute-done.2.refs_4_.refs_3_
  29.4 1.2 %collective-permute-start.10 = (bf16[384,512]{1,0:T(8,128)(2,1)S(1)}, bf16[384,512]{1,0:T(8,128)(2,1)}, u32[]{:S(2)}, u32[]{:S(2)}) collective-permute-start(bf16[384,512]{1,0:T(8,128)(2,1)S(1)} %collective-permute-done.2.refs_4_.refs_3_), channel_id=1, source_target_pairs={{0,1},{1,0},{6,7},{7,6},{2,4},{3,5},{4,2},{5,3},{8,9},{9,8},{14,15... | collective-permute-start | bytes 1179656 | tf_op jit(solution)/shard_map/ppermute | solution.py:270
  30.5 0.0 collective-permute-done.3.refs_5_.refs_4_
  30.5 1.3 %collective-permute-start.11 = (bf16[384,512]{1,0:T(8,128)(2,1)S(1)}, bf16[384,512]{1,0:T(8,128)(2,1)}, u32[]{:S(2)}, u32[]{:S(2)}) collective-permute-start(bf16[384,512]{1,0:T(8,128)(2,1)S(1)} %collective-permute-done.3.refs_5_.refs_4_), channel_id=1, source_target_pairs={{2,0},{3,1},{4,6},{5,7},{10,8},{11,9},{12,14},{13,15},{18,16},{19,... | collective-permute-start | bytes 1179656 | tf_op jit(solution)/shard_map/ppermute | solution.py:270
  31.8 1.7 %shard_map.109 = (bf16[32,2,1280]{2,1,0:T(2,128)(2,1)}, s32[1,256]{1,0:T(1,128)S(1)}, f32[2,1024]{1,0:T(2,128)S(1)}) custom-call(s32[1,256]{1,0:T(1,128)} %bitcast.14, f32[2,1024]{1,0:T(2,128)} %bitcast.13, bf16[2,1024]{1,0:T(2,128)(2,1)} %rows_far.1), custom_call_target="tpu_custom_call" | custom-call | bytes 262144 | tf_op jit(solution)/shard_map/pallas_call | solution.py:119
  33.5 6.0 %all-to-all-start = ((bf16[32,2,1280]{2,1,0:T(2,128)(2,1)}), bf16[32,2,1280]{2,1,0:T(2,128)(2,1)S(1)}, u32[]{:S(2)}, u32[]{:S(2)}) async-start(bf16[32,2,1280]{2,1,0:T(2,128)(2,1)} %get-tuple-element.21), calls=%async_computation | async-start | bytes 327680 | tf_op jit(solution)/shard_map/all_to_all | solution.py:423
  39.5 0.0 collective-permute-done.5.refs_7_.refs_11_
  39.5 0.3 collective-permute-start.6
  39.8 0.0 collective-permute-done.4.refs_6_.refs_10_
  39.8 0.3 collective-permute-start.7
  40.1 7.4 %all-to-all-done.got = bf16[32,2,1280]{2,1,0:T(2,128)(2,1)S(1)} async-done(((bf16[32,2,1280]{2,1,0:T(2,128)(2,1)}), bf16[32,2,1280]{2,1,0:T(2,128)(2,1)S(1)}, u32[]{:S(2)}, u32[]{:S(2)}) %all-to-all-start) | async-done | bytes 163872 | tf_op jit(solution)/shard_map/all_to_all | solution.py:423
  47.5 0.3 shard_map.110
  47.9 2.1 %shard_map.111 = (f32[512,1024]{1,0:T(8,128)S(1)}, bf16[512,1024]{1,0:T(8,128)(2,1)S(1)}, bf16[256,1536]{1,0:T(8,128)(2,1)S(1)}) custom-call(bf16[512,64]{1,0:T(8,128)(2,1)S(1)} %get-tuple-element.26.after.chosen, bf16[256,1024]{1,0:T(8,128)(2,1)} %bitcast.12, s32[1,1024]{1,0:T(1,128)} %lengths_far.1, bf16[512,1024]{1,0:T(8,128)(2,1)} %constant.4.clone.refs_0_, ...), custom_call_target="tpu_custom_call" | custom-call | flops 536870912 | bytes 5242880 | tf_op jit(solution)/shard_map/pallas_call | solution.py:145
  50.0 0.0 collective-permute-done.12.refs_9_
  50.0 0.2 collective-permute-start.17
  50.2 0.0 collective-permute-done.10.refs_7_
  50.2 0.4 collective-permute-start.15
  50.6 0.0 collective-permute-done.11.refs_8_
  50.6 0.1 collective-permute-start.16
  50.7 0.9 %shard_map.112.given = f32[256,1024]{1,0:T(8,128)S(1)} custom-call(s32[8]{0:T(128)S(1)} %copy-done.5, bf16[64,1024]{1,0:T(8,128)(2,1)S(1)} %get-tuple-element.24.given, bf16[64,1024]{1,0:T(8,128)(2,1)S(1)} %get-tuple-element.25.normed, bf16[512,64]{1,0:T(8,128)(2,1)S(1)} %get-tuple-element.26.after.chosen, f32[2,1024]{1,0:T(2,128)S(1)} %get-tuple-element.23.gains, ...), custom_call_target="tpu_custom_call" | custom-call | flops 2147483648 | bytes 4194304 | tf_op jit(solution)/shard_map/pallas_call | solution.py:239
  51.7 0.0 copy-start
  51.7 0.0 copy-start.1
  51.7 0.0 collective-permute-done.6.refs_8_.refs_12_
  51.7 3.1 %collective-permute-start.13 = (bf16[192,512]{1,0:T(8,128)(2,1)S(1)}, bf16[192,512]{1,0:T(8,128)(2,1)S(1)}, u32[]{:S(2)}, u32[]{:S(2)}) collective-permute-start(bf16[192,512]{1,0:T(8,128)(2,1)S(1)} %collective-permute-done.8.refs_5_), channel_id=1, source_target_pairs={{0,8},{8,0},{16,24},{24,16},{1,9},{9,1},{17,25},{25,17},{2,10},{10... | collective-permute-start | bytes 589832 | tf_op jit(solution)/shard_map/ppermute | solution.py:255
  54.8 0.0 collective-permute-done.7.refs_9_.refs_13_
  54.8 0.1 collective-permute-start.14
  54.9 3.0 %shard_map.113 = (f32[256,1024]{1,0:T(8,128)S(1)}, bf16[256,1024]{1,0:T(8,128)(2,1)S(1)}) custom-call(s32[8]{0:T(128)S(1)} %copy-done.5, f32[256,1024]{1,0:T(8,128)S(1)} %shard_map.112.given, bf16[64,1024]{1,0:T(8,128)(2,1)S(1)} %get-tuple-element.25.normed, bf16[512,64]{1,0:T(8,128)(2,1)S(1)} %get-tuple-element.26.after.chosen, ...), custom_call_target="tpu_custom_call" | custom-call | flops 2147483648 | bytes 4194304 | tf_op jit(solution)/shard_map/pallas_call | solution.py:239
  57.9 0.0 copy-start.2
  57.9 1.1 %shard_map.115 = (bf16[256,1024]{1,0:T(8,128)(2,1)S(1)}, f32[256,1024]{1,0:T(8,128)S(1)}, f32[256,1024]{1,0:T(8,128)S(1)}) custom-call(bf16[256,1024]{1,0:T(8,128)(2,1)S(1)} %get-tuple-element.31.inner, bf16[128,1024]{1,0:T(8,128)(2,1)S(1)} %bitcast.7, bf16[128,1024]{1,0:T(8,128)(2,1)S(1)} %bitcast.9, ...), custom_call_target="tpu_custom_call" | custom-call | flops 1073741824 | bytes 4194304 | tf_op jit(solution)/shard_map/pallas_call | solution.py:384
  59.0 0.0 collective-permute-done.13.refs_14_
  59.0 0.0 collective-permute-done.14.refs_15_
  59.0 0.0 collective-permute-done.17.refs_18_
  59.0 0.0 collective-permute-done.15.refs_16_
  59.1 3.6 %shard_map.116 = bf16[256,1024]{1,0:T(8,128)(2,1)} custom-call(f32[256,1024]{1,0:T(8,128)S(1)} %get-tuple-element.30.hidden, bf16[256,1024]{1,0:T(8,128)(2,1)S(1)} %get-tuple-element.33.given, f32[256,1024]{1,0:T(8,128)S(1)} %get-tuple-element.34.gate_sums, f32[256,1024]{1,0:T(8,128)S(1)} %get-tuple-element.35.up_sums, bf16[128,1024]{1,0:T(8,128)(2,1)S(1)} %bitcast.11, ...), custom_call_target="tpu_custom_call" | custom-call | flops 536870912 | bytes 4194304 | tf_op jit(solution)/shard_map/pallas_call | solution.py:390
  (10 shorter events, 0.0 us)
Async XLA Ops:
  0.0 50.7 %copy-start.5 = (s32[8]{0:T(128)S(1)}, s32[8]{0:T(128)}, u32[]{:S(2)}) copy-start(s32[8]{0:T(128)} %lengths.3) | copy-start | bytes 100
  1.1 12.2 %collective-permute-start.1 = (bf16[384,512]{1,0:T(8,128)(2,1)S(1)}, bf16[384,512]{1,0:T(8,128)(2,1)S(1)}, u32[]{:S(2)}, u32[]{:S(2)}) collective-permute-start(bf16[384,512]{1,0:T(8,128)(2,1)S(1)} %get-tuple-element.32), channel_id=1, source_target_pairs={{0,1},{1,0},{6,7},{7,6},{2,4},{3,5},{4,2},{5,3},{8,9},{9,8},{14,15... | collective-permute-start | bytes 1179656 | tf_op jit(solution)/shard_map/ppermute | solution.py:270
  4.2 11.1 %collective-permute-start = (bf16[384,512]{1,0:T(8,128)(2,1)S(1)}, bf16[384,512]{1,0:T(8,128)(2,1)S(1)}, u32[]{:S(2)}, u32[]{:S(2)}) collective-permute-start(bf16[384,512]{1,0:T(8,128)(2,1)S(1)} %get-tuple-element.32), channel_id=1, source_target_pairs={{0,2},{1,3},{2,0},{3,1},{4,6},{5,7},{6,4},{7,5},{8,10},{9,11},{10,... | collective-permute-start | bytes 1179656 | tf_op jit(solution)/shard_map/ppermute | solution.py:270
  5.8 16.5 %collective-permute-start.8 = (bf16[192,512]{1,0:T(8,128)(2,1)S(1)}, bf16[192,512]{1,0:T(8,128)(2,1)S(1)}, u32[]{:S(2)}, u32[]{:S(2)}) collective-permute-start(bf16[192,512]{1,0:T(8,128)(2,1)S(1)} %get-tuple-element.36), channel_id=1, source_target_pairs={{0,7},{1,6},{2,3},{3,2},{4,5},{5,4},{6,1},{7,0},{8,15},{9,14},{10,... | collective-permute-start | bytes 589832 | tf_op jit(solution)/shard_map/ppermute | solution.py:270
  13.3 16.1 %collective-permute-start.2 = (bf16[384,512]{1,0:T(8,128)(2,1)S(1)}, bf16[384,512]{1,0:T(8,128)(2,1)S(1)}, u32[]{:S(2)}, u32[]{:S(2)}) collective-permute-start(bf16[384,512]{1,0:T(8,128)(2,1)S(1)} %collective-permute-done.1.refs_3_.refs_2_), channel_id=1, source_target_pairs={{0,2},{1,3},{2,0},{3,1},{4,6},{5,7},{6,4},{7,5},{8,10},{9,11},{10,... | collective-permute-start | bytes 1179656 | tf_op jit(solution)/shard_map/ppermute | solution.py:270
  15.3 15.2 %collective-permute-start.3 = (bf16[384,512]{1,0:T(8,128)(2,1)S(1)}, bf16[384,512]{1,0:T(8,128)(2,1)S(1)}, u32[]{:S(2)}, u32[]{:S(2)}) collective-permute-start(bf16[384,512]{1,0:T(8,128)(2,1)S(1)} %collective-permute-done.refs_2_.refs_1_), channel_id=1, source_target_pairs={{0,1},{1,0},{6,7},{7,6},{2,4},{3,5},{4,2},{5,3},{8,9},{9,8},{14,15... | collective-permute-start | bytes 1179656 | tf_op jit(solution)/shard_map/ppermute | solution.py:270
  22.3 5.7 %collective-permute-start.9 = (bf16[192,512]{1,0:T(8,128)(2,1)S(1)}, bf16[192,512]{1,0:T(8,128)(2,1)S(1)}, u32[]{:S(2)}, u32[]{:S(2)}) collective-permute-start(bf16[192,512]{1,0:T(8,128)(2,1)S(1)} %collective-permute-done.8.refs_5_), channel_id=1, source_target_pairs={{0,16},{8,24},{16,0},{24,8},{1,17},{9,25},{17,1},{25,9},{2,18},{10... | collective-permute-start | bytes 589832 | tf_op jit(solution)/shard_map/ppermute | solution.py:255
  23.8 15.8 %collective-permute-start.5 = (bf16[384,512]{1,0:T(8,128)(2,1)S(1)}, bf16[384,512]{1,0:T(8,128)(2,1)S(1)}, u32[]{:S(2)}, u32[]{:S(2)}) collective-permute-start(bf16[384,512]{1,0:T(8,128)(2,1)S(1)} %collective-permute-done.1.refs_3_.refs_2_), channel_id=1, source_target_pairs={{0,8},{8,0},{16,24},{24,16},{1,9},{9,1},{17,25},{25,17},{2,10},{10... | collective-permute-start | bytes 1179656 | tf_op jit(solution)/shard_map/ppermute | solution.py:255
  23.8 16.1 %collective-permute-start.4 = (bf16[384,512]{1,0:T(8,128)(2,1)S(1)}, bf16[384,512]{1,0:T(8,128)(2,1)S(1)}, u32[]{:S(2)}, u32[]{:S(2)}) collective-permute-start(bf16[384,512]{1,0:T(8,128)(2,1)S(1)} %collective-permute-done.refs_2_.refs_1_), channel_id=1, source_target_pairs={{0,8},{8,0},{16,24},{24,16},{1,9},{9,1},{17,25},{25,17},{2,10},{10... | collective-permute-start | bytes 1179656 | tf_op jit(solution)/shard_map/ppermute | solution.py:255
  27.9 11.6 %copy-start.3 = (bf16[192,512]{1,0:T(8,128)(2,1)}, bf16[192,512]{1,0:T(8,128)(2,1)S(1)}, u32[]{:S(2)}) copy-start(bf16[192,512]{1,0:T(8,128)(2,1)S(1)} %collective-permute-done.9.refs_6_) | copy-start | bytes 589828
  27.9 22.1 %collective-permute-start.12 = (bf16[384,512]{1,0:T(8,128)(2,1)S(1)}, bf16[384,512]{1,0:T(8,128)(2,1)}, u32[]{:S(2)}, u32[]{:S(2)}) collective-permute-start(bf16[384,512]{1,0:T(8,128)(2,1)S(1)} %collective-permute-done.1.refs_3_.refs_2_), channel_id=1, source_target_pairs={{2,3},{3,2},{4,5},{5,4},{10,11},{11,10},{12,13},{13,12},{18,19},{1... | collective-permute-start | bytes 1179656 | tf_op jit(solution)/shard_map/ppermute | solution.py:270
  29.4 20.9 %collective-permute-start.10 = (bf16[384,512]{1,0:T(8,128)(2,1)S(1)}, bf16[384,512]{1,0:T(8,128)(2,1)}, u32[]{:S(2)}, u32[]{:S(2)}) collective-permute-start(bf16[384,512]{1,0:T(8,128)(2,1)S(1)} %collective-permute-done.2.refs_4_.refs_3_), channel_id=1, source_target_pairs={{0,1},{1,0},{6,7},{7,6},{2,4},{3,5},{4,2},{5,3},{8,9},{9,8},{14,15... | collective-permute-start | bytes 1179656 | tf_op jit(solution)/shard_map/ppermute | solution.py:270
  30.5 20.1 %collective-permute-start.11 = (bf16[384,512]{1,0:T(8,128)(2,1)S(1)}, bf16[384,512]{1,0:T(8,128)(2,1)}, u32[]{:S(2)}, u32[]{:S(2)}) collective-permute-start(bf16[384,512]{1,0:T(8,128)(2,1)S(1)} %collective-permute-done.3.refs_5_.refs_4_), channel_id=1, source_target_pairs={{2,0},{3,1},{4,6},{5,7},{10,8},{11,9},{12,14},{13,15},{18,16},{19,... | collective-permute-start | bytes 1179656 | tf_op jit(solution)/shard_map/ppermute | solution.py:270
  33.5 14.0 %all-to-all-start = ((bf16[32,2,1280]{2,1,0:T(2,128)(2,1)}), bf16[32,2,1280]{2,1,0:T(2,128)(2,1)S(1)}, u32[]{:S(2)}, u32[]{:S(2)}) async-start(bf16[32,2,1280]{2,1,0:T(2,128)(2,1)} %get-tuple-element.21), calls=%async_computation | async-start | bytes 327680 | tf_op jit(solution)/shard_map/all_to_all | solution.py:423
  39.5 12.2 %collective-permute-start.6 = (bf16[384,512]{1,0:T(8,128)(2,1)S(1)}, bf16[384,512]{1,0:T(8,128)(2,1)S(1)}, u32[]{:S(2)}, u32[]{:S(2)}) collective-permute-start(bf16[384,512]{1,0:T(8,128)(2,1)S(1)} %collective-permute-done.2.refs_4_.refs_3_), channel_id=1, source_target_pairs={{0,8},{8,0},{16,24},{24,16},{1,9},{9,1},{17,25},{25,17},{2,10},{10... | collective-permute-start | bytes 1179656 | tf_op jit(solution)/shard_map/ppermute | solution.py:255
  39.8 15.0 %collective-permute-start.7 = (bf16[384,512]{1,0:T(8,128)(2,1)S(1)}, bf16[384,512]{1,0:T(8,128)(2,1)S(1)}, u32[]{:S(2)}, u32[]{:S(2)}) collective-permute-start(bf16[384,512]{1,0:T(8,128)(2,1)S(1)} %collective-permute-done.3.refs_5_.refs_4_), channel_id=1, source_target_pairs={{0,8},{8,0},{16,24},{24,16},{1,9},{9,1},{17,25},{25,17},{2,10},{10... | collective-permute-start | bytes 1179656 | tf_op jit(solution)/shard_map/ppermute | solution.py:255
  50.0 9.0 %collective-permute-start.17 = (bf16[384,512]{1,0:T(8,128)(2,1)}, bf16[384,512]{1,0:T(8,128)(2,1)S(1)}, u32[]{:S(2)}, u32[]{:S(2)}) collective-permute-start(bf16[384,512]{1,0:T(8,128)(2,1)} %collective-permute-done.12.refs_9_), channel_id=1, source_target_pairs={{0,8},{8,0},{16,24},{24,16},{1,9},{9,1},{17,25},{25,17},{2,10},{10... | collective-permute-start | bytes 1179656 | tf_op jit(solution)/shard_map/ppermute | solution.py:255
  50.2 8.8 %collective-permute-start.15 = (bf16[384,512]{1,0:T(8,128)(2,1)}, bf16[384,512]{1,0:T(8,128)(2,1)S(1)}, u32[]{:S(2)}, u32[]{:S(2)}) collective-permute-start(bf16[384,512]{1,0:T(8,128)(2,1)} %collective-permute-done.10.refs_7_), channel_id=1, source_target_pairs={{0,8},{8,0},{16,24},{24,16},{1,9},{9,1},{17,25},{25,17},{2,10},{10... | collective-permute-start | bytes 1179656 | tf_op jit(solution)/shard_map/ppermute | solution.py:255
  50.6 8.5 %collective-permute-start.16 = (bf16[384,512]{1,0:T(8,128)(2,1)}, bf16[384,512]{1,0:T(8,128)(2,1)S(1)}, u32[]{:S(2)}, u32[]{:S(2)}) collective-permute-start(bf16[384,512]{1,0:T(8,128)(2,1)} %collective-permute-done.11.refs_8_), channel_id=1, source_target_pairs={{0,8},{8,0},{16,24},{24,16},{1,9},{9,1},{17,25},{25,17},{2,10},{10... | collective-permute-start | bytes 1179656 | tf_op jit(solution)/shard_map/ppermute | solution.py:255
  50.7 4.1 %copy-start.4 = (bf16[192,512]{1,0:T(8,128)(2,1)S(1)}, bf16[192,512]{1,0:T(8,128)(2,1)}, u32[]{:S(2)}) copy-start(bf16[192,512]{1,0:T(8,128)(2,1)} %copy-done.3) | copy-start | bytes 589828
  51.7 6.2 %copy-start = (bf16[1,128,1024]{2,1,0:T(8,128)(2,1)S(1)}, bf16[1,128,1024]{2,1,0:T(8,128)(2,1)}, u32[]{:S(2)}) copy-start(bf16[1,128,1024]{2,1,0:T(8,128)(2,1)} %param.17) | copy-start | bytes 786436
  51.7 6.2 %copy-start.1 = (bf16[1,128,1024]{2,1,0:T(8,128)(2,1)S(1)}, bf16[1,128,1024]{2,1,0:T(8,128)(2,1)}, u32[]{:S(2)}) copy-start(bf16[1,128,1024]{2,1,0:T(8,128)(2,1)} %param.18) | copy-start | bytes 786436
  51.7 7.3 %collective-permute-start.13 = (bf16[192,512]{1,0:T(8,128)(2,1)S(1)}, bf16[192,512]{1,0:T(8,128)(2,1)S(1)}, u32[]{:S(2)}, u32[]{:S(2)}) collective-permute-start(bf16[192,512]{1,0:T(8,128)(2,1)S(1)} %collective-permute-done.8.refs_5_), channel_id=1, source_target_pairs={{0,8},{8,0},{16,24},{24,16},{1,9},{9,1},{17,25},{25,17},{2,10},{10... | collective-permute-start | bytes 589832 | tf_op jit(solution)/shard_map/ppermute | solution.py:255
  54.8 4.2 %collective-permute-start.14 = (bf16[192,512]{1,0:T(8,128)(2,1)S(1)}, bf16[192,512]{1,0:T(8,128)(2,1)S(1)}, u32[]{:S(2)}, u32[]{:S(2)}) collective-permute-start(bf16[192,512]{1,0:T(8,128)(2,1)S(1)} %copy-done.4), channel_id=1, source_target_pairs={{0,8},{8,0},{16,24},{24,16},{1,9},{9,1},{17,25},{25,17},{2,10},{10... | collective-permute-start | bytes 589832 | tf_op jit(solution)/shard_map/ppermute | solution.py:255
  57.9 1.2 %copy-start.2 = (bf16[1,128,1024]{2,1,0:T(8,128)(2,1)S(1)}, bf16[1,128,1024]{2,1,0:T(8,128)(2,1)}, u32[]{:S(2)}) copy-start(bf16[1,128,1024]{2,1,0:T(8,128)(2,1)} %param.19) | copy-start | bytes 786436

commit v5 on v4

--- a/solution.py
+++ b/solution.py
@@ -342,32 +342,43 @@
     return spots, read, own_cols, in_order
 
 
+def activate(gate_sum, up_sum):
+    return (gate_sum / (1.0 + jnp.exp(-gate_sum)) * up_sum).astype(jnp.bfloat16)
+
+
 def open_kernel(inner, *refs):
-    pieces, (ordered, gate_sums, up_sums) = refs[:-3], refs[-3:]
-    shares, mine, theirs = pieces[:2], pieces[2:6], pieces[6:]
+    pieces, (ordered, own_active, gate_sums, up_sums) = refs[:-4], refs[-4:]
+    shares, mine, theirs = pieces[:2], pieces[2:11], pieces[11:]
     depth = shares[0].shape[0]
     spots, read, _, in_order = travelled(shares, mine, theirs, depth)
     in_order(inner, ordered)
-    x = ordered[:, : 5 * depth]
-    for i, (part, start) in enumerate(spots):
-        cols = slice(i * lane_chunk, (i + 1) * lane_chunk)
-        gate_sums[:, cols] = dot(x, read(0, part, start, lane_chunk, range(5)))
-        up_sums[:, cols] = dot(x, read(1, part, start, lane_chunk, range(5)))
-
-
-def close_kernel(hidden, given, gate_sums, up_sums, *refs):
+    for part, start in spots:
+        cols = slice(start, start + lane_chunk)
+        span = range(5 if part else 8)
+        x = ordered[:, : len(span) * depth]
+        gate_sum = dot(x, read(0, part, start, lane_chunk, span))
+        up_sum = dot(x, read(1, part, start, lane_chunk, span))
+        if part:
+            gate_sums[:, cols], up_sums[:, cols] = gate_sum, up_sum
+        else:
+            own_active[:, cols] = activate(gate_sum, up_sum)
+
+
+def close_kernel(hidden, given, own_active, gate_sums, up_sums, *refs):
     pieces, (out, ordered, active) = refs[:-3], refs[-3:]
     shares, mine, theirs = pieces[:1], pieces[1:10], pieces[10:]
     depth = shares[0].shape[0]
     spots, read, own_cols, in_order = travelled([None, None, *shares], mine, theirs, depth)
     x = given[:, 5 * depth :]
-    for i, (part, start) in enumerate(spots):
-        cols = slice(i * lane_chunk, (i + 1) * lane_chunk)
-        gate_sum = gate_sums[:, cols] + dot(x, read(0, part, start, lane_chunk, (5, 6, 7)))
-        up_sum = up_sums[:, cols] + dot(x, read(1, part, start, lane_chunk, (5, 6, 7)))
-        active[:, own_cols(part, start, lane_chunk)] = (
-            gate_sum / (1.0 + jnp.exp(-gate_sum)) * up_sum
-        ).astype(jnp.bfloat16)
+    for part, start in spots:
+        cols = slice(start, start + lane_chunk)
+        if part:
+            gate_sum = gate_sums[:, cols] + dot(x, read(0, part, start, lane_chunk, (5, 6, 7)))
+            up_sum = up_sums[:, cols] + dot(x, read(1, part, start, lane_chunk, (5, 6, 7)))
+            units = activate(gate_sum, up_sum)
+        else:
+            units = own_active[:, cols]
+        active[:, own_cols(part, start, lane_chunk)] = units
     in_order(active, ordered)
     x = ordered[...]
     for part, start in spots:
@@ -379,13 +390,13 @@
 
 def hop_feed(inner, hidden, shares, mine, theirs):
     (count, width), inside = inner.shape, shares[0].shape[1]
-    sums = shape(count, inside, jnp.float32)
-    early = [*shares[:2], *mine[:4], *theirs[:4]]
-    ordered, gate_sums, up_sums = call(
-        open_kernel, (shape(count, width), sums, sums), [whole()] * (1 + len(early)),
-        4 * count * width * inside, 4 << 20, 8,
+    sums = shape(count, inside // 2, jnp.float32)
+    early = [*shares[:2], *mine, *theirs[:4]]
+    opened = call(
+        open_kernel, (shape(count, width), shape(count, inside // 2), sums, sums),
+        [whole()] * (1 + len(early)), 4 * count * width * inside, 4 << 20, 8,
     )(inner, *early)
-    late = [hidden, ordered, gate_sums, up_sums, shares[2], *mine, *theirs]
+    late = [hidden, *opened, shares[2], *mine, *theirs]
     scratch = [pltpu.VMEM((count, inside), jnp.bfloat16), pltpu.VMEM((count, inside), jnp.bfloat16)]
     return call(
         close_kernel, shape(count, width), [whole()] * len(late),

time: 63 us -> 63.3 us (level)
  starting transfers between devices: 26.7 us -> 25.4 us
  Pallas kernels: 13.9 us -> 14.9 us
  local copies, waits for them, and re-layouts: 0.03 us -> 0.7 us
    pallas_call x1, Pallas kernels: 1.09 us -> 2.34 us  [hop_feed(): call(open_kernel, (shape(count, width), shape(count, inside // 2), sums,...]
    pallas_call x1, Pallas kernels: 0.35 us -> 1.26 us  [shelve(): call(shelve_kernel, (rows, rows, pltpu.VMEM((2 * count, items), jnp.bfloa...]
    ppermute x8, starting transfers between devices: 14.2 us -> 13.5 us  [send(): return lax.ppermute(block, 'col', route)]
    unnamed x12 -> x18, local copies, waits for them, and re-layouts: 0.03 us -> 0.7 us
    pallas_call x1, Pallas kernels: 1.68 us -> 1.01 us  [greet(): call(greet_kernel, out, [whole(pltpu.HBM)] * 3, 0, 1 << 18, 4, scratch)]
  transfers between devices with their start and end apart: 19 -> 19, of which waited for: 5 -> 5; matrix products, arithmetic and copies ran while one was open for 0% -> 0% of each run, Pallas kernels for 15% -> 17%
where the time goes in v5:
time: 63.3 us; the launch traced here: 62.9 us
  starting transfers between devices  25.4 us (40%)
  waiting for transfers between devices  21.7 us (34%)
  Pallas kernels  14.9 us (24%)
  local copies, waits for them, and re-layouts  0.7 us (1%)
    ppermute x8, starting transfers between devices, send(): return lax.ppermute(block, 'col', route)  13.5 us
    ppermute x8, waiting for transfers between devices, send(): return lax.ppermute(block, 'col', route)  10.9 us
    all_to_all x1, waiting for transfers between devices, body(): got = lax.all_to_all(sent, both, 0, 0)  7.4 us
    ppermute x10, starting transfers between devices, partner(): lax.ppermute(block, 'row', [(i, i ^ distance) for i in range(lax.axis_siz...  6.01 us
    all_to_all x1, starting transfers between devices, body(): got = lax.all_to_all(sent, both, 0, 0)  5.85 us
    pallas_call x2, Pallas kernels, mix(): call(mix_kernel, out, [whole(pltpu.SMEM)] + [whole()] * len(operands), 8...  3.87 us
    ppermute x10, waiting for transfers between devices, partner(): lax.ppermute(block, 'row', [(i, i ^ distance) for i in range(lax.axis_siz...  3.44 us
    pallas_call x1, Pallas kernels, hop_feed(): call(close_kernel, shape(count, width), [whole()] * len(late), 2 * count...  3.19 us
  transfers between devices with their start and end apart: 19, of which 5 were waited for; matrix products, arithmetic and copies ran while one was open for 0% of the time, Pallas kernels for 17%

profile of v5, /device:TPU:0, one launch (start us, length us, event | category | flops | bytes accessed | tf_op | source)
XLA Modules:
  0.0 62.9 jit_solution(4980161243133237830)
XLA Ops:
  0.0 1.1 %shard_map.114 = (bf16[384,512]{1,0:T(8,128)(2,1)S(1)}, bf16[192,512]{1,0:T(8,128)(2,1)S(1)}) custom-call(bf16[128,1024]{1,0:T(8,128)(2,1)} %bitcast.6, bf16[128,1024]{1,0:T(8,128)(2,1)} %bitcast.8, bf16[128,1024]{1,0:T(8,128)(2,1)} %bitcast.10), custom_call_target="tpu_custom_call" | custom-call | bytes 1048576 | tf_op jit(solution)/shard_map/pallas_call | solution.py:88
  1.1 3.1 %collective-permute-start.1 = (bf16[384,512]{1,0:T(8,128)(2,1)S(1)}, bf16[384,512]{1,0:T(8,128)(2,1)S(1)}, u32[]{:S(2)}, u32[]{:S(2)}) collective-permute-start(bf16[384,512]{1,0:T(8,128)(2,1)S(1)} %get-tuple-element.33), channel_id=1, source_target_pairs={{0,1},{1,0},{6,7},{7,6},{2,4},{3,5},{4,2},{5,3},{8,9},{9,8},{14,15... | collective-permute-start | bytes 1179656 | tf_op jit(solution)/shard_map/ppermute | solution.py:270
  4.2 1.6 %collective-permute-start = (bf16[384,512]{1,0:T(8,128)(2,1)S(1)}, bf16[384,512]{1,0:T(8,128)(2,1)S(1)}, u32[]{:S(2)}, u32[]{:S(2)}) collective-permute-start(bf16[384,512]{1,0:T(8,128)(2,1)S(1)} %get-tuple-element.33), channel_id=1, source_target_pairs={{0,2},{1,3},{2,0},{3,1},{4,6},{5,7},{6,4},{7,5},{8,10},{9,11},{10,... | collective-permute-start | bytes 1179656 | tf_op jit(solution)/shard_map/ppermute | solution.py:270
  5.8 2.3 %collective-permute-start.4 = (bf16[192,512]{1,0:T(8,128)(2,1)S(1)}, bf16[192,512]{1,0:T(8,128)(2,1)S(1)}, u32[]{:S(2)}, u32[]{:S(2)}) collective-permute-start(bf16[192,512]{1,0:T(8,128)(2,1)S(1)} %get-tuple-element.34), channel_id=1, source_target_pairs={{0,7},{1,6},{2,3},{3,2},{4,5},{5,4},{6,1},{7,0},{8,15},{9,14},{10,... | collective-permute-start | bytes 589832 | tf_op jit(solution)/shard_map/ppermute | solution.py:270
  8.1 5.2 %collective-permute-done.1.refs_3_.refs_2_ = bf16[384,512]{1,0:T(8,128)(2,1)S(1)} collective-permute-done((bf16[384,512]{1,0:T(8,128)(2,1)S(1)}, bf16[384,512]{1,0:T(8,128)(2,1)S(1)}, u32[]{:S(2)}, u32[]{:S(2)}) %collective-permute-start.1) | collective-permute-done | bytes 393248 | tf_op jit(solution)/shard_map/ppermute | solution.py:270
  13.3 1.8 %collective-permute-start.2 = (bf16[384,512]{1,0:T(8,128)(2,1)S(1)}, bf16[384,512]{1,0:T(8,128)(2,1)S(1)}, u32[]{:S(2)}, u32[]{:S(2)}) collective-permute-start(bf16[384,512]{1,0:T(8,128)(2,1)S(1)} %collective-permute-done.1.refs_3_.refs_2_), channel_id=1, source_target_pairs={{0,2},{1,3},{2,0},{3,1},{4,6},{5,7},{6,4},{7,5},{8,10},{9,11},{10,... | collective-permute-start | bytes 1179656 | tf_op jit(solution)/shard_map/ppermute | solution.py:270
  15.1 0.2 collective-permute-done.refs_2_.refs_1_
  15.3 1.5 %collective-permute-start.3 = (bf16[384,512]{1,0:T(8,128)(2,1)S(1)}, bf16[384,512]{1,0:T(8,128)(2,1)S(1)}, u32[]{:S(2)}, u32[]{:S(2)}) collective-permute-start(bf16[384,512]{1,0:T(8,128)(2,1)S(1)} %collective-permute-done.refs_2_.refs_1_), channel_id=1, source_target_pairs={{0,1},{1,0},{6,7},{7,6},{2,4},{3,5},{4,2},{5,3},{8,9},{9,8},{14,15... | collective-permute-start | bytes 1179656 | tf_op jit(solution)/shard_map/ppermute | solution.py:270
  16.8 5.5 %collective-permute-done.4.refs_6_.refs_5_ = bf16[192,512]{1,0:T(8,128)(2,1)S(1)} collective-permute-done((bf16[192,512]{1,0:T(8,128)(2,1)S(1)}, bf16[192,512]{1,0:T(8,128)(2,1)S(1)}, u32[]{:S(2)}, u32[]{:S(2)}) %collective-permute-start.4) | collective-permute-done | bytes 196640 | tf_op jit(solution)/shard_map/ppermute | solution.py:270
  22.3 1.5 %collective-permute-start.5 = (bf16[192,512]{1,0:T(8,128)(2,1)S(1)}, bf16[192,512]{1,0:T(8,128)(2,1)S(1)}, u32[]{:S(2)}, u32[]{:S(2)}) collective-permute-start(bf16[192,512]{1,0:T(8,128)(2,1)S(1)} %collective-permute-done.4.refs_6_.refs_5_), channel_id=1, source_target_pairs={{0,16},{8,24},{16,0},{24,8},{1,17},{9,25},{17,1},{25,9},{2,18},{10... | collective-permute-start | bytes 589832 | tf_op jit(solution)/shard_map/ppermute | solution.py:255
  23.8 0.7 %collective-permute-start.8 = (bf16[384,512]{1,0:T(8,128)(2,1)S(1)}, bf16[384,512]{1,0:T(8,128)(2,1)S(1)}, u32[]{:S(2)}, u32[]{:S(2)}) collective-permute-start(bf16[384,512]{1,0:T(8,128)(2,1)S(1)} %collective-permute-done.1.refs_3_.refs_2_), channel_id=1, source_target_pairs={{2,3},{3,2},{4,5},{5,4},{10,11},{11,10},{12,13},{13,12},{18,19},{1... | collective-permute-start | bytes 1179656 | tf_op jit(solution)/shard_map/ppermute | solution.py:270
  24.4 0.1 collective-permute-start.10
  24.5 3.4 %collective-permute-done.5.refs_7_.refs_6_ = bf16[192,512]{1,0:T(8,128)(2,1)S(1)} collective-permute-done((bf16[192,512]{1,0:T(8,128)(2,1)S(1)}, bf16[192,512]{1,0:T(8,128)(2,1)S(1)}, u32[]{:S(2)}, u32[]{:S(2)}) %collective-permute-start.5) | collective-permute-done | bytes 196640 | tf_op jit(solution)/shard_map/ppermute | solution.py:255
  27.9 0.0 collective-permute-start.9
  27.9 0.0 collective-permute-done.2.refs_4_.refs_3_
  28.0 1.2 %collective-permute-start.6 = (bf16[384,512]{1,0:T(8,128)(2,1)S(1)}, bf16[384,512]{1,0:T(8,128)(2,1)S(1)}, u32[]{:S(2)}, u32[]{:S(2)}) collective-permute-start(bf16[384,512]{1,0:T(8,128)(2,1)S(1)} %collective-permute-done.2.refs_4_.refs_3_), channel_id=1, source_target_pairs={{0,1},{1,0},{6,7},{7,6},{2,4},{3,5},{4,2},{5,3},{8,9},{9,8},{14,15... | collective-permute-start | bytes 1179656 | tf_op jit(solution)/shard_map/ppermute | solution.py:270
  29.2 0.0 collective-permute-done.3.refs_5_.refs_4_
  29.2 1.3 %collective-permute-start.7 = (bf16[384,512]{1,0:T(8,128)(2,1)S(1)}, bf16[384,512]{1,0:T(8,128)(2,1)S(1)}, u32[]{:S(2)}, u32[]{:S(2)}) collective-permute-start(bf16[384,512]{1,0:T(8,128)(2,1)S(1)} %collective-permute-done.3.refs_5_.refs_4_), channel_id=1, source_target_pairs={{2,0},{3,1},{4,6},{5,7},{10,8},{11,9},{12,14},{13,15},{18,16},{19,... | collective-permute-start | bytes 1179656 | tf_op jit(solution)/shard_map/ppermute | solution.py:270
  30.5 1.0 %shard_map.109 = (bf16[32,2,1280]{2,1,0:T(2,128)(2,1)S(1)}, s32[1,256]{1,0:T(1,128)S(1)}, f32[2,1024]{1,0:T(2,128)S(1)}) custom-call(s32[1,256]{1,0:T(1,128)} %bitcast.14, f32[2,1024]{1,0:T(2,128)} %bitcast.13, bf16[2,1024]{1,0:T(2,128)(2,1)} %rows_far.1), custom_call_target="tpu_custom_call" | custom-call | bytes 262144 | tf_op jit(solution)/shard_map/pallas_call | solution.py:119
  31.5 0.7 %copy-done.7 = bf16[32,2,1280]{2,1,0:T(2,128)(2,1)} copy-done((bf16[32,2,1280]{2,1,0:T(2,128)(2,1)}, bf16[32,2,1280]{2,1,0:T(2,128)(2,1)S(1)}, u32[]{:S(2)}) %copy-start.7) | copy-done | bytes 163864
  32.2 5.8 %all-to-all-start = ((bf16[32,2,1280]{2,1,0:T(2,128)(2,1)}), bf16[32,2,1280]{2,1,0:T(2,128)(2,1)}, u32[]{:S(2)}, u32[]{:S(2)}) async-start(bf16[32,2,1280]{2,1,0:T(2,128)(2,1)} %copy-done.7), calls=%async_computation | async-start | bytes 327680 | tf_op jit(solution)/shard_map/all_to_all | solution.py:434
  38.0 0.0 collective-permute-done.8.refs_10_.refs_9_
  38.0 0.3 collective-permute-start.11
  38.3 0.0 collective-permute-done.10.refs_12_.refs_11_
  38.3 0.3 collective-permute-start.12
  38.6 7.4 %all-to-all-done.got = bf16[32,2,1280]{2,1,0:T(2,128)(2,1)} async-done(((bf16[32,2,1280]{2,1,0:T(2,128)(2,1)}), bf16[32,2,1280]{2,1,0:T(2,128)(2,1)}, u32[]{:S(2)}, u32[]{:S(2)}) %all-to-all-start) | async-done | bytes 163872 | tf_op jit(solution)/shard_map/all_to_all | solution.py:434
  46.0 1.3 %shard_map.110 = (bf16[64,1024]{1,0:T(8,128)(2,1)S(1)}, bf16[64,1024]{1,0:T(8,128)(2,1)S(1)}, bf16[512,64]{1,0:T(8,128)(2,1)S(1)}) custom-call(bf16[32,2,1280]{2,1,0:T(2,128)(2,1)} %all-to-all-done.got, s32[1,256]{1,0:T(1,128)S(1)} %get-tuple-element.23.own, f32[2,1024]{1,0:T(2,128)S(1)} %get-tuple-element.24.gains), custom_call_target="tpu_custom_call" | custom-call | flops 1048576 | bytes 524288 | tf_op jit(solution)/shard_map/pallas_call | solution.py:186
  47.3 2.1 %shard_map.111 = (f32[512,1024]{1,0:T(8,128)S(1)}, bf16[512,1024]{1,0:T(8,128)(2,1)S(1)}, bf16[256,1536]{1,0:T(8,128)(2,1)S(1)}) custom-call(bf16[512,64]{1,0:T(8,128)(2,1)S(1)} %get-tuple-element.27.after.chosen, bf16[256,1024]{1,0:T(8,128)(2,1)} %bitcast.12, s32[1,1024]{1,0:T(1,128)} %lengths_far.1, bf16[512,1024]{1,0:T(8,128)(2,1)} %constant.4.clone.refs_0_, ...), custom_call_target="tpu_custom_call" | custom-call | flops 536870912 | bytes 5242880 | tf_op jit(solution)/shard_map/pallas_call | solution.py:145
  49.5 0.0 collective-permute-done.9.refs_11_.refs_10_
  49.5 0.2 collective-permute-start.17
  49.7 0.0 collective-permute-done.6.refs_8_.refs_7_
  49.7 0.4 collective-permute-start.15
  50.0 0.0 collective-permute-done.7.refs_9_.refs_8_
  50.0 0.1 collective-permute-start.16
  50.2 0.9 %shard_map.112.given = f32[256,1024]{1,0:T(8,128)S(1)} custom-call(s32[8]{0:T(128)S(1)} %copy-done.8, bf16[64,1024]{1,0:T(8,128)(2,1)S(1)} %get-tuple-element.25.given, bf16[64,1024]{1,0:T(8,128)(2,1)S(1)} %get-tuple-element.26.normed, bf16[512,64]{1,0:T(8,128)(2,1)S(1)} %get-tuple-element.27.after.chosen, f32[2,1024]{1,0:T(2,128)S(1)} %get-tuple-element.24.gains, ...), custom_call_target="tpu_custom_call" | custom-call | flops 2147483648 | bytes 4194304 | tf_op jit(solution)/shard_map/pallas_call | solution.py:239
  51.1 0.0 copy-start
  51.1 0.0 copy-start.1
  51.1 0.0 collective-permute-done.11.refs_13_.refs_12_
  51.2 3.1 %collective-permute-start.13 = (bf16[192,512]{1,0:T(8,128)(2,1)S(1)}, bf16[192,512]{1,0:T(8,128)(2,1)S(1)}, u32[]{:S(2)}, u32[]{:S(2)}) collective-permute-start(bf16[192,512]{1,0:T(8,128)(2,1)S(1)} %copy-done.4), channel_id=1, source_target_pairs={{0,8},{8,0},{16,24},{24,16},{1,9},{9,1},{17,25},{25,17},{2,10},{10... | collective-permute-start | bytes 589832 | tf_op jit(solution)/shard_map/ppermute | solution.py:255
  54.2 0.0 collective-permute-done.12.refs_14_.refs_13_
  54.2 0.1 collective-permute-start.14
  54.3 2.9 %shard_map.113 = (f32[256,1024]{1,0:T(8,128)S(1)}, bf16[256,1024]{1,0:T(8,128)(2,1)S(1)}) custom-call(s32[8]{0:T(128)S(1)} %copy-done.8, f32[256,1024]{1,0:T(8,128)S(1)} %shard_map.112.given, bf16[64,1024]{1,0:T(8,128)(2,1)S(1)} %get-tuple-element.26.normed, bf16[512,64]{1,0:T(8,128)(2,1)S(1)} %get-tuple-element.27.after.chosen, ...), custom_call_target="tpu_custom_call" | custom-call | flops 2147483648 | bytes 4194304 | tf_op jit(solution)/shard_map/pallas_call | solution.py:239
  57.3 0.0 copy-start.2
  57.3 2.3 %shard_map.115 = (bf16[256,1024]{1,0:T(8,128)(2,1)S(1)}, bf16[256,512]{1,0:T(8,128)(2,1)S(1)}, f32[256,512]{1,0:T(8,128)S(1)}, f32[256,512]{1,0:T(8,128)S(1)}) custom-call(bf16[256,1024]{1,0:T(8,128)(2,1)S(1)} %get-tuple-element.32.inner, bf16[128,1024]{1,0:T(8,128)(2,1)S(1)} %bitcast.7, bf16[128,1024]{1,0:T(8,128)(2,1)S(1)} %bitcast.9, ...), custom_call_target="tpu_custom_call" | custom-call | flops 1073741824 | bytes 4194304 | tf_op jit(solution)/shard_map/pallas_call | solution.py:395
  59.7 0.0 collective-permute-done.14.refs_15_
  59.7 0.0 collective-permute-done.17.refs_18_
  59.7 0.0 collective-permute-done.16.refs_17_
  59.7 3.2 %shard_map.116 = bf16[256,1024]{1,0:T(8,128)(2,1)} custom-call(f32[256,1024]{1,0:T(8,128)S(1)} %get-tuple-element.31.hidden, bf16[256,1024]{1,0:T(8,128)(2,1)S(1)} %get-tuple-element.35.given, bf16[256,512]{1,0:T(8,128)(2,1)S(1)} %get-tuple-element.36.own_active, f32[256,512]{1,0:T(8,128)S(1)} %get-tuple-element.37.gate_sums, ...), custom_call_target="tpu_custom_call" | custom-call | flops 536870912 | bytes 4194304 | tf_op jit(solution)/shard_map/pallas_call | solution.py:401
  (16 shorter events, 0.0 us)
Async XLA Ops:
  0.0 50.2 %copy-start.8 = (s32[8]{0:T(128)S(1)}, s32[8]{0:T(128)}, u32[]{:S(2)}) copy-start(s32[8]{0:T(128)} %lengths.3) | copy-start | bytes 100
  1.1 12.2 %collective-permute-start.1 = (bf16[384,512]{1,0:T(8,128)(2,1)S(1)}, bf16[384,512]{1,0:T(8,128)(2,1)S(1)}, u32[]{:S(2)}, u32[]{:S(2)}) collective-permute-start(bf16[384,512]{1,0:T(8,128)(2,1)S(1)} %get-tuple-element.33), channel_id=1, source_target_pairs={{0,1},{1,0},{6,7},{7,6},{2,4},{3,5},{4,2},{5,3},{8,9},{9,8},{14,15... | collective-permute-start | bytes 1179656 | tf_op jit(solution)/shard_map/ppermute | solution.py:270
  4.2 11.1 %collective-permute-start = (bf16[384,512]{1,0:T(8,128)(2,1)S(1)}, bf16[384,512]{1,0:T(8,128)(2,1)S(1)}, u32[]{:S(2)}, u32[]{:S(2)}) collective-permute-start(bf16[384,512]{1,0:T(8,128)(2,1)S(1)} %get-tuple-element.33), channel_id=1, source_target_pairs={{0,2},{1,3},{2,0},{3,1},{4,6},{5,7},{6,4},{7,5},{8,10},{9,11},{10,... | collective-permute-start | bytes 1179656 | tf_op jit(solution)/shard_map/ppermute | solution.py:270
  5.8 16.5 %collective-permute-start.4 = (bf16[192,512]{1,0:T(8,128)(2,1)S(1)}, bf16[192,512]{1,0:T(8,128)(2,1)S(1)}, u32[]{:S(2)}, u32[]{:S(2)}) collective-permute-start(bf16[192,512]{1,0:T(8,128)(2,1)S(1)} %get-tuple-element.34), channel_id=1, source_target_pairs={{0,7},{1,6},{2,3},{3,2},{4,5},{5,4},{6,1},{7,0},{8,15},{9,14},{10,... | collective-permute-start | bytes 589832 | tf_op jit(solution)/shard_map/ppermute | solution.py:270
  13.3 14.7 %collective-permute-start.2 = (bf16[384,512]{1,0:T(8,128)(2,1)S(1)}, bf16[384,512]{1,0:T(8,128)(2,1)S(1)}, u32[]{:S(2)}, u32[]{:S(2)}) collective-permute-start(bf16[384,512]{1,0:T(8,128)(2,1)S(1)} %collective-permute-done.1.refs_3_.refs_2_), channel_id=1, source_target_pairs={{0,2},{1,3},{2,0},{3,1},{4,6},{5,7},{6,4},{7,5},{8,10},{9,11},{10,... | collective-permute-start | bytes 1179656 | tf_op jit(solution)/shard_map/ppermute | solution.py:270
  15.3 13.9 %collective-permute-start.3 = (bf16[384,512]{1,0:T(8,128)(2,1)S(1)}, bf16[384,512]{1,0:T(8,128)(2,1)S(1)}, u32[]{:S(2)}, u32[]{:S(2)}) collective-permute-start(bf16[384,512]{1,0:T(8,128)(2,1)S(1)} %collective-permute-done.refs_2_.refs_1_), channel_id=1, source_target_pairs={{0,1},{1,0},{6,7},{7,6},{2,4},{3,5},{4,2},{5,3},{8,9},{9,8},{14,15... | collective-permute-start | bytes 1179656 | tf_op jit(solution)/shard_map/ppermute | solution.py:270
  22.3 6.9 %copy-start.3 = (bf16[192,512]{1,0:T(8,128)(2,1)}, bf16[192,512]{1,0:T(8,128)(2,1)S(1)}, u32[]{:S(2)}) copy-start(bf16[192,512]{1,0:T(8,128)(2,1)S(1)} %collective-permute-done.4.refs_6_.refs_5_) | copy-start | bytes 589828
  22.3 5.7 %collective-permute-start.5 = (bf16[192,512]{1,0:T(8,128)(2,1)S(1)}, bf16[192,512]{1,0:T(8,128)(2,1)S(1)}, u32[]{:S(2)}, u32[]{:S(2)}) collective-permute-start(bf16[192,512]{1,0:T(8,128)(2,1)S(1)} %collective-permute-done.4.refs_6_.refs_5_), channel_id=1, source_target_pairs={{0,16},{8,24},{16,0},{24,8},{1,17},{9,25},{17,1},{25,9},{2,18},{10... | collective-permute-start | bytes 589832 | tf_op jit(solution)/shard_map/ppermute | solution.py:255
  23.8 14.3 %collective-permute-start.8 = (bf16[384,512]{1,0:T(8,128)(2,1)S(1)}, bf16[384,512]{1,0:T(8,128)(2,1)S(1)}, u32[]{:S(2)}, u32[]{:S(2)}) collective-permute-start(bf16[384,512]{1,0:T(8,128)(2,1)S(1)} %collective-permute-done.1.refs_3_.refs_2_), channel_id=1, source_target_pairs={{2,3},{3,2},{4,5},{5,4},{10,11},{11,10},{12,13},{13,12},{18,19},{1... | collective-permute-start | bytes 1179656 | tf_op jit(solution)/shard_map/ppermute | solution.py:270
  24.4 13.9 %collective-permute-start.10 = (bf16[384,512]{1,0:T(8,128)(2,1)S(1)}, bf16[384,512]{1,0:T(8,128)(2,1)S(1)}, u32[]{:S(2)}, u32[]{:S(2)}) collective-permute-start(bf16[384,512]{1,0:T(8,128)(2,1)S(1)} %collective-permute-done.1.refs_3_.refs_2_), channel_id=1, source_target_pairs={{0,8},{8,0},{16,24},{24,16},{1,9},{9,1},{17,25},{25,17},{2,10},{10... | collective-permute-start | bytes 1179656 | tf_op jit(solution)/shard_map/ppermute | solution.py:255
  27.9 2.5 %copy-start.5 = (bf16[192,512]{1,0:T(8,128)(2,1)}, bf16[192,512]{1,0:T(8,128)(2,1)S(1)}, u32[]{:S(2)}) copy-start(bf16[192,512]{1,0:T(8,128)(2,1)S(1)} %collective-permute-done.5.refs_7_.refs_6_) | copy-start | bytes 589828
  27.9 21.5 %collective-permute-start.9 = (bf16[384,512]{1,0:T(8,128)(2,1)S(1)}, bf16[384,512]{1,0:T(8,128)(2,1)S(1)}, u32[]{:S(2)}, u32[]{:S(2)}) collective-permute-start(bf16[384,512]{1,0:T(8,128)(2,1)S(1)} %collective-permute-done.refs_2_.refs_1_), channel_id=1, source_target_pairs={{0,8},{8,0},{16,24},{24,16},{1,9},{9,1},{17,25},{25,17},{2,10},{10... | collective-permute-start | bytes 1179656 | tf_op jit(solution)/shard_map/ppermute | solution.py:255
  28.0 21.7 %collective-permute-start.6 = (bf16[384,512]{1,0:T(8,128)(2,1)S(1)}, bf16[384,512]{1,0:T(8,128)(2,1)S(1)}, u32[]{:S(2)}, u32[]{:S(2)}) collective-permute-start(bf16[384,512]{1,0:T(8,128)(2,1)S(1)} %collective-permute-done.2.refs_4_.refs_3_), channel_id=1, source_target_pairs={{0,1},{1,0},{6,7},{7,6},{2,4},{3,5},{4,2},{5,3},{8,9},{9,8},{14,15... | collective-permute-start | bytes 1179656 | tf_op jit(solution)/shard_map/ppermute | solution.py:270
  29.2 20.9 %collective-permute-start.7 = (bf16[384,512]{1,0:T(8,128)(2,1)S(1)}, bf16[384,512]{1,0:T(8,128)(2,1)S(1)}, u32[]{:S(2)}, u32[]{:S(2)}) collective-permute-start(bf16[384,512]{1,0:T(8,128)(2,1)S(1)} %collective-permute-done.3.refs_5_.refs_4_), channel_id=1, source_target_pairs={{2,0},{3,1},{4,6},{5,7},{10,8},{11,9},{12,14},{13,15},{18,16},{19,... | collective-permute-start | bytes 1179656 | tf_op jit(solution)/shard_map/ppermute | solution.py:270
  31.5 0.7 %copy-start.7 = (bf16[32,2,1280]{2,1,0:T(2,128)(2,1)}, bf16[32,2,1280]{2,1,0:T(2,128)(2,1)S(1)}, u32[]{:S(2)}) copy-start(bf16[32,2,1280]{2,1,0:T(2,128)(2,1)S(1)} %get-tuple-element.22) | copy-start | bytes 491524
  32.2 13.8 %all-to-all-start = ((bf16[32,2,1280]{2,1,0:T(2,128)(2,1)}), bf16[32,2,1280]{2,1,0:T(2,128)(2,1)}, u32[]{:S(2)}, u32[]{:S(2)}) async-start(bf16[32,2,1280]{2,1,0:T(2,128)(2,1)} %copy-done.7), calls=%async_computation | async-start | bytes 327680 | tf_op jit(solution)/shard_map/all_to_all | solution.py:434
  38.0 13.1 %collective-permute-start.11 = (bf16[384,512]{1,0:T(8,128)(2,1)S(1)}, bf16[384,512]{1,0:T(8,128)(2,1)}, u32[]{:S(2)}, u32[]{:S(2)}) collective-permute-start(bf16[384,512]{1,0:T(8,128)(2,1)S(1)} %collective-permute-done.2.refs_4_.refs_3_), channel_id=1, source_target_pairs={{0,8},{8,0},{16,24},{24,16},{1,9},{9,1},{17,25},{25,17},{2,10},{10... | collective-permute-start | bytes 1179656 | tf_op jit(solution)/shard_map/ppermute | solution.py:255
  38.3 15.9 %collective-permute-start.12 = (bf16[384,512]{1,0:T(8,128)(2,1)S(1)}, bf16[384,512]{1,0:T(8,128)(2,1)}, u32[]{:S(2)}, u32[]{:S(2)}) collective-permute-start(bf16[384,512]{1,0:T(8,128)(2,1)S(1)} %collective-permute-done.3.refs_5_.refs_4_), channel_id=1, source_target_pairs={{0,8},{8,0},{16,24},{24,16},{1,9},{9,1},{17,25},{25,17},{2,10},{10... | collective-permute-start | bytes 1179656 | tf_op jit(solution)/shard_map/ppermute | solution.py:255
  49.5 10.2 %collective-permute-start.17 = (bf16[384,512]{1,0:T(8,128)(2,1)S(1)}, bf16[384,512]{1,0:T(8,128)(2,1)S(1)}, u32[]{:S(2)}, u32[]{:S(2)}) collective-permute-start(bf16[384,512]{1,0:T(8,128)(2,1)S(1)} %collective-permute-done.8.refs_10_.refs_9_), channel_id=1, source_target_pairs={{0,8},{8,0},{16,24},{24,16},{1,9},{9,1},{17,25},{25,17},{2,10},{10... | collective-permute-start | bytes 1179656 | tf_op jit(solution)/shard_map/ppermute | solution.py:255
  49.7 10.0 %collective-permute-start.15 = (bf16[384,512]{1,0:T(8,128)(2,1)S(1)}, bf16[384,512]{1,0:T(8,128)(2,1)S(1)}, u32[]{:S(2)}, u32[]{:S(2)}) collective-permute-start(bf16[384,512]{1,0:T(8,128)(2,1)S(1)} %collective-permute-done.6.refs_8_.refs_7_), channel_id=1, source_target_pairs={{0,8},{8,0},{16,24},{24,16},{1,9},{9,1},{17,25},{25,17},{2,10},{10... | collective-permute-start | bytes 1179656 | tf_op jit(solution)/shard_map/ppermute | solution.py:255
  50.0 9.7 %collective-permute-start.16 = (bf16[384,512]{1,0:T(8,128)(2,1)S(1)}, bf16[384,512]{1,0:T(8,128)(2,1)S(1)}, u32[]{:S(2)}, u32[]{:S(2)}) collective-permute-start(bf16[384,512]{1,0:T(8,128)(2,1)S(1)} %collective-permute-done.7.refs_9_.refs_8_), channel_id=1, source_target_pairs={{0,8},{8,0},{16,24},{24,16},{1,9},{9,1},{17,25},{25,17},{2,10},{10... | collective-permute-start | bytes 1179656 | tf_op jit(solution)/shard_map/ppermute | solution.py:255
  50.2 1.0 %copy-start.4 = (bf16[192,512]{1,0:T(8,128)(2,1)S(1)}, bf16[192,512]{1,0:T(8,128)(2,1)}, u32[]{:S(2)}) copy-start(bf16[192,512]{1,0:T(8,128)(2,1)} %copy-done.3) | copy-start | bytes 589828
  50.2 4.1 %copy-start.6 = (bf16[192,512]{1,0:T(8,128)(2,1)S(1)}, bf16[192,512]{1,0:T(8,128)(2,1)}, u32[]{:S(2)}) copy-start(bf16[192,512]{1,0:T(8,128)(2,1)} %copy-done.5) | copy-start | bytes 589828
  51.1 6.2 %copy-start = (bf16[1,128,1024]{2,1,0:T(8,128)(2,1)S(1)}, bf16[1,128,1024]{2,1,0:T(8,128)(2,1)}, u32[]{:S(2)}) copy-start(bf16[1,128,1024]{2,1,0:T(8,128)(2,1)} %param.17) | copy-start | bytes 786436
  51.1 6.2 %copy-start.1 = (bf16[1,128,1024]{2,1,0:T(8,128)(2,1)S(1)}, bf16[1,128,1024]{2,1,0:T(8,128)(2,1)}, u32[]{:S(2)}) copy-start(bf16[1,128,1024]{2,1,0:T(8,128)(2,1)} %param.18) | copy-start | bytes 786436
  51.2 8.5 %collective-permute-start.13 = (bf16[192,512]{1,0:T(8,128)(2,1)S(1)}, bf16[192,512]{1,0:T(8,128)(2,1)S(1)}, u32[]{:S(2)}, u32[]{:S(2)}) collective-permute-start(bf16[192,512]{1,0:T(8,128)(2,1)S(1)} %copy-done.4), channel_id=1, source_target_pairs={{0,8},{8,0},{16,24},{24,16},{1,9},{9,1},{17,25},{25,17},{2,10},{10... | collective-permute-start | bytes 589832 | tf_op jit(solution)/shard_map/ppermute | solution.py:255
  54.2 5.4 %collective-permute-start.14 = (bf16[192,512]{1,0:T(8,128)(2,1)S(1)}, bf16[192,512]{1,0:T(8,128)(2,1)S(1)}, u32[]{:S(2)}, u32[]{:S(2)}) collective-permute-start(bf16[192,512]{1,0:T(8,128)(2,1)S(1)} %copy-done.6), channel_id=1, source_target_pairs={{0,8},{8,0},{16,24},{24,16},{1,9},{9,1},{17,25},{25,17},{2,10},{10... | collective-permute-start | bytes 589832 | tf_op jit(solution)/shard_map/ppermute | solution.py:255
  57.3 2.4 %copy-start.2 = (bf16[1,128,1024]{2,1,0:T(8,128)(2,1)S(1)}, bf16[1,128,1024]{2,1,0:T(8,128)(2,1)}, u32[]{:S(2)}) copy-start(bf16[1,128,1024]{2,1,0:T(8,128)(2,1)} %param.19) | copy-start | bytes 786436

commit v6 on v5

--- a/solution.py
+++ b/solution.py
@@ -48,12 +48,12 @@
     return [pltpu.with_memory_space_constraint(a, pltpu.VMEM) for a in arrays]
 
 
-def call(kernel, out_shape, in_specs, flops, nbytes, limit, scratch=()):
+def call(kernel, out_shape, in_specs, flops, nbytes, limit, scratch=(), out_specs=None):
     return pl.pallas_call(
         kernel,
         out_shape=out_shape,
         in_specs=in_specs,
-        out_specs=jax.tree.map(lambda _: whole(), out_shape),
+        out_specs=out_specs or jax.tree.map(lambda _: whole(), out_shape),
         scratch_shapes=list(scratch),
         compiler_params=pltpu.CompilerParams(vmem_limit_bytes=limit << 20),
         cost_estimate=pl.CostEstimate(flops=flops, bytes_accessed=nbytes, transcendentals=0),
@@ -365,7 +365,7 @@
 
 
 def close_kernel(hidden, given, own_active, gate_sums, up_sums, *refs):
-    pieces, (out, ordered, active) = refs[:-3], refs[-3:]
+    pieces, (out_far, out, ordered, active, sems) = refs[:-5], refs[-5:]
     shares, mine, theirs = pieces[:1], pieces[1:10], pieces[10:]
     depth = shares[0].shape[0]
     spots, read, own_cols, in_order = travelled([None, None, *shares], mine, theirs, depth)
@@ -381,11 +381,16 @@
         active[:, own_cols(part, start, lane_chunk)] = units
     in_order(active, ordered)
     x = ordered[...]
-    for part, start in spots:
+    copies = []
+    for i, (part, start) in enumerate(spots):
         cols = own_cols(part, start, lane_chunk)
         out[:, cols] = (hidden[:, cols] + dot(x, read(2, part, start, lane_chunk, range(8)))).astype(
             jnp.bfloat16
         )
+        copies.append(pltpu.make_async_copy(out.at[:, cols], out_far.at[:, cols], sems.at[i]))
+        copies[-1].start()
+    for copy in copies:
+        copy.wait()
 
 
 def hop_feed(inner, hidden, shares, mine, theirs):
@@ -397,10 +402,12 @@
         [whole()] * (1 + len(early)), 4 * count * width * inside, 4 << 20, 8,
     )(inner, *early)
     late = [hidden, *opened, shares[2], *mine, *theirs]
-    scratch = [pltpu.VMEM((count, inside), jnp.bfloat16), pltpu.VMEM((count, inside), jnp.bfloat16)]
+    scratch = [pltpu.VMEM((count, width), jnp.bfloat16)]
+    scratch += [pltpu.VMEM((count, inside), jnp.bfloat16)] * 2
+    scratch.append(pltpu.SemaphoreType.DMA((width // lane_chunk,)))
     return call(
         close_kernel, shape(count, width), [whole()] * len(late),
-        2 * count * width * inside, 4 << 20, 8, scratch,
+        2 * count * width * inside, 4 << 20, 8, scratch, whole(pltpu.HBM),
     )(*late)
 
 

time: 63.3 us -> 63.3 us (level)
  no operation moved by 1% of the time
where the time goes in v6:
time: 63.3 us; the launch traced here: 62.9 us
  starting transfers between devices  25.4 us (40%)
  waiting for transfers between devices  21.7 us (34%)
  Pallas kernels  14.9 us (24%)
  local copies, waits for them, and re-layouts  0.7 us (1%)
    ppermute x8, starting transfers between devices, send(): return lax.ppermute(block, 'col', route)  13.5 us
    ppermute x8, waiting for transfers between devices, send(): return lax.ppermute(block, 'col', route)  10.9 us
    all_to_all x1, waiting for transfers between devices, body(): got = lax.all_to_all(sent, both, 0, 0)  7.4 us
    ppermute x10, starting transfers between devices, partner(): lax.ppermute(block, 'row', [(i, i ^ distance) for i in range(lax.axis_siz...  6.01 us
    all_to_all x1, starting transfers between devices, body(): got = lax.all_to_all(sent, both, 0, 0)  5.85 us
    pallas_call x2, Pallas kernels, mix(): call(mix_kernel, out, [whole(pltpu.SMEM)] + [whole()] * len(operands), 8...  3.87 us
    ppermute x10, waiting for transfers between devices, partner(): lax.ppermute(block, 'row', [(i, i ^ distance) for i in range(lax.axis_siz...  3.44 us
    pallas_call x1, Pallas kernels, hop_feed(): call(close_kernel, shape(count, width), [whole()] * len(late), 2 * count...  3.16 us
  transfers between devices with their start and end apart: 19, of which 5 were waited for; matrix products, arithmetic and copies ran while one was open for 0% of the time, Pallas kernels for 17%

profile of v6, /device:TPU:0, one launch (start us, length us, event | category | flops | bytes accessed | tf_op | source)
XLA Modules:
  0.0 62.9 jit_solution(12375935761090136971)
XLA Ops:
  0.0 1.1 %shard_map.114 = (bf16[384,512]{1,0:T(8,128)(2,1)S(1)}, bf16[192,512]{1,0:T(8,128)(2,1)S(1)}) custom-call(bf16[128,1024]{1,0:T(8,128)(2,1)} %bitcast.6, bf16[128,1024]{1,0:T(8,128)(2,1)} %bitcast.8, bf16[128,1024]{1,0:T(8,128)(2,1)} %bitcast.10), custom_call_target="tpu_custom_call" | custom-call | bytes 1048576 | tf_op jit(solution)/shard_map/pallas_call | solution.py:88
  1.1 3.1 %collective-permute-start.1 = (bf16[384,512]{1,0:T(8,128)(2,1)S(1)}, bf16[384,512]{1,0:T(8,128)(2,1)S(1)}, u32[]{:S(2)}, u32[]{:S(2)}) collective-permute-start(bf16[384,512]{1,0:T(8,128)(2,1)S(1)} %get-tuple-element.33), channel_id=1, source_target_pairs={{0,1},{1,0},{6,7},{7,6},{2,4},{3,5},{4,2},{5,3},{8,9},{9,8},{14,15... | collective-permute-start | bytes 1179656 | tf_op jit(solution)/shard_map/ppermute | solution.py:270
  4.2 1.6 %collective-permute-start = (bf16[384,512]{1,0:T(8,128)(2,1)S(1)}, bf16[384,512]{1,0:T(8,128)(2,1)S(1)}, u32[]{:S(2)}, u32[]{:S(2)}) collective-permute-start(bf16[384,512]{1,0:T(8,128)(2,1)S(1)} %get-tuple-element.33), channel_id=1, source_target_pairs={{0,2},{1,3},{2,0},{3,1},{4,6},{5,7},{6,4},{7,5},{8,10},{9,11},{10,... | collective-permute-start | bytes 1179656 | tf_op jit(solution)/shard_map/ppermute | solution.py:270
  5.8 2.3 %collective-permute-start.4 = (bf16[192,512]{1,0:T(8,128)(2,1)S(1)}, bf16[192,512]{1,0:T(8,128)(2,1)S(1)}, u32[]{:S(2)}, u32[]{:S(2)}) collective-permute-start(bf16[192,512]{1,0:T(8,128)(2,1)S(1)} %get-tuple-element.34), channel_id=1, source_target_pairs={{0,7},{1,6},{2,3},{3,2},{4,5},{5,4},{6,1},{7,0},{8,15},{9,14},{10,... | collective-permute-start | bytes 589832 | tf_op jit(solution)/shard_map/ppermute | solution.py:270
  8.1 5.2 %collective-permute-done.1.refs_3_.refs_2_ = bf16[384,512]{1,0:T(8,128)(2,1)S(1)} collective-permute-done((bf16[384,512]{1,0:T(8,128)(2,1)S(1)}, bf16[384,512]{1,0:T(8,128)(2,1)S(1)}, u32[]{:S(2)}, u32[]{:S(2)}) %collective-permute-start.1) | collective-permute-done | bytes 393248 | tf_op jit(solution)/shard_map/ppermute | solution.py:270
  13.3 1.8 %collective-permute-start.2 = (bf16[384,512]{1,0:T(8,128)(2,1)S(1)}, bf16[384,512]{1,0:T(8,128)(2,1)S(1)}, u32[]{:S(2)}, u32[]{:S(2)}) collective-permute-start(bf16[384,512]{1,0:T(8,128)(2,1)S(1)} %collective-permute-done.1.refs_3_.refs_2_), channel_id=1, source_target_pairs={{0,2},{1,3},{2,0},{3,1},{4,6},{5,7},{6,4},{7,5},{8,10},{9,11},{10,... | collective-permute-start | bytes 1179656 | tf_op jit(solution)/shard_map/ppermute | solution.py:270
  15.1 0.2 collective-permute-done.refs_2_.refs_1_
  15.3 1.5 %collective-permute-start.3 = (bf16[384,512]{1,0:T(8,128)(2,1)S(1)}, bf16[384,512]{1,0:T(8,128)(2,1)S(1)}, u32[]{:S(2)}, u32[]{:S(2)}) collective-permute-start(bf16[384,512]{1,0:T(8,128)(2,1)S(1)} %collective-permute-done.refs_2_.refs_1_), channel_id=1, source_target_pairs={{0,1},{1,0},{6,7},{7,6},{2,4},{3,5},{4,2},{5,3},{8,9},{9,8},{14,15... | collective-permute-start | bytes 1179656 | tf_op jit(solution)/shard_map/ppermute | solution.py:270
  16.8 5.5 %collective-permute-done.4.refs_6_.refs_5_ = bf16[192,512]{1,0:T(8,128)(2,1)S(1)} collective-permute-done((bf16[192,512]{1,0:T(8,128)(2,1)S(1)}, bf16[192,512]{1,0:T(8,128)(2,1)S(1)}, u32[]{:S(2)}, u32[]{:S(2)}) %collective-permute-start.4) | collective-permute-done | bytes 196640 | tf_op jit(solution)/shard_map/ppermute | solution.py:270
  22.3 1.5 %collective-permute-start.5 = (bf16[192,512]{1,0:T(8,128)(2,1)S(1)}, bf16[192,512]{1,0:T(8,128)(2,1)S(1)}, u32[]{:S(2)}, u32[]{:S(2)}) collective-permute-start(bf16[192,512]{1,0:T(8,128)(2,1)S(1)} %collective-permute-done.4.refs_6_.refs_5_), channel_id=1, source_target_pairs={{0,16},{8,24},{16,0},{24,8},{1,17},{9,25},{17,1},{25,9},{2,18},{10... | collective-permute-start | bytes 589832 | tf_op jit(solution)/shard_map/ppermute | solution.py:255
  23.8 0.7 %collective-permute-start.8 = (bf16[384,512]{1,0:T(8,128)(2,1)S(1)}, bf16[384,512]{1,0:T(8,128)(2,1)S(1)}, u32[]{:S(2)}, u32[]{:S(2)}) collective-permute-start(bf16[384,512]{1,0:T(8,128)(2,1)S(1)} %collective-permute-done.1.refs_3_.refs_2_), channel_id=1, source_target_pairs={{2,3},{3,2},{4,5},{5,4},{10,11},{11,10},{12,13},{13,12},{18,19},{1... | collective-permute-start | bytes 1179656 | tf_op jit(solution)/shard_map/ppermute | solution.py:270
  24.4 0.1 collective-permute-start.10
  24.5 3.4 %collective-permute-done.5.refs_7_.refs_6_ = bf16[192,512]{1,0:T(8,128)(2,1)S(1)} collective-permute-done((bf16[192,512]{1,0:T(8,128)(2,1)S(1)}, bf16[192,512]{1,0:T(8,128)(2,1)S(1)}, u32[]{:S(2)}, u32[]{:S(2)}) %collective-permute-start.5) | collective-permute-done | bytes 196640 | tf_op jit(solution)/shard_map/ppermute | solution.py:255
  27.9 0.0 collective-permute-start.9
  27.9 0.0 collective-permute-done.2.refs_4_.refs_3_
  28.0 1.2 %collective-permute-start.6 = (bf16[384,512]{1,0:T(8,128)(2,1)S(1)}, bf16[384,512]{1,0:T(8,128)(2,1)S(1)}, u32[]{:S(2)}, u32[]{:S(2)}) collective-permute-start(bf16[384,512]{1,0:T(8,128)(2,1)S(1)} %collective-permute-done.2.refs_4_.refs_3_), channel_id=1, source_target_pairs={{0,1},{1,0},{6,7},{7,6},{2,4},{3,5},{4,2},{5,3},{8,9},{9,8},{14,15... | collective-permute-start | bytes 1179656 | tf_op jit(solution)/shard_map/ppermute | solution.py:270
  29.2 0.0 collective-permute-done.3.refs_5_.refs_4_
  29.2 1.3 %collective-permute-start.7 = (bf16[384,512]{1,0:T(8,128)(2,1)S(1)}, bf16[384,512]{1,0:T(8,128)(2,1)S(1)}, u32[]{:S(2)}, u32[]{:S(2)}) collective-permute-start(bf16[384,512]{1,0:T(8,128)(2,1)S(1)} %collective-permute-done.3.refs_5_.refs_4_), channel_id=1, source_target_pairs={{2,0},{3,1},{4,6},{5,7},{10,8},{11,9},{12,14},{13,15},{18,16},{19,... | collective-permute-start | bytes 1179656 | tf_op jit(solution)/shard_map/ppermute | solution.py:270
  30.5 1.0 %shard_map.109 = (bf16[32,2,1280]{2,1,0:T(2,128)(2,1)S(1)}, s32[1,256]{1,0:T(1,128)S(1)}, f32[2,1024]{1,0:T(2,128)S(1)}) custom-call(s32[1,256]{1,0:T(1,128)} %bitcast.14, f32[2,1024]{1,0:T(2,128)} %bitcast.13, bf16[2,1024]{1,0:T(2,128)(2,1)} %rows_far.1), custom_call_target="tpu_custom_call" | custom-call | bytes 262144 | tf_op jit(solution)/shard_map/pallas_call | solution.py:119
  31.5 0.7 %copy-done.7 = bf16[32,2,1280]{2,1,0:T(2,128)(2,1)} copy-done((bf16[32,2,1280]{2,1,0:T(2,128)(2,1)}, bf16[32,2,1280]{2,1,0:T(2,128)(2,1)S(1)}, u32[]{:S(2)}) %copy-start.7) | copy-done | bytes 163864
  32.2 5.8 %all-to-all-start = ((bf16[32,2,1280]{2,1,0:T(2,128)(2,1)}), bf16[32,2,1280]{2,1,0:T(2,128)(2,1)}, u32[]{:S(2)}, u32[]{:S(2)}) async-start(bf16[32,2,1280]{2,1,0:T(2,128)(2,1)} %copy-done.7), calls=%async_computation | async-start | bytes 327680 | tf_op jit(solution)/shard_map/all_to_all | solution.py:441
  38.0 0.0 collective-permute-done.8.refs_10_.refs_9_
  38.0 0.3 collective-permute-start.11
  38.3 0.0 collective-permute-done.10.refs_12_.refs_11_
  38.3 0.3 collective-permute-start.12
  38.6 7.4 %all-to-all-done.got = bf16[32,2,1280]{2,1,0:T(2,128)(2,1)} async-done(((bf16[32,2,1280]{2,1,0:T(2,128)(2,1)}), bf16[32,2,1280]{2,1,0:T(2,128)(2,1)}, u32[]{:S(2)}, u32[]{:S(2)}) %all-to-all-start) | async-done | bytes 163872 | tf_op jit(solution)/shard_map/all_to_all | solution.py:441
  46.0 1.3 %shard_map.110 = (bf16[64,1024]{1,0:T(8,128)(2,1)S(1)}, bf16[64,1024]{1,0:T(8,128)(2,1)S(1)}, bf16[512,64]{1,0:T(8,128)(2,1)S(1)}) custom-call(bf16[32,2,1280]{2,1,0:T(2,128)(2,1)} %all-to-all-done.got, s32[1,256]{1,0:T(1,128)S(1)} %get-tuple-element.23.own, f32[2,1024]{1,0:T(2,128)S(1)} %get-tuple-element.24.gains), custom_call_target="tpu_custom_call" | custom-call | flops 1048576 | bytes 524288 | tf_op jit(solution)/shard_map/pallas_call | solution.py:186
  47.3 2.1 %shard_map.111 = (f32[512,1024]{1,0:T(8,128)S(1)}, bf16[512,1024]{1,0:T(8,128)(2,1)S(1)}, bf16[256,1536]{1,0:T(8,128)(2,1)S(1)}) custom-call(bf16[512,64]{1,0:T(8,128)(2,1)S(1)} %get-tuple-element.27.after.chosen, bf16[256,1024]{1,0:T(8,128)(2,1)} %bitcast.12, s32[1,1024]{1,0:T(1,128)} %lengths_far.1, bf16[512,1024]{1,0:T(8,128)(2,1)} %constant.4.clone.refs_0_, ...), custom_call_target="tpu_custom_call" | custom-call | flops 536870912 | bytes 5242880 | tf_op jit(solution)/shard_map/pallas_call | solution.py:145
  49.5 0.0 collective-permute-done.9.refs_11_.refs_10_
  49.5 0.2 collective-permute-start.17
  49.7 0.0 collective-permute-done.6.refs_8_.refs_7_
  49.7 0.4 collective-permute-start.15
  50.0 0.0 collective-permute-done.7.refs_9_.refs_8_
  50.0 0.1 collective-permute-start.16
  50.2 0.9 %shard_map.112.given = f32[256,1024]{1,0:T(8,128)S(1)} custom-call(s32[8]{0:T(128)S(1)} %copy-done.8, bf16[64,1024]{1,0:T(8,128)(2,1)S(1)} %get-tuple-element.25.given, bf16[64,1024]{1,0:T(8,128)(2,1)S(1)} %get-tuple-element.26.normed, bf16[512,64]{1,0:T(8,128)(2,1)S(1)} %get-tuple-element.27.after.chosen, f32[2,1024]{1,0:T(2,128)S(1)} %get-tuple-element.24.gains, ...), custom_call_target="tpu_custom_call" | custom-call | flops 2147483648 | bytes 4194304 | tf_op jit(solution)/shard_map/pallas_call | solution.py:239
  51.1 0.0 copy-start
  51.1 0.0 copy-start.1
  51.1 0.0 collective-permute-done.11.refs_13_.refs_12_
  51.2 3.1 %collective-permute-start.13 = (bf16[192,512]{1,0:T(8,128)(2,1)S(1)}, bf16[192,512]{1,0:T(8,128)(2,1)S(1)}, u32[]{:S(2)}, u32[]{:S(2)}) collective-permute-start(bf16[192,512]{1,0:T(8,128)(2,1)S(1)} %copy-done.4), channel_id=1, source_target_pairs={{0,8},{8,0},{16,24},{24,16},{1,9},{9,1},{17,25},{25,17},{2,10},{10... | collective-permute-start | bytes 589832 | tf_op jit(solution)/shard_map/ppermute | solution.py:255
  54.2 0.0 collective-permute-done.12.refs_14_.refs_13_
  54.2 0.1 collective-permute-start.14
  54.3 2.9 %shard_map.113 = (f32[256,1024]{1,0:T(8,128)S(1)}, bf16[256,1024]{1,0:T(8,128)(2,1)S(1)}) custom-call(s32[8]{0:T(128)S(1)} %copy-done.8, f32[256,1024]{1,0:T(8,128)S(1)} %shard_map.112.given, bf16[64,1024]{1,0:T(8,128)(2,1)S(1)} %get-tuple-element.26.normed, bf16[512,64]{1,0:T(8,128)(2,1)S(1)} %get-tuple-element.27.after.chosen, ...), custom_call_target="tpu_custom_call" | custom-call | flops 2147483648 | bytes 4194304 | tf_op jit(solution)/shard_map/pallas_call | solution.py:239
  57.3 0.0 copy-start.2
  57.3 2.3 %shard_map.115 = (bf16[256,1024]{1,0:T(8,128)(2,1)S(1)}, bf16[256,512]{1,0:T(8,128)(2,1)S(1)}, f32[256,512]{1,0:T(8,128)S(1)}, f32[256,512]{1,0:T(8,128)S(1)}) custom-call(bf16[256,1024]{1,0:T(8,128)(2,1)S(1)} %get-tuple-element.32.inner, bf16[128,1024]{1,0:T(8,128)(2,1)S(1)} %bitcast.7, bf16[128,1024]{1,0:T(8,128)(2,1)S(1)} %bitcast.9, ...), custom_call_target="tpu_custom_call" | custom-call | flops 1073741824 | bytes 4194304 | tf_op jit(solution)/shard_map/pallas_call | solution.py:400
  59.7 0.0 collective-permute-done.14.refs_15_
  59.7 0.0 collective-permute-done.17.refs_18_
  59.7 0.0 collective-permute-done.16.refs_17_
  59.7 3.2 %shard_map.116 = bf16[256,1024]{1,0:T(8,128)(2,1)} custom-call(f32[256,1024]{1,0:T(8,128)S(1)} %get-tuple-element.31.hidden, bf16[256,1024]{1,0:T(8,128)(2,1)S(1)} %get-tuple-element.35.given, bf16[256,512]{1,0:T(8,128)(2,1)S(1)} %get-tuple-element.36.own_active, f32[256,512]{1,0:T(8,128)S(1)} %get-tuple-element.37.gate_sums, ...), custom_call_target="tpu_custom_call" | custom-call | flops 536870912 | bytes 4194304 | tf_op jit(solution)/shard_map/pallas_call | solution.py:408
  (16 shorter events, 0.0 us)
Async XLA Ops:
  0.0 50.2 %copy-start.8 = (s32[8]{0:T(128)S(1)}, s32[8]{0:T(128)}, u32[]{:S(2)}) copy-start(s32[8]{0:T(128)} %lengths.3) | copy-start | bytes 100
  1.1 12.2 %collective-permute-start.1 = (bf16[384,512]{1,0:T(8,128)(2,1)S(1)}, bf16[384,512]{1,0:T(8,128)(2,1)S(1)}, u32[]{:S(2)}, u32[]{:S(2)}) collective-permute-start(bf16[384,512]{1,0:T(8,128)(2,1)S(1)} %get-tuple-element.33), channel_id=1, source_target_pairs={{0,1},{1,0},{6,7},{7,6},{2,4},{3,5},{4,2},{5,3},{8,9},{9,8},{14,15... | collective-permute-start | bytes 1179656 | tf_op jit(solution)/shard_map/ppermute | solution.py:270
  4.2 11.1 %collective-permute-start = (bf16[384,512]{1,0:T(8,128)(2,1)S(1)}, bf16[384,512]{1,0:T(8,128)(2,1)S(1)}, u32[]{:S(2)}, u32[]{:S(2)}) collective-permute-start(bf16[384,512]{1,0:T(8,128)(2,1)S(1)} %get-tuple-element.33), channel_id=1, source_target_pairs={{0,2},{1,3},{2,0},{3,1},{4,6},{5,7},{6,4},{7,5},{8,10},{9,11},{10,... | collective-permute-start | bytes 1179656 | tf_op jit(solution)/shard_map/ppermute | solution.py:270
  5.8 16.5 %collective-permute-start.4 = (bf16[192,512]{1,0:T(8,128)(2,1)S(1)}, bf16[192,512]{1,0:T(8,128)(2,1)S(1)}, u32[]{:S(2)}, u32[]{:S(2)}) collective-permute-start(bf16[192,512]{1,0:T(8,128)(2,1)S(1)} %get-tuple-element.34), channel_id=1, source_target_pairs={{0,7},{1,6},{2,3},{3,2},{4,5},{5,4},{6,1},{7,0},{8,15},{9,14},{10,... | collective-permute-start | bytes 589832 | tf_op jit(solution)/shard_map/ppermute | solution.py:270
  13.3 14.7 %collective-permute-start.2 = (bf16[384,512]{1,0:T(8,128)(2,1)S(1)}, bf16[384,512]{1,0:T(8,128)(2,1)S(1)}, u32[]{:S(2)}, u32[]{:S(2)}) collective-permute-start(bf16[384,512]{1,0:T(8,128)(2,1)S(1)} %collective-permute-done.1.refs_3_.refs_2_), channel_id=1, source_target_pairs={{0,2},{1,3},{2,0},{3,1},{4,6},{5,7},{6,4},{7,5},{8,10},{9,11},{10,... | collective-permute-start | bytes 1179656 | tf_op jit(solution)/shard_map/ppermute | solution.py:270
  15.3 13.9 %collective-permute-start.3 = (bf16[384,512]{1,0:T(8,128)(2,1)S(1)}, bf16[384,512]{1,0:T(8,128)(2,1)S(1)}, u32[]{:S(2)}, u32[]{:S(2)}) collective-permute-start(bf16[384,512]{1,0:T(8,128)(2,1)S(1)} %collective-permute-done.refs_2_.refs_1_), channel_id=1, source_target_pairs={{0,1},{1,0},{6,7},{7,6},{2,4},{3,5},{4,2},{5,3},{8,9},{9,8},{14,15... | collective-permute-start | bytes 1179656 | tf_op jit(solution)/shard_map/ppermute | solution.py:270
  22.3 6.9 %copy-start.3 = (bf16[192,512]{1,0:T(8,128)(2,1)}, bf16[192,512]{1,0:T(8,128)(2,1)S(1)}, u32[]{:S(2)}) copy-start(bf16[192,512]{1,0:T(8,128)(2,1)S(1)} %collective-permute-done.4.refs_6_.refs_5_) | copy-start | bytes 589828
  22.3 5.7 %collective-permute-start.5 = (bf16[192,512]{1,0:T(8,128)(2,1)S(1)}, bf16[192,512]{1,0:T(8,128)(2,1)S(1)}, u32[]{:S(2)}, u32[]{:S(2)}) collective-permute-start(bf16[192,512]{1,0:T(8,128)(2,1)S(1)} %collective-permute-done.4.refs_6_.refs_5_), channel_id=1, source_target_pairs={{0,16},{8,24},{16,0},{24,8},{1,17},{9,25},{17,1},{25,9},{2,18},{10... | collective-permute-start | bytes 589832 | tf_op jit(solution)/shard_map/ppermute | solution.py:255
  23.8 14.3 %collective-permute-start.8 = (bf16[384,512]{1,0:T(8,128)(2,1)S(1)}, bf16[384,512]{1,0:T(8,128)(2,1)S(1)}, u32[]{:S(2)}, u32[]{:S(2)}) collective-permute-start(bf16[384,512]{1,0:T(8,128)(2,1)S(1)} %collective-permute-done.1.refs_3_.refs_2_), channel_id=1, source_target_pairs={{2,3},{3,2},{4,5},{5,4},{10,11},{11,10},{12,13},{13,12},{18,19},{1... | collective-permute-start | bytes 1179656 | tf_op jit(solution)/shard_map/ppermute | solution.py:270
  24.4 13.9 %collective-permute-start.10 = (bf16[384,512]{1,0:T(8,128)(2,1)S(1)}, bf16[384,512]{1,0:T(8,128)(2,1)S(1)}, u32[]{:S(2)}, u32[]{:S(2)}) collective-permute-start(bf16[384,512]{1,0:T(8,128)(2,1)S(1)} %collective-permute-done.1.refs_3_.refs_2_), channel_id=1, source_target_pairs={{0,8},{8,0},{16,24},{24,16},{1,9},{9,1},{17,25},{25,17},{2,10},{10... | collective-permute-start | bytes 1179656 | tf_op jit(solution)/shard_map/ppermute | solution.py:255
  27.9 2.5 %copy-start.5 = (bf16[192,512]{1,0:T(8,128)(2,1)}, bf16[192,512]{1,0:T(8,128)(2,1)S(1)}, u32[]{:S(2)}) copy-start(bf16[192,512]{1,0:T(8,128)(2,1)S(1)} %collective-permute-done.5.refs_7_.refs_6_) | copy-start | bytes 589828
  27.9 21.5 %collective-permute-start.9 = (bf16[384,512]{1,0:T(8,128)(2,1)S(1)}, bf16[384,512]{1,0:T(8,128)(2,1)S(1)}, u32[]{:S(2)}, u32[]{:S(2)}) collective-permute-start(bf16[384,512]{1,0:T(8,128)(2,1)S(1)} %collective-permute-done.refs_2_.refs_1_), channel_id=1, source_target_pairs={{0,8},{8,0},{16,24},{24,16},{1,9},{9,1},{17,25},{25,17},{2,10},{10... | collective-permute-start | bytes 1179656 | tf_op jit(solution)/shard_map/ppermute | solution.py:255
  28.0 21.7 %collective-permute-start.6 = (bf16[384,512]{1,0:T(8,128)(2,1)S(1)}, bf16[384,512]{1,0:T(8,128)(2,1)S(1)}, u32[]{:S(2)}, u32[]{:S(2)}) collective-permute-start(bf16[384,512]{1,0:T(8,128)(2,1)S(1)} %collective-permute-done.2.refs_4_.refs_3_), channel_id=1, source_target_pairs={{0,1},{1,0},{6,7},{7,6},{2,4},{3,5},{4,2},{5,3},{8,9},{9,8},{14,15... | collective-permute-start | bytes 1179656 | tf_op jit(solution)/shard_map/ppermute | solution.py:270
  29.2 20.9 %collective-permute-start.7 = (bf16[384,512]{1,0:T(8,128)(2,1)S(1)}, bf16[384,512]{1,0:T(8,128)(2,1)S(1)}, u32[]{:S(2)}, u32[]{:S(2)}) collective-permute-start(bf16[384,512]{1,0:T(8,128)(2,1)S(1)} %collective-permute-done.3.refs_5_.refs_4_), channel_id=1, source_target_pairs={{2,0},{3,1},{4,6},{5,7},{10,8},{11,9},{12,14},{13,15},{18,16},{19,... | collective-permute-start | bytes 1179656 | tf_op jit(solution)/shard_map/ppermute | solution.py:270
  31.5 0.7 %copy-start.7 = (bf16[32,2,1280]{2,1,0:T(2,128)(2,1)}, bf16[32,2,1280]{2,1,0:T(2,128)(2,1)S(1)}, u32[]{:S(2)}) copy-start(bf16[32,2,1280]{2,1,0:T(2,128)(2,1)S(1)} %get-tuple-element.22) | copy-start | bytes 491524
  32.2 13.8 %all-to-all-start = ((bf16[32,2,1280]{2,1,0:T(2,128)(2,1)}), bf16[32,2,1280]{2,1,0:T(2,128)(2,1)}, u32[]{:S(2)}, u32[]{:S(2)}) async-start(bf16[32,2,1280]{2,1,0:T(2,128)(2,1)} %copy-done.7), calls=%async_computation | async-start | bytes 327680 | tf_op jit(solution)/shard_map/all_to_all | solution.py:441
  38.0 13.1 %collective-permute-start.11 = (bf16[384,512]{1,0:T(8,128)(2,1)S(1)}, bf16[384,512]{1,0:T(8,128)(2,1)}, u32[]{:S(2)}, u32[]{:S(2)}) collective-permute-start(bf16[384,512]{1,0:T(8,128)(2,1)S(1)} %collective-permute-done.2.refs_4_.refs_3_), channel_id=1, source_target_pairs={{0,8},{8,0},{16,24},{24,16},{1,9},{9,1},{17,25},{25,17},{2,10},{10... | collective-permute-start | bytes 1179656 | tf_op jit(solution)/shard_map/ppermute | solution.py:255
  38.3 15.9 %collective-permute-start.12 = (bf16[384,512]{1,0:T(8,128)(2,1)S(1)}, bf16[384,512]{1,0:T(8,128)(2,1)}, u32[]{:S(2)}, u32[]{:S(2)}) collective-permute-start(bf16[384,512]{1,0:T(8,128)(2,1)S(1)} %collective-permute-done.3.refs_5_.refs_4_), channel_id=1, source_target_pairs={{0,8},{8,0},{16,24},{24,16},{1,9},{9,1},{17,25},{25,17},{2,10},{10... | collective-permute-start | bytes 1179656 | tf_op jit(solution)/shard_map/ppermute | solution.py:255
  49.5 10.2 %collective-permute-start.17 = (bf16[384,512]{1,0:T(8,128)(2,1)S(1)}, bf16[384,512]{1,0:T(8,128)(2,1)S(1)}, u32[]{:S(2)}, u32[]{:S(2)}) collective-permute-start(bf16[384,512]{1,0:T(8,128)(2,1)S(1)} %collective-permute-done.8.refs_10_.refs_9_), channel_id=1, source_target_pairs={{0,8},{8,0},{16,24},{24,16},{1,9},{9,1},{17,25},{25,17},{2,10},{10... | collective-permute-start | bytes 1179656 | tf_op jit(solution)/shard_map/ppermute | solution.py:255
  49.7 10.0 %collective-permute-start.15 = (bf16[384,512]{1,0:T(8,128)(2,1)S(1)}, bf16[384,512]{1,0:T(8,128)(2,1)S(1)}, u32[]{:S(2)}, u32[]{:S(2)}) collective-permute-start(bf16[384,512]{1,0:T(8,128)(2,1)S(1)} %collective-permute-done.6.refs_8_.refs_7_), channel_id=1, source_target_pairs={{0,8},{8,0},{16,24},{24,16},{1,9},{9,1},{17,25},{25,17},{2,10},{10... | collective-permute-start | bytes 1179656 | tf_op jit(solution)/shard_map/ppermute | solution.py:255
  50.0 9.7 %collective-permute-start.16 = (bf16[384,512]{1,0:T(8,128)(2,1)S(1)}, bf16[384,512]{1,0:T(8,128)(2,1)S(1)}, u32[]{:S(2)}, u32[]{:S(2)}) collective-permute-start(bf16[384,512]{1,0:T(8,128)(2,1)S(1)} %collective-permute-done.7.refs_9_.refs_8_), channel_id=1, source_target_pairs={{0,8},{8,0},{16,24},{24,16},{1,9},{9,1},{17,25},{25,17},{2,10},{10... | collective-permute-start | bytes 1179656 | tf_op jit(solution)/shard_map/ppermute | solution.py:255
  50.2 1.0 %copy-start.4 = (bf16[192,512]{1,0:T(8,128)(2,1)S(1)}, bf16[192,512]{1,0:T(8,128)(2,1)}, u32[]{:S(2)}) copy-start(bf16[192,512]{1,0:T(8,128)(2,1)} %copy-done.3) | copy-start | bytes 589828
  50.2 4.1 %copy-start.6 = (bf16[192,512]{1,0:T(8,128)(2,1)S(1)}, bf16[192,512]{1,0:T(8,128)(2,1)}, u32[]{:S(2)}) copy-start(bf16[192,512]{1,0:T(8,128)(2,1)} %copy-done.5) | copy-start | bytes 589828
  51.1 6.2 %copy-start = (bf16[1,128,1024]{2,1,0:T(8,128)(2,1)S(1)}, bf16[1,128,1024]{2,1,0:T(8,128)(2,1)}, u32[]{:S(2)}) copy-start(bf16[1,128,1024]{2,1,0:T(8,128)(2,1)} %param.17) | copy-start | bytes 786436
  51.1 6.2 %copy-start.1 = (bf16[1,128,1024]{2,1,0:T(8,128)(2,1)S(1)}, bf16[1,128,1024]{2,1,0:T(8,128)(2,1)}, u32[]{:S(2)}) copy-start(bf16[1,128,1024]{2,1,0:T(8,128)(2,1)} %param.18) | copy-start | bytes 786436
  51.2 8.5 %collective-permute-start.13 = (bf16[192,512]{1,0:T(8,128)(2,1)S(1)}, bf16[192,512]{1,0:T(8,128)(2,1)S(1)}, u32[]{:S(2)}, u32[]{:S(2)}) collective-permute-start(bf16[192,512]{1,0:T(8,128)(2,1)S(1)} %copy-done.4), channel_id=1, source_target_pairs={{0,8},{8,0},{16,24},{24,16},{1,9},{9,1},{17,25},{25,17},{2,10},{10... | collective-permute-start | bytes 589832 | tf_op jit(solution)/shard_map/ppermute | solution.py:255
  54.2 5.4 %collective-permute-start.14 = (bf16[192,512]{1,0:T(8,128)(2,1)S(1)}, bf16[192,512]{1,0:T(8,128)(2,1)S(1)}, u32[]{:S(2)}, u32[]{:S(2)}) collective-permute-start(bf16[192,512]{1,0:T(8,128)(2,1)S(1)} %copy-done.6), channel_id=1, source_target_pairs={{0,8},{8,0},{16,24},{24,16},{1,9},{9,1},{17,25},{25,17},{2,10},{10... | collective-permute-start | bytes 589832 | tf_op jit(solution)/shard_map/ppermute | solution.py:255
  57.3 2.4 %copy-start.2 = (bf16[1,128,1024]{2,1,0:T(8,128)(2,1)S(1)}, bf16[1,128,1024]{2,1,0:T(8,128)(2,1)}, u32[]{:S(2)}) copy-start(bf16[1,128,1024]{2,1,0:T(8,128)(2,1)} %param.19) | copy-start | bytes 786436
